TPU v7x, 32 devices: a whole 2x2x4 slice. The times are simulated.
32 devices in a mesh: seq: 4 (over y, core), wsh: 8 (over z, x).
Axes of the slice: x: 2, y: 2, z: 4, core: 2. Of those that a mesh axis runs over, the one named last changes fastest.
Arguments:
- tokens: bfloat16 [8, 1024, 2048], P('wsh', 'seq'), may hold values from -6 to 6
- token_document: int32 [8, 1024], P('wsh', 'seq'), may hold values from 0 to 7, never falling along the last dimension, each value on 1 to 512 neighbouring positions
- document_adapter: int32 [8, 8], P('wsh'), may hold values from 0 to 7
- attention_norm_gain: float32 [2048], replicated, may hold values from 0.5 to 1.5
- feedforward_norm_gain: float32 [2048], replicated, may hold values from 0.5 to 1.5
- query_weight: bfloat16 [2048, 2048], P('wsh'), may hold values from -0.375 to 0.375
- key_weight: bfloat16 [2048, 512], P('wsh'), may hold values from -0.375 to 0.375
- value_weight: bfloat16 [2048, 512], P('wsh'), may hold values from -0.125 to 0.125
- output_weight: bfloat16 [2048, 2048], P('wsh'), may hold values from -1.5 to 1.5
- gate_weight: bfloat16 [2048, 8192], P('wsh'), may hold values from -0.125 to 0.125
- up_weight: bfloat16 [2048, 8192], P('wsh'), may hold values from -0.125 to 0.125
- down_weight: bfloat16 [8192, 2048], P('wsh'), may hold values from -0.375 to 0.375
- attention_down_maps: bfloat16 [2048, 8, 48], replicated, may hold values from -0.125 to 0.125
- query_exit_maps: bfloat16 [8, 16, 2048], replicated, may hold values from -1.5 to 1.5
- key_value_exit_maps: bfloat16 [2, 8, 16, 512], replicated, may hold values from -1.5 to 1.5
- output_entry_maps: bfloat16 [2048, 8, 16], replicated, may hold values from -0.125 to 0.125
- output_exit_maps: bfloat16 [8, 16, 2048], replicated, may hold values from -1.5 to 1.5
- feedforward_entry_maps: bfloat16 [2048, 8, 32], replicated, may hold values from -0.125 to 0.125
- feedforward_exit_maps: bfloat16 [2, 8, 16, 8192], replicated, may hold values from -1.5 to 1.5
- down_entry_maps: bfloat16 [8192, 8, 16], replicated, may hold values from -0.0625 to 0.0625
- down_exit_maps: bfloat16 [8, 16, 2048], replicated, may hold values from -1.5 to 1.5
- cotangent: bfloat16 [8, 1024, 2048], P('wsh', 'seq'), may hold values from -6 to 6
Outputs:
- layer_out: bfloat16 [8, 1024, 2048], P('wsh', 'seq')
- grad_tokens: float32 [8, 1024, 2048], P('wsh', 'seq')
- attention_input_gradient: float32 [2048, 8, 48], replicated
- query_output_gradient: float32 [8, 16, 2048], replicated
- grad_b_kv: float32 [2, 8, 16, 512], replicated
- output_input_gradient: float32 [2048, 8, 16], replicated
- output_output_gradient: float32 [8, 16, 2048], replicated
- feedforward_input_gradient: float32 [2048, 8, 32], replicated
- grad_b_mlp: float32 [2, 8, 16, 8192], replicated
- down_input_gradient: float32 [8192, 8, 16], replicated
- down_output_gradient: float32 [8, 16, 2048], replicated
Inputs may be any that keep to these rules, and one draw needn't show every extreme that they name: `token_document`: document numbers of one stream never fall along it; each document has 1 to 512 tokens.
All inputs are finite; a program needn't handle non-finite values.
Results may differ from a plain program's by a relative error of at most 0.018.
Values may be sent and summed in bfloat16 or wider, within the bound.
No kernel may reach another device: no remote copies, remote signals or barrier semaphores. Data moves between devices by JAX's collectives and lax.ppermute only.
A program may use at most 320 MiB of HBM per device.

v0:
```python
import jax
import jax.numpy as jnp
from jax import lax
from jax.sharding import PartitionSpec as P

QUERY_HEADS = 32
KEY_HEADS = 8
HEAD_WIDTH = 64


EPSILON = 1e-05
RESIDUAL_MULT = 0.22
SCORE_MULT = 0.015625
ROPE_BASE = 10000000.0
MASKED = -1e30


def low_dot(left, right):
    return jnp.dot(left, right, preferred_element_type=jnp.float32)


def gradient_product(left, right):
    return lax.dot_general(
        left, right, (((0,), (0,)), ((), ())), preferred_element_type=jnp.float32
    )


def reverse_product(left, right):
    return lax.dot_general(
        left, right, (((1,), (1,)), ((), ())), preferred_element_type=jnp.float32
    )


def normed(values, gain):
    norm_scale = lax.rsqrt(jnp.mean(values * values, axis=-1, keepdims=True) + EPSILON)
    return (values * norm_scale * gain, norm_scale)


def normed_back(values, norm_scale, gain, grad_in):
    scaled = grad_in * gain
    cubed = norm_scale * norm_scale * norm_scale
    return norm_scale * scaled - values * cubed * jnp.mean(scaled * values, axis=-1, keepdims=True)


def rope_tables(positions, head_size):
    half_size = head_size // 2
    inv_freq = ROPE_BASE ** (-(jnp.arange(half_size).astype(jnp.float32) * 2.0) / head_size)
    angles = positions.astype(jnp.float32)[:, None] * inv_freq[None, :]
    return (jnp.cos(angles)[:, None, :], jnp.sin(angles)[:, None, :])


def rotate(values, cos_tab, sin_tab):
    half_size = values.shape[-1] // 2
    former = values[..., :half_size]
    latter = values[..., half_size:]
    return jnp.concatenate(
        [former * cos_tab - latter * sin_tab, latter * cos_tab + former * sin_tab], axis=-1
    )


def rotate_back(values, cos_tab, sin_tab):
    half_size = values.shape[-1] // 2
    former = values[..., :half_size]
    latter = values[..., half_size:]
    return jnp.concatenate(
        [former * cos_tab + latter * sin_tab, latter * cos_tab - former * sin_tab], axis=-1
    )


def select_rows(inputs, down_flat, choose_adapter, ranks):
    full_rank = low_dot(inputs, down_flat).reshape(inputs.shape[0], -1, ranks)
    return (full_rank * choose_adapter[:, :, None]).astype(jnp.bfloat16)


def rank_columns(picked, lower, upper):
    return picked[:, :, lower:upper].reshape(picked.shape[0], -1)


def on_device(
    tokens,
    token_document,
    document_adapter,
    attention_norm_gain,
    feedforward_norm_gain,
    query_weight,
    key_weight,
    value_weight,
    output_weight,
    gate_weight,
    up_weight,
    down_weight,
    attention_down_maps,
    query_exit_maps,
    key_value_exit_maps,
    output_entry_maps,
    output_exit_maps,
    feedforward_entry_maps,
    feedforward_exit_maps,
    down_entry_maps,
    down_exit_maps,
    cotangent,
):
    token_rows = tokens.shape[1]
    width_of_model = tokens.shape[2]
    adapter_table = attention_down_maps.shape[1]
    adapter_rank_size = query_exit_maps.shape[1]
    flattened_rank = adapter_table * adapter_rank_size
    doc_count = document_adapter.shape[1]
    per_kv = QUERY_HEADS // KEY_HEADS
    hidden_state = tokens[0].astype(jnp.float32)
    local_docs = token_document[0]
    doc_hot = (local_docs[:, None] == jnp.arange(doc_count, dtype=jnp.int32)[None, :]).astype(
        jnp.int32
    )
    owner_row = jnp.sum(doc_hot * document_adapter[0][None, :], axis=1)
    choose_adapter = (
        owner_row[:, None] == jnp.arange(adapter_table, dtype=jnp.int32)[None, :]
    ).astype(jnp.float32)
    choose_low = choose_adapter.astype(jnp.bfloat16)
    positions = lax.axis_index("seq") * token_rows + jnp.arange(token_rows, dtype=jnp.int32)
    cos_tab, sin_tab = rope_tables(positions, HEAD_WIDTH)
    attention_input_maps = attention_down_maps.reshape(width_of_model, -1)
    query_output_maps = query_exit_maps.reshape(flattened_rank, -1)
    key_output_maps = key_value_exit_maps[0].reshape(flattened_rank, -1)
    value_output_maps = key_value_exit_maps[1].reshape(flattened_rank, -1)
    output_input_maps = output_entry_maps.reshape(output_entry_maps.shape[0], -1)
    output_output_maps = output_exit_maps.reshape(flattened_rank, -1)
    feedforward_input_maps = feedforward_entry_maps.reshape(width_of_model, -1)
    gate_output_maps = feedforward_exit_maps[0].reshape(flattened_rank, -1)
    upward_output_maps = feedforward_exit_maps[1].reshape(flattened_rank, -1)
    down_input_maps = down_entry_maps.reshape(down_entry_maps.shape[0], -1)
    down_output_maps = down_exit_maps.reshape(flattened_rank, -1)
    attn_full = (
        lax.all_gather(query_weight, "wsh", axis=0, tiled=True),
        lax.all_gather(key_weight, "wsh", axis=0, tiled=True),
        lax.all_gather(value_weight, "wsh", axis=0, tiled=True),
        lax.all_gather(output_weight, "wsh", axis=0, tiled=True),
    )
    query_full, key_full, value_full, out_full = attn_full
    first_normed, scale_one = normed(hidden_state, attention_norm_gain)
    first_normed = first_normed.astype(jnp.bfloat16)
    selected_first = select_rows(
        first_normed, attention_input_maps, choose_adapter, 3 * adapter_rank_size
    )
    query_projected = low_dot(first_normed, query_full) + low_dot(
        rank_columns(selected_first, 0, adapter_rank_size), query_output_maps
    )
    key_projected = low_dot(first_normed, key_full) + low_dot(
        rank_columns(selected_first, adapter_rank_size, 2 * adapter_rank_size), key_output_maps
    )
    value_projected = low_dot(first_normed, value_full) + low_dot(
        rank_columns(selected_first, 2 * adapter_rank_size, 3 * adapter_rank_size),
        value_output_maps,
    )
    query_rot = (
        rotate(query_projected.reshape(token_rows, QUERY_HEADS, HEAD_WIDTH), cos_tab, sin_tab)
        .astype(jnp.bfloat16)
        .reshape(token_rows, -1)
    )
    key_rot = (
        rotate(key_projected.reshape(token_rows, KEY_HEADS, HEAD_WIDTH), cos_tab, sin_tab)
        .astype(jnp.bfloat16)
        .reshape(token_rows, -1)
    )
    value_low = value_projected.astype(jnp.bfloat16)
    query_heads, key_heads, value_heads = (
        lax.all_to_all(query_rot, "seq", split_axis=1, concat_axis=0, tiled=True),
        lax.all_to_all(key_rot, "seq", split_axis=1, concat_axis=0, tiled=True),
        lax.all_to_all(value_low, "seq", split_axis=1, concat_axis=0, tiled=True),
    )
    document_line = lax.all_gather(local_docs, "seq", axis=0, tiled=True)
    token_length = query_heads.shape[0]
    kv_dev = key_heads.shape[1] // HEAD_WIDTH
    block_rows = min(512, token_length)
    block_count = token_length // block_rows
    query_four = query_heads.reshape(token_length, kv_dev, per_kv, HEAD_WIDTH)
    key_three = key_heads.reshape(token_length, kv_dev, HEAD_WIDTH)
    value_three = value_heads.reshape(token_length, kv_dev, HEAD_WIDTH)
    key_pos = jnp.arange(token_length, dtype=jnp.int32)

    def scores_of(first_row):
        query_rows = lax.dynamic_slice_in_dim(query_four, first_row, block_rows, 0)
        row_docs = lax.dynamic_slice_in_dim(document_line, first_row, block_rows, 0)
        row_pos = first_row + jnp.arange(block_rows, dtype=jnp.int32)
        allowed = (row_docs[:, None] == document_line[None, :]) & (
            key_pos[None, :] <= row_pos[:, None]
        )
        raw_scores = jnp.einsum(
            "qkgd,skd->kgqs", query_rows, key_three, preferred_element_type=jnp.float32
        )
        return (jnp.where(allowed[None, None], SCORE_MULT * raw_scores, MASKED), query_rows)

    def forward_block(running_totals, block_index):
        logits, query_rows = scores_of(block_index * block_rows)
        row_max = jnp.max(logits, axis=-1, keepdims=True)
        shifted = jnp.exp(logits - row_max)
        row_sum = jnp.sum(shifted, axis=-1, keepdims=True)
        probs_low = (shifted / row_sum).astype(jnp.bfloat16)
        mixed_rows = jnp.einsum(
            "kgqs,skd->qkgd", probs_low, value_three, preferred_element_type=jnp.float32
        )
        log_total = row_max[..., 0] + jnp.log(row_sum[..., 0])
        return (
            running_totals,
            (mixed_rows.reshape(block_rows, -1).astype(jnp.bfloat16), log_total),
        )

    block_ids = jnp.arange(block_count, dtype=jnp.int32)
    _, (attn_blocks, log_totals) = lax.scan(forward_block, 0, block_ids)
    attn_heads = attn_blocks.reshape(token_length, -1)
    attention_result = lax.all_to_all(attn_heads, "seq", split_axis=0, concat_axis=1, tiled=True)
    selected_output = select_rows(
        attention_result, output_input_maps, choose_adapter, adapter_rank_size
    )
    attention_path = low_dot(attention_result, out_full) + low_dot(
        selected_output.reshape(token_rows, -1), output_output_maps
    )
    middle = hidden_state + RESIDUAL_MULT * attention_path
    mlp_full = (
        lax.all_gather(gate_weight, "wsh", axis=0, tiled=True),
        lax.all_gather(up_weight, "wsh", axis=0, tiled=True),
        lax.all_gather(down_weight, "wsh", axis=0, tiled=True),
    )
    gate_full, upper_full, down_full = mlp_full
    second_normed, scale_two = normed(middle, feedforward_norm_gain)
    second_normed = second_normed.astype(jnp.bfloat16)
    selected_second = select_rows(
        second_normed, feedforward_input_maps, choose_adapter, 2 * adapter_rank_size
    )
    gate_activation = low_dot(second_normed, gate_full) + low_dot(
        rank_columns(selected_second, 0, adapter_rank_size), gate_output_maps
    )
    upward_activation = low_dot(second_normed, upper_full) + low_dot(
        rank_columns(selected_second, adapter_rank_size, 2 * adapter_rank_size), upward_output_maps
    )
    sigma_gate = jax.nn.sigmoid(gate_activation)
    swish = gate_activation * sigma_gate
    combined_activation = (swish * upward_activation).astype(jnp.bfloat16)
    selected_down = select_rows(
        combined_activation, down_input_maps, choose_adapter, adapter_rank_size
    )
    feedforward_path = low_dot(combined_activation, down_full) + low_dot(
        selected_down.reshape(token_rows, -1), down_output_maps
    )
    layer_out = (middle + RESIDUAL_MULT * feedforward_path).astype(jnp.bfloat16)[None]
    output_gradient = cotangent[0].astype(jnp.float32)
    mlp_back = (
        lax.all_gather(gate_weight, "wsh", axis=0, tiled=True),
        lax.all_gather(up_weight, "wsh", axis=0, tiled=True),
        lax.all_gather(down_weight, "wsh", axis=0, tiled=True),
    )
    gate_back, upper_back, down_back = mlp_back
    feedforward_gradient = (RESIDUAL_MULT * output_gradient).astype(jnp.bfloat16)
    down_output_gradient = gradient_product(
        selected_down.reshape(token_rows, -1), feedforward_gradient
    )
    d_picked_down = (
        reverse_product(feedforward_gradient, down_output_maps)
        .reshape(token_rows, adapter_table, adapter_rank_size)
        .astype(jnp.bfloat16)
        * choose_low[:, :, None]
    )
    d_picked_down = d_picked_down.reshape(token_rows, -1)
    down_input_gradient = gradient_product(combined_activation, d_picked_down)
    d_mixed = reverse_product(feedforward_gradient, down_back) + reverse_product(
        d_picked_down, down_input_maps
    )
    gate_gradient = (
        d_mixed * upward_activation * sigma_gate * (1.0 + gate_activation * (1.0 - sigma_gate))
    ).astype(jnp.bfloat16)
    upward_gradient = (d_mixed * swish).astype(jnp.bfloat16)
    gate_output_gradient = gradient_product(
        rank_columns(selected_second, 0, adapter_rank_size), gate_gradient
    )
    upward_output_gradient = gradient_product(
        rank_columns(selected_second, adapter_rank_size, 2 * adapter_rank_size), upward_gradient
    )
    d_picked_two = jnp.concatenate(
        [
            reverse_product(gate_gradient, gate_output_maps).reshape(
                token_rows, adapter_table, adapter_rank_size
            ),
            reverse_product(upward_gradient, upward_output_maps).reshape(
                token_rows, adapter_table, adapter_rank_size
            ),
        ],
        axis=2,
    )
    d_picked_two = (d_picked_two.astype(jnp.bfloat16) * choose_low[:, :, None]).reshape(
        token_rows, -1
    )
    feedforward_input_gradient = gradient_product(second_normed, d_picked_two)
    d_normed_two = (
        reverse_product(gate_gradient, gate_back)
        + reverse_product(upward_gradient, upper_back)
        + reverse_product(d_picked_two, feedforward_input_maps)
    )
    grad_middle = output_gradient + normed_back(
        middle, scale_two, feedforward_norm_gain, d_normed_two
    )
    grad_b_mlp = jnp.stack(
        [
            gate_output_gradient.reshape(adapter_table, adapter_rank_size, -1),
            upward_output_gradient.reshape(adapter_table, adapter_rank_size, -1),
        ]
    )
    mlp_terms = (
        feedforward_input_gradient.reshape(feedforward_entry_maps.shape),
        grad_b_mlp,
        down_input_gradient.reshape(down_entry_maps.shape),
        down_output_gradient.reshape(down_exit_maps.shape),
    )
    attn_back = (
        lax.all_gather(query_weight, "wsh", axis=0, tiled=True),
        lax.all_gather(key_weight, "wsh", axis=0, tiled=True),
        lax.all_gather(value_weight, "wsh", axis=0, tiled=True),
        lax.all_gather(output_weight, "wsh", axis=0, tiled=True),
    )
    query_back, key_back, value_back, out_back = attn_back
    attention_gradient = (RESIDUAL_MULT * grad_middle).astype(jnp.bfloat16)
    output_output_gradient = gradient_product(
        selected_output.reshape(token_rows, -1), attention_gradient
    )
    d_picked_out = (
        reverse_product(attention_gradient, output_output_maps)
        .reshape(token_rows, adapter_table, adapter_rank_size)
        .astype(jnp.bfloat16)
        * choose_low[:, :, None]
    )
    d_picked_out = d_picked_out.reshape(token_rows, -1)
    output_input_gradient = gradient_product(attention_result, d_picked_out)
    d_attended = (
        reverse_product(attention_gradient, out_back)
        + reverse_product(d_picked_out, output_input_maps)
    ).astype(jnp.bfloat16)
    d_heads = lax.all_to_all(d_attended, "seq", split_axis=1, concat_axis=0, tiled=True)
    d_heads_four = d_heads.reshape(token_length, kv_dev, per_kv, HEAD_WIDTH)

    def backward_block(running_totals, block_items):
        d_key_sum, d_value_sum = running_totals
        block_index, log_total = block_items
        first_row = block_index * block_rows
        logits, query_rows = scores_of(first_row)
        probs = jnp.exp(logits - log_total[..., None])
        d_rows = lax.dynamic_slice_in_dim(d_heads_four, first_row, block_rows, 0)
        d_probs = jnp.einsum(
            "qkgd,skd->kgqs", d_rows, value_three, preferred_element_type=jnp.float32
        )
        inner = jnp.sum(probs * d_probs, axis=-1, keepdims=True)
        d_logits = (probs * (d_probs - inner)).astype(jnp.bfloat16)
        d_query_rows = SCORE_MULT * jnp.einsum(
            "kgqs,skd->qkgd", d_logits, key_three, preferred_element_type=jnp.float32
        )
        d_key_sum = d_key_sum + SCORE_MULT * jnp.einsum(
            "kgqs,qkgd->skd", d_logits, query_rows, preferred_element_type=jnp.float32
        )
        d_value_sum = d_value_sum + jnp.einsum(
            "kgqs,qkgd->skd", probs.astype(jnp.bfloat16), d_rows, preferred_element_type=jnp.float32
        )
        return ((d_key_sum, d_value_sum), d_query_rows.astype(jnp.bfloat16).reshape(block_rows, -1))

    zero_keys = jnp.zeros((token_length, kv_dev, HEAD_WIDTH), jnp.float32)
    (d_key_sum, d_value_sum), d_query_blocks = lax.scan(
        backward_block, (zero_keys, zero_keys), (block_ids, log_totals)
    )
    d_query_heads = d_query_blocks.reshape(token_length, -1)
    d_key_heads = d_key_sum.astype(jnp.bfloat16).reshape(token_length, -1)
    d_value_heads = d_value_sum.astype(jnp.bfloat16).reshape(token_length, -1)
    d_query_rot, d_key_rot, value_gradient = (
        lax.all_to_all(d_query_heads, "seq", split_axis=0, concat_axis=1, tiled=True),
        lax.all_to_all(d_key_heads, "seq", split_axis=0, concat_axis=1, tiled=True),
        lax.all_to_all(d_value_heads, "seq", split_axis=0, concat_axis=1, tiled=True),
    )
    query_gradient = (
        rotate_back(
            d_query_rot.astype(jnp.float32).reshape(token_rows, QUERY_HEADS, HEAD_WIDTH),
            cos_tab,
            sin_tab,
        )
        .reshape(token_rows, -1)
        .astype(jnp.bfloat16)
    )
    key_gradient = (
        rotate_back(
            d_key_rot.astype(jnp.float32).reshape(token_rows, KEY_HEADS, HEAD_WIDTH),
            cos_tab,
            sin_tab,
        )
        .reshape(token_rows, -1)
        .astype(jnp.bfloat16)
    )
    query_output_gradient = gradient_product(
        rank_columns(selected_first, 0, adapter_rank_size), query_gradient
    )
    key_output_gradient = gradient_product(
        rank_columns(selected_first, adapter_rank_size, 2 * adapter_rank_size), key_gradient
    )
    value_output_gradient = gradient_product(
        rank_columns(selected_first, 2 * adapter_rank_size, 3 * adapter_rank_size), value_gradient
    )
    d_picked_one = jnp.concatenate(
        [
            reverse_product(query_gradient, query_output_maps).reshape(
                token_rows, adapter_table, adapter_rank_size
            ),
            reverse_product(key_gradient, key_output_maps).reshape(
                token_rows, adapter_table, adapter_rank_size
            ),
            reverse_product(value_gradient, value_output_maps).reshape(
                token_rows, adapter_table, adapter_rank_size
            ),
        ],
        axis=2,
    )
    d_picked_one = (d_picked_one.astype(jnp.bfloat16) * choose_low[:, :, None]).reshape(
        token_rows, -1
    )
    attention_input_gradient = gradient_product(first_normed, d_picked_one)
    d_normed_one = (
        reverse_product(query_gradient, query_back)
        + reverse_product(key_gradient, key_back)
        + reverse_product(value_gradient, value_back)
        + reverse_product(d_picked_one, attention_input_maps)
    )
    hidden_gradient = grad_middle + normed_back(
        hidden_state, scale_one, attention_norm_gain, d_normed_one
    )
    grad_b_kv = jnp.stack(
        [
            key_output_gradient.reshape(adapter_table, adapter_rank_size, -1),
            value_output_gradient.reshape(adapter_table, adapter_rank_size, -1),
        ]
    )
    attn_terms = (
        attention_input_gradient.reshape(attention_down_maps.shape),
        query_output_gradient.reshape(query_exit_maps.shape),
        grad_b_kv,
        output_input_gradient.reshape(output_entry_maps.shape),
        output_output_gradient.reshape(output_exit_maps.shape),
    )
    summed = lax.psum(attn_terms + mlp_terms, ("seq", "wsh"))
    return (layer_out, hidden_gradient[None]) + tuple(summed)


def solution(mesh):
    in_specs = (
        P("wsh", "seq", None),
        P("wsh", "seq"),
        P("wsh", None),
        P(),
        P(),
        P("wsh", None),
        P("wsh", None),
        P("wsh", None),
        P("wsh", None),
        P("wsh", None),
        P("wsh", None),
        P("wsh", None),
        P(),
        P(),
        P(),
        P(),
        P(),
        P(),
        P(),
        P(),
        P(),
        P("wsh", "seq", None),
    )
    out_specs = (
        P("wsh", "seq", None),
        P("wsh", "seq", None),
        P(),
        P(),
        P(),
        P(),
        P(),
        P(),
        P(),
        P(),
        P(),
    )
    return jax.shard_map(
        on_device, mesh=mesh, in_specs=in_specs, out_specs=out_specs, check_vma=False
    )
```

profile of v0, /device:TPU:0, one launch (start us, length us, event | category | flops | bytes accessed | tf_op | source)
XLA Modules:
  0.0 2948.2 jit_solution(18061158279480522673)
XLA Ops:
  19.7 42.3 %all-gather.11.cloned.1.call-done = bf16[2048,512]{1,0:T(8,128)(2,1)} async-done(((bf16[256,512]{1,0:T(8,128)(2,1)}), bf16[2048,512]{1,0:T(8,128)(2,1)}) %all-gather.11.cloned.1.call-update) | async-done | bytes 2097168 | tf_op jit(solution)/shard_map/all_gather | solution.py:135
  72.5 39.3 %all-gather.13.cloned.1.call-done = bf16[2048,512]{1,0:T(8,128)(2,1)} async-done(((bf16[256,512]{1,0:T(8,128)(2,1)}), bf16[2048,512]{1,0:T(8,128)(2,1)}) %all-gather.13.cloned.1.call-update) | async-done | bytes 2097168 | tf_op jit(solution)/shard_map/all_gather | solution.py:136
  114.9 122.0 %all-gather.9.cloned.1.call-done = bf16[2048,2048]{1,0:T(8,128)(2,1)} async-done(((bf16[256,2048]{1,0:T(8,128)(2,1)}), bf16[2048,2048]{1,0:T(8,128)(2,1)}) %all-gather.9.cloned.1.call-update) | async-done | bytes 8388624 | tf_op jit(solution)/shard_map/all_gather | solution.py:134
  266.9 10.5 all-gather
  287.8 37.5 %while.28 = (s32[]{:T(128)}, bf16[2,512,512]{2,1,0:T(8,128)(2,1)}, f32[2,2,4,512]{3,2,1,0:T(4,128)S(1)}, s32[2]{0:T(128)S(1)}, s32[1024]{0:T(1024)S(1)}, /*index...) while((s32[]{:T(128)}, bf16[2,512,512]{2,1,0:T(8,128)(2,1)}, ...), condition=%wide.region_5.6_spmd.clone, body=%wide.region_2.5_spmd.clone.sunk | while | flops 1125904896 | bytes 57293528 | solution.py:209
  334.5 9.8 all-to-all-done.3
  371.0 627.9 %all-gather.19.cloned.1.call-done = bf16[2048,8192]{1,0:T(8,128)(2,1)} async-done(((bf16[256,8192]{1,0:T(8,128)(2,1)}), bf16[2048,8192]{1,0:T(8,128)(2,1)}) %all-gather.19.cloned.1.call-update) | async-done | bytes 33554448 | tf_op jit(solution)/shard_map/all_gather | solution.py:221
  998.9 18.8 fusion.187
  1025.7 612.2 %all-gather.17.cloned.1.call-done = bf16[2048,8192]{1,0:T(8,128)(2,1)} async-done(((bf16[256,8192]{1,0:T(8,128)(2,1)}), bf16[2048,8192]{1,0:T(8,128)(2,1)}) %all-gather.17.cloned.1.call-update) | async-done | bytes 33554448 | tf_op jit(solution)/shard_map/all_gather | solution.py:220
  1637.9 19.8 fusion.186
  1657.7 619.4 %all-gather.21.cloned.1.call-done = bf16[8192,2048]{1,0:T(8,128)(2,1)} async-done(((bf16[1024,2048]{1,0:T(8,128)(2,1)}), bf16[8192,2048]{1,0:T(8,128)(2,1)}) %all-gather.21.cloned.1.call-update) | async-done | bytes 33554448 | tf_op jit(solution)/shard_map/all_gather | solution.py:222
  2277.1 21.3 convolution_add_fusion.2
  2298.4 13.4 multiply_convert_fusion.1
  2326.5 16.9 fusion.188
  2343.4 19.4 multiply_reduce_fusion
  2395.7 109.5 %while.29 = (s32[]{:T(128)}, f32[1024,2,64]{0,2,1:T(8,128)S(1)}, f32[1024,2,64]{0,2,1:T(8,128)}, bf16[2,512,512]{2,1,0:T(8,128)(2,1)}, s32[2]{0:T(128)S(1)}, /*i...) while((s32[]{:T(128)}, f32[1024,2,64]{0,2,1:T(8,128)S(1)}, ...), condition=%wide.region_10.11_spmd.clone, body=%wide.region_8.10_spmd.clone.sunk | while | flops 2750018048 | bytes 181795728 | solution.py:363
  2406.2 12.1 fusion.279
  2418.3 12.0 fusion.280
  2452.5 8.2 fusion.277
  2460.7 12.1 fusion.279
  2472.8 12.0 fusion.280
  2530.6 12.3 all-to-all-done.5
  2555.6 19.2 fusion.77
  2587.2 335.8 %all-reduce.3.cloned.1.call-done = (f32[2048,8,48]{0,2,1:T(8,128)}, f32[8,16,2048]{2,1,0:T(8,128)}, f32[2,8,16,512]{3,2,1,0:T(8,128)}, f32[2048,8,16]{0,2,1:T(8,...) async-done(((f32[2048,8,48]{0,2,1:T(8,128)}, ...) | async-done | bytes 22544400 | tf_op jit(solution)/shard_map/psum | solution.py:441
  (375 shorter events, 312.6 us)
Async XLA Ops:
  7.2 322.6 %copy-start = (bf16[8192,8,16]{0,2,1:T(8,128)(2,1)S(1)}, bf16[8192,8,16]{0,2,1:T(8,128)(2,1)}, u32[]{:S(2)}) copy-start(bf16[8192,8,16]{0,2,1:T(8,128)(2,1)} %param.45) | copy-start | bytes 6291460
  7.2 54.8 %all-gather.11.cloned.1.call-start = ((), (), s32[]{:S(2)}) async-start(), calls=%async_computation.9 | async-start | bytes 2359296 | tf_op jit(solution)/shard_map/all_gather | solution.py:135
  7.9 103.8 %all-gather.13.cloned.1.call-start = ((), (), s32[]{:S(2)}) async-start(), calls=%async_computation.10 | async-start | bytes 2359296 | tf_op jit(solution)/shard_map/all_gather | solution.py:136
  8.7 228.2 %all-gather.9.cloned.1.call-start = ((), (), s32[]{:S(2)}) async-start(), calls=%async_computation.8 | async-start | bytes 9437184 | tf_op jit(solution)/shard_map/all_gather | solution.py:134
  9.4 352.2 %all-gather.15.cloned.1.call-start = ((), (), s32[]{:S(2)}) async-start(), calls=%async_computation.11 | async-start | bytes 9437184 | tf_op jit(solution)/shard_map/all_gather | solution.py:137
  10.0 988.9 %all-gather.19.cloned.1.call-start = ((), (), s32[]{:S(2)}) async-start(), calls=%async_computation.13 | async-start | bytes 37748736 | tf_op jit(solution)/shard_map/all_gather | solution.py:221
  10.6 1627.3 %all-gather.17.cloned.1.call-start = ((), (), s32[]{:S(2)}) async-start(), calls=%async_computation.12 | async-start | bytes 37748736 | tf_op jit(solution)/shard_map/all_gather | solution.py:220
  11.2 2265.9 %all-gather.21.cloned.1.call-start = ((), (), s32[]{:S(2)}) async-start(), calls=%async_computation.14 | async-start | bytes 37748736 | tf_op jit(solution)/shard_map/all_gather | solution.py:222
  13.3 223.6 %copy-start.72 = (f32[256]{0:T(256)}, f32[256]{0:T(256)S(1)}, u32[]{:S(2)}) copy-start(f32[256]{0:T(256)S(1)} %get-tuple-element.276) | copy-start | bytes 3076
  13.3 264.1 %copy-start.50 = (bf16[256,8]{0,1:T(8,128)(2,1)}, bf16[256,8]{0,1:T(8,128)(2,1)S(1)}, u32[]{:S(2)}) copy-start(bf16[256,8]{0,1:T(8,128)(2,1)S(1)} %get-tuple-element.279) | copy-start | bytes 12292
  13.5 237.6 %copy-start.46 = (f32[256,32]{0,1:T(8,128)}, f32[256,32]{0,1:T(8,128)S(1)}, u32[]{:S(2)}) copy-start(f32[256,32]{0,1:T(8,128)S(1)} %get-tuple-element.273) | copy-start | bytes 98308
  13.5 237.6 %copy-start.48 = (f32[256,32]{0,1:T(8,128)}, f32[256,32]{0,1:T(8,128)S(1)}, u32[]{:S(2)}) copy-start(f32[256,32]{0,1:T(8,128)S(1)} %get-tuple-element.274) | copy-start | bytes 98308
  69.0 178.7 %all-to-all-start.1 = ((bf16[256,4,128]{0,2,1:T(8,128)(2,1)}), bf16[256,4,128]{0,2,1:T(8,128)(2,1)S(1)}, u32[]{:S(2)}, u32[]{:S(2)}) async-start(bf16[256,4,128]{0,2,1:T(8,128)(2,1)} %bitcast.516), calls=%async_computation.1 | async-start | bytes 524288 | tf_op jit(solution)/shard_map/all_to_all | solution.py:168
  247.7 9.4 all-to-all-start.2
  257.8 24.2 all-to-all-start
  325.3 19.0 all-to-all-start.3
  370.5 647.2 %copy-start.43 = (bf16[256,2048]{1,0:T(8,128)(2,1)}, bf16[256,2048]{1,0:T(8,128)(2,1)S(1)}, u32[]{:S(2)}) copy-start(bf16[256,2048]{1,0:T(8,128)(2,1)S(1)} %multiply_convert_fusion.4) | copy-start | bytes 3145732
  1025.7 1251.4 %copy-start.20 = (bf16[1,256,2048]{2,1,0:T(8,128)(2,1)S(1)}, bf16[1,256,2048]{2,1,0:T(8,128)(2,1)}, u32[]{:S(2)}) copy-start(bf16[1,256,2048]{2,1,0:T(8,128)(2,1)} %param.47) | copy-start | bytes 3145732
  2372.7 17.9 all-to-all-start.4
  2395.6 114.0 %copy-start.69 = (bf16[256,8,16]{0,2,1:T(8,128)(2,1)S(1)}, bf16[256,8,16]{0,2,1:T(8,128)(2,1)}, u32[]{:S(2)}) copy-start(bf16[256,8,16]{0,2,1:T(8,128)(2,1)} %fusion.109) | copy-start | bytes 196612
  2506.2 9.4 all-to-all-start.6
  2515.6 9.4 all-to-all-start.7
  2525.0 17.9 all-to-all-start.5
  2528.5 394.5 %all-reduce.3.cloned.1.call-start = ((), (), s32[]{:S(2)}) async-start(), calls=%async_computation.15 | async-start | bytes 45088768 | tf_op jit(solution)/shard_map/psum | solution.py:441
  (88 other events, 505.3 us)
Sparse Core Ops, SparseCore 0:
  10.1 51.7 all-gather.10
  64.1 47.6 all-gather.12
  113.9 122.9 all-gather.8
  238.9 122.6 all-gather.14
  363.0 635.8 all-gather.18
  1000.2 637.6 all-gather.16
  1639.4 637.6 all-gather.20
  2552.7 370.2 all-reduce.2
where the time goes:
time: 2960 us; the launch traced here: 2950 us
  waiting for transfers between devices  2440 us (82%)
  matrix products  308 us (10%)
  local copies, waits for them, and re-layouts  83.3 us (3%)
  other arithmetic  53.1 us (2%)
  starting transfers between devices  29.7 us (1%)
    all_gather x1, waiting for transfers between devices, on_device(): lax.all_gather(up_weight, 'wsh', axis=0, tiled=True)  628 us
    all_gather x1, waiting for transfers between devices, on_device(): lax.all_gather(down_weight, 'wsh', axis=0, tiled=True)  619 us
    all_gather x1, waiting for transfers between devices, on_device(): lax.all_gather(gate_weight, 'wsh', axis=0, tiled=True)  612 us
    psum x1, waiting for transfers between devices, on_device(): summed = lax.psum(attn_terms + mlp_terms, ('seq', 'wsh'))  336 us
    all_gather x1, waiting for transfers between devices, on_device(): lax.all_gather(query_weight, 'wsh', axis=0, tiled=True)  122 us
    dot_general x18, matrix products, low_dot(): return jnp.dot(left, right, preferred_element_type=jnp.float32)  117 us
    dot_general x18, matrix products, reverse_product(): lax.dot_general(left, right, (((1,), (1,)), ((), ())), preferred_element_...  81.8 us
  transfers between devices with their start and end apart: 16, of which 14 were waited for; matrix products, arithmetic and copies ran while one was open for 7% of the time, Pallas kernels for 0%

commit v1 on v0

v1 whole, which is shorter than its diff:
```python
import functools

import jax
import jax.numpy as jnp
from jax import lax
from jax.experimental import pallas as pl
from jax.experimental.pallas import tpu as pltpu
from jax.sharding import PartitionSpec as P

QUERY_HEADS = 32
KEY_HEADS = 8
HEAD_WIDTH = 64
LANES = 128
PACK = 512
TILE = 256

EPSILON = 1e-05
RESIDUAL_MULT = 0.22
SCORE_MULT = 0.015625
ROPE_BASE = 10000000.0
MASKED = -1e30

BF = jnp.bfloat16
F32 = jnp.float32

CORE_SWAP = [(s, s ^ 1) for s in range(4)]
Y_SWAP = [(s, s ^ 2) for s in range(4)]
X_SWAP = [(w, w ^ 1) for w in range(8)]


def z_shift(steps):
    return [(2 * z + x, 2 * ((z + steps) % 4) + x) for z in range(4) for x in range(2)]


def low_dot(left, right):
    return jnp.dot(left, right, preferred_element_type=F32)


def gradient_product(left, right):
    return lax.dot_general(left, right, (((0,), (0,)), ((), ())), preferred_element_type=F32)


def reverse_product(left, right):
    return lax.dot_general(left, right, (((1,), (1,)), ((), ())), preferred_element_type=F32)


def normed(values, gain):
    norm_scale = lax.rsqrt(jnp.mean(values * values, axis=-1, keepdims=True) + EPSILON)
    return (values * norm_scale * gain, norm_scale)


def normed_back(values, norm_scale, gain, grad_in):
    scaled = grad_in * gain
    cubed = norm_scale * norm_scale * norm_scale
    return norm_scale * scaled - values * cubed * jnp.mean(scaled * values, axis=-1, keepdims=True)


def rope_tables(positions, head_size):
    half_size = head_size // 2
    inv_freq = ROPE_BASE ** (-(jnp.arange(half_size).astype(F32) * 2.0) / head_size)
    angles = positions.astype(F32)[:, None] * inv_freq[None, :]
    return (jnp.cos(angles)[:, None, :], jnp.sin(angles)[:, None, :])


def rotate(values, cos_tab, sin_tab):
    half_size = values.shape[-1] // 2
    former = values[..., :half_size]
    latter = values[..., half_size:]
    return jnp.concatenate(
        [former * cos_tab - latter * sin_tab, latter * cos_tab + former * sin_tab], axis=-1
    )


def cut(values, start, size, axis):
    return lax.dynamic_slice_in_dim(values, start, size, axis)


def pick(values, index, axis):
    return lax.dynamic_index_in_dim(values, index, axis, keepdims=False)


def adapter_mask(owner, ranks, adapters):
    lane = jnp.arange(adapters * ranks, dtype=jnp.int32) // ranks
    return (owner[:, None] == lane[None, :]).astype(F32)


def fold(masked, ranks, offset):
    rows = jnp.arange(masked.shape[1], dtype=jnp.int32) % ranks
    lanes = jnp.arange(LANES, dtype=jnp.int32) - offset
    return low_dot(masked.astype(BF), (rows[:, None] == lanes[None, :]).astype(BF))


def spread(folded, owner, ranks, offset, adapters):
    rows = jnp.arange(LANES, dtype=jnp.int32) - offset
    lanes = jnp.arange(adapters * ranks, dtype=jnp.int32) % ranks
    wide = low_dot(folded.astype(BF), (rows[:, None] == lanes[None, :]).astype(BF))
    return (wide * adapter_mask(owner, ranks, adapters)).astype(BF)


def pack(values):
    parts = [values[:, i : i + PACK] for i in range(0, values.shape[1], PACK)]
    return jnp.concatenate(parts, axis=0)


class Mover:
    def __init__(self, seq_size, wsh_size):
        self.seq_size, self.wsh_size = seq_size, wsh_size
        self.fast = seq_size == 4 and wsh_size == 8
        self.s, self.w = lax.axis_index("seq"), lax.axis_index("wsh")
        self.y, self.c = self.s // 2, self.s % 2
        self.z, self.x = self.w // 2, self.w % 2
        self.lanes = {"x": [], "y": [], "z": []}
        self.depth = 6

    def send(self, values, axis, pairs, lane, depth=2):
        sent = self.lanes[lane]
        if len(sent) >= depth:
            values, _ = lax.optimization_barrier((values, sent[-depth]))
        result = lax.ppermute(values, axis, pairs)
        sent.append(result)
        return result

    def gather_rows(self, chunk):
        if not self.fast:
            return lax.all_gather(chunk, "wsh", axis=0, tiled=True)
        slots = []
        for r in range(4):
            held = chunk
            if r:
                held = self.send(chunk, "wsh", z_shift(r), "z", self.depth)
            slots += [held, self.send(held, "wsh", X_SWAP, "x", self.depth)]
        return jnp.concatenate(slots, axis=0)

    def slot_owner(self, k):
        if not self.fast:
            return k
        return 2 * ((self.z - k // 2) % 4) + (self.x ^ (k % 2))

    def slot_of(self, w):
        if not self.fast:
            return w
        return 2 * ((self.z - w // 2) % 4) + (self.x ^ (w % 2))

    def to_slots(self, values, block):
        if not self.fast:
            return values
        parts = [cut(values, self.slot_owner(k) * block, block, 1) for k in range(self.wsh_size)]
        return jnp.concatenate(parts, axis=1)

    def from_slots(self, values, block):
        if not self.fast:
            return values
        parts = [cut(values, self.slot_of(w) * block, block, 1) for w in range(self.wsh_size)]
        return jnp.concatenate(parts, axis=1)

    def head_rows(self, weight):
        rows = weight.shape[0]
        per = self.wsh_size // self.seq_size
        if not self.fast:
            return cut(
                lax.all_gather(weight, "wsh", axis=0, tiled=True),
                self.s * per * rows,
                per * rows,
                0,
            )
        piece = rows // 4
        mine = jnp.where(self.z == self.s, cut(weight, self.z * piece, piece, 0), 0)
        for r in range(1, 4):
            pairs = [
                (8 * s + 2 * s + x, 8 * s + 2 * ((s + r) % 4) + x)
                for s in range(4)
                for x in range(2)
            ]
            out = cut(weight, ((self.z + r) % 4) * piece, piece, 0)
            mine = mine + self.send(out, ("seq", "wsh"), pairs, "z", self.depth)
        return mine

    def head_rows_done(self, slots, rows):
        if not self.fast:
            return slots
        piece = rows // 4
        blocks = slots.reshape(4, 2, piece, slots.shape[1])
        out = []
        for shard in range(2):
            for j in range(4):
                one = pick(blocks, (self.z - j) % 4, 0)
                out.append(pick(one, self.x ^ shard, 0))
        return jnp.concatenate(out, axis=0)

    def gather_tokens(self, values):
        if not self.fast:
            return lax.all_gather(values, "seq", axis=0, tiled=True)
        other = self.send(values, "seq", Y_SWAP, "y")
        first = self.y == 0
        column = jnp.stack([jnp.where(first, values, other), jnp.where(first, other, values)])
        partner = lax.ppermute(column, "seq", CORE_SWAP)
        first = self.c == 0
        whole = jnp.stack(
            [jnp.where(first, column, partner), jnp.where(first, partner, column)], axis=1
        )
        return whole.reshape((4 * values.shape[0],) + values.shape[1:])

    def scatter_tokens(self, *partials):
        if not self.fast:
            return [
                lax.psum_scatter(v.astype(BF), "seq", scatter_dimension=0, tiled=True).astype(F32)
                for v in partials
            ]
        rows = partials[0].shape[0] // 4
        blocks = [v.reshape(2, 2, rows, v.shape[1]) for v in partials]
        out = jnp.concatenate([pick(v, 1 - self.c, 1).astype(BF) for v in blocks], axis=2)
        got = lax.ppermute(out, "seq", CORE_SWAP).astype(F32)
        mine = jnp.concatenate([pick(v, self.c, 1) for v in blocks], axis=2)
        away = (pick(mine, 1 - self.y, 0) + pick(got, 1 - self.y, 0)).astype(BF)
        other = self.send(away, "seq", Y_SWAP, "y").astype(F32)
        total = pick(mine, self.y, 0) + pick(got, self.y, 0) + other
        found, at = [], 0
        for v in partials:
            found.append(total[:, at : at + v.shape[1]])
            at += v.shape[1]
        return found

    def sum_small(self, partial):
        if not self.fast:
            return lax.psum(partial, "seq")
        total = partial.astype(F32) + lax.ppermute(partial, "seq", CORE_SWAP).astype(F32)
        other = self.send(total.astype(BF), "seq", Y_SWAP, "y")
        return total + other.astype(F32)

    def sum_plain(self, grad):
        total = lax.psum(grad.astype(BF), "wsh")
        return lax.all_gather(total.astype(BF), "seq", axis=0).astype(F32)

    def sum_hidden(self, grads, hid_block):
        if not self.fast:
            found = []
            for grad in grads:
                rows = grad.shape[0]
                wide = self.sum_plain(grad).reshape(self.seq_size, rows, self.wsh_size, hid_block)
                found.append(wide.transpose(1, 2, 0, 3).reshape(rows, -1))
            return [jnp.stack(found[:2]), found[2]]
        parts = self.sum_gather(jnp.concatenate([pack(v) for v in grads], axis=0))
        s = self.s.astype(jnp.int32)[None]
        return [
            final_hidden(parts, s, 0, 2),
            final_hidden(parts, s, 8 * LANES, 1)[0],
        ]

    def sum_features(self, grads, key=None, value=None):
        if not self.fast:
            grads = grads + ([key, value] if key is not None else [])
            found = []
            for grad in grads:
                found.append(self.sum_plain(grad).transpose(1, 0, 2).reshape(grad.shape[0], -1))
            return found[:-2] + [jnp.stack(found[-2:])] if key is not None else found
        packed = list(grads)
        if key is not None:
            rest = jnp.zeros((key.shape[0], PACK - 2 * LANES), F32)
            packed.append(jnp.concatenate([key, value, rest], axis=1))
        parts = self.sum_gather(jnp.concatenate(packed, axis=0))
        s = self.s.astype(jnp.int32)[None]
        found, at = [], 0
        for grad in grads:
            found.append(final_features(parts, s, at, grad.shape[0]))
            at += grad.shape[0]
        if key is not None:
            found.append(final_kv(parts, s, at))
        return found

    def sum_gather(self, packed):
        rows = packed.shape[0]
        halves = packed.reshape(2, rows // 2, PACK)
        got = self.send(pick(halves, 1 - self.x, 0).astype(BF), "wsh", X_SWAP, "x")
        half = pick(halves, self.x, 0) + got.astype(F32)
        blocks = half.reshape(4, rows // 8, PACK)
        total = pick(blocks, self.z, 0)
        for r in range(1, 4):
            out = pick(blocks, (self.z + r) % 4, 0).astype(BF)
            total = total + self.send(out, "wsh", z_shift(r), "z", 3).astype(F32)
        own = total.astype(BF)
        got = [own] + [self.send(own, "wsh", z_shift(r), "z", 3) for r in range(1, 4)]
        ring = jnp.stack(got)
        half = jnp.concatenate([pick(ring, (self.z - j) % 4, 0) for j in range(4)], axis=0)
        other = self.send(half, "wsh", X_SWAP, "x")
        first = self.x == 0
        part = jnp.concatenate([jnp.where(first, half, other), jnp.where(first, other, half)])
        core = lax.ppermute(part, "seq", CORE_SWAP)
        other = self.send(part, "seq", Y_SWAP, "y")
        return part, core, other, lax.ppermute(other, "seq", CORE_SWAP)


def choose_part(s_ref, parts, out_ref, axis):
    k = s_ref[0] ^ pl.program_id(axis)
    low = jnp.where(k % 2 == 0, parts[0][...], parts[1][...])
    high = jnp.where(k % 2 == 0, parts[2][...], parts[3][...])
    value = jnp.where(k < 2, low, high).astype(F32)
    out_ref[...] = value.reshape(out_ref.shape)


def final_call(parts, s, grid, part_block, part_map, out_shape, out_block, out_map):
    def body(s_ref, a, b, c, d, out_ref):
        choose_part(s_ref, (a, b, c, d), out_ref, len(grid) - 1)

    return pl.pallas_call(
        body,
        grid_spec=pltpu.PrefetchScalarGridSpec(
            num_scalar_prefetch=1,
            grid=grid,
            in_specs=[pl.BlockSpec(part_block, part_map)] * 4,
            out_specs=pl.BlockSpec(out_block, out_map),
        ),
        out_shape=jax.ShapeDtypeStruct(out_shape, F32),
        name="finish",
    )(s, *parts)


def final_features(parts, s, row, rows):
    at = row // LANES
    return final_call(
        parts,
        s,
        (rows // LANES, 4),
        (LANES, PACK),
        lambda i, j, _: (at + i, 0),
        (rows, 4 * PACK),
        (LANES, PACK),
        lambda i, j, _: (i, j),
    )


def final_hidden(parts, s, row, count):
    at = row // LANES
    return final_call(
        parts,
        s,
        (count, 8, 4),
        (LANES, TILE),
        lambda n, w, j, _: (at + 4 * n + w // 2, w % 2),
        (count, LANES, 32 * TILE),
        (1, LANES, TILE),
        lambda n, w, j, _: (n, 0, 4 * w + j),
    )


def final_kv(parts, s, row):
    at = row // LANES
    return final_call(
        parts,
        s,
        (2, 4),
        (LANES, LANES),
        lambda n, j, _: (at, n),
        (2, LANES, 4 * LANES),
        (1, LANES, LANES),
        lambda n, j, _: (n, 0, j),
    )


def half_lanes(rows, half):
    lane = lax.broadcasted_iota(jnp.int32, (rows, LANES), 1)
    return (lane < HEAD_WIDTH) if half == 0 else (lane >= HEAD_WIDTH)


def turn(values, cos_tab, sin_tab):
    lane = lax.broadcasted_iota(jnp.int32, values.shape, 1)
    swapped = jnp.where(
        lane % HEAD_WIDTH < HEAD_WIDTH // 2,
        pltpu.roll(values, LANES - HEAD_WIDTH // 2, 1),
        pltpu.roll(values, HEAD_WIDTH // 2, 1),
    )
    return values * cos_tab + swapped * sin_tab


def twice(values, half):
    other = pltpu.roll(values, HEAD_WIDTH, 1)
    first = half_lanes(values.shape[0], 0)
    return jnp.where(first, values, other) if half == 0 else jnp.where(first, other, values)


def qkv_body(x_ref, w_ref, la_q, la_k, la_v, exit_q, exit_kv, cos_ref, sin_ref, q_ref, k_ref, v_ref):
    cos_tab, sin_tab = cos_ref[...], sin_ref[...]
    product = low_dot(x_ref[...], w_ref[...])
    q_cols = q_ref.shape[1]
    query = product[:, :q_cols] + low_dot(la_q[...], exit_q[...])
    for i in range(0, q_cols, LANES):
        q_ref[:, i : i + LANES] = turn(query[:, i : i + LANES], cos_tab, sin_tab).astype(BF)
    key = product[:, q_cols : q_cols + LANES] + low_dot(la_k[...], exit_kv[0])
    key = turn(key, cos_tab, sin_tab)
    value = product[:, q_cols + LANES :] + low_dot(la_v[...], exit_kv[1])
    for half in range(2):
        k_ref[:, half * LANES : (half + 1) * LANES] = twice(key, half).astype(BF)
        v_ref[:, half * LANES : (half + 1) * LANES] = twice(value, half).astype(BF)


def qkv_call(x, weights, la_q, la_k, la_v, exit_q, exit_kv, cos_tab, sin_tab):
    rows, width = x.shape[0], weights.shape[0]
    q_cols = exit_q.shape[1]

    def tile(columns):
        return pl.BlockSpec((TILE, columns), lambda i: (i, 0))

    return pl.pallas_call(
        qkv_body,
        grid=(rows // TILE,),
        in_specs=[
            tile(width),
            pl.BlockSpec(weights.shape, lambda i: (0, 0)),
            tile(LANES),
            tile(LANES),
            tile(LANES),
            pl.BlockSpec(exit_q.shape, lambda i: (0, 0)),
            pl.BlockSpec(exit_kv.shape, lambda i: (0, 0, 0)),
            tile(LANES),
            tile(LANES),
        ],
        out_specs=[tile(q_cols), tile(2 * LANES), tile(2 * LANES)],
        out_shape=[
            jax.ShapeDtypeStruct((rows, q_cols), BF),
            jax.ShapeDtypeStruct((rows, 2 * LANES), BF),
            jax.ShapeDtypeStruct((rows, 2 * LANES), BF),
        ],
        name="qkv",
        cost_estimate=pl.CostEstimate(
            flops=2 * rows * width * weights.shape[1], bytes_accessed=12 << 20, transcendentals=0
        ),
    )(x, weights, la_q, la_k, la_v, exit_q, exit_kv, cos_tab, sin_tab)


def allowed_pairs(i, t, doc_col, doc_row):
    start = pl.multiple_of(t * TILE, TILE)
    rows = i * TILE + lax.broadcasted_iota(jnp.int32, (TILE, TILE), 0)
    keys = start + lax.broadcasted_iota(jnp.int32, (TILE, TILE), 1)
    return (doc_col[...] == doc_row[:, pl.ds(start, TILE)]) & (keys <= rows)


def forward_body(first_ref, q_ref, k_ref, v_ref, doc_col, doc_row, o_ref, lse_ref, m_s, l_s, acc_s):
    i = pl.program_id(1)
    m_s[...] = jnp.full_like(m_s, MASKED)
    l_s[...] = jnp.zeros_like(l_s)
    acc_s[...] = jnp.zeros_like(acc_s)

    def step(t, carry):
        allowed = allowed_pairs(i, t, doc_col, doc_row)
        start = pl.multiple_of(t * TILE, TILE)
        keys, vals = k_ref[pl.ds(start, TILE), :], v_ref[pl.ds(start, TILE), :]
        for h in range(4):
            pair = q_ref[:, (h // 2) * LANES : (h // 2 + 1) * LANES]
            query = jnp.where(half_lanes(TILE, h % 2), pair, jnp.zeros_like(pair))
            logits = jnp.where(allowed, SCORE_MULT * reverse_product(query, keys), MASKED)
            old = m_s[h]
            top = jnp.maximum(old, jnp.max(logits, axis=1, keepdims=True))
            shrink = jnp.exp(old - top)
            shifted = jnp.exp(logits - top)
            m_s[h] = top
            l_s[h] = l_s[h] * shrink + jnp.sum(shifted, axis=1, keepdims=True)
            acc_s[h] = acc_s[h] * shrink + low_dot(shifted.astype(BF), vals)
        return carry

    lax.fori_loop(first_ref[i], i + 1, step, 0)
    lane = lax.broadcasted_iota(jnp.int32, (TILE, LANES), 1)
    total = jnp.zeros((TILE, LANES), F32)
    for p in range(2):
        both = [acc_s[2 * p + n] / l_s[2 * p + n] for n in range(2)]
        o_ref[:, p * LANES : (p + 1) * LANES] = jnp.where(
            half_lanes(TILE, 0), both[0], both[1]
        ).astype(BF)
    for h in range(4):
        total = jnp.where(lane == h, m_s[h] + jnp.log(l_s[h]), total)
    lse_ref[...] = total


def attention_call(first, query, keys, values, doc_col, doc_row):
    rows = query.shape[0]
    group = query.shape[1] // 2
    return pl.pallas_call(
        forward_body,
        grid_spec=pltpu.PrefetchScalarGridSpec(
            num_scalar_prefetch=1,
            grid=(2, rows // TILE),
            in_specs=[
                pl.BlockSpec((TILE, group), lambda j, i, _: (i, j)),
                pl.BlockSpec((rows, LANES), lambda j, i, _: (0, j)),
                pl.BlockSpec((rows, LANES), lambda j, i, _: (0, j)),
                pl.BlockSpec((TILE, 1), lambda j, i, _: (i, 0)),
                pl.BlockSpec((1, rows), lambda j, i, _: (0, 0)),
            ],
            out_specs=[
                pl.BlockSpec((TILE, group), lambda j, i, _: (i, j)),
                pl.BlockSpec((TILE, LANES), lambda j, i, _: (i, j)),
            ],
            scratch_shapes=[
                pltpu.VMEM((4, TILE, 1), F32),
                pltpu.VMEM((4, TILE, 1), F32),
                pltpu.VMEM((4, TILE, LANES), F32),
            ],
        ),
        out_shape=[
            jax.ShapeDtypeStruct(query.shape, BF),
            jax.ShapeDtypeStruct((rows, 2 * LANES), F32),
        ],
        name="attention",
        cost_estimate=pl.CostEstimate(
            flops=8 * 4 * rows * rows * LANES,
            bytes_accessed=6 << 20,
            transcendentals=8 * rows * rows,
        ),
    )(first, query, keys, values, doc_col, doc_row)


def backward_body(
    first_ref, q_ref, k_ref, v_ref, do_ref, o_ref, lse_ref, doc_col, doc_row, cos_ref, sin_ref,
    cos_all, sin_all, dq_ref, dk_ref, dv_ref, dq_s, dk_s, dv_s,
):
    i = pl.program_id(1)

    @pl.when(i == 0)
    def _():
        dk_s[...] = jnp.zeros_like(dk_s)
        dv_s[...] = jnp.zeros_like(dv_s)

    dq_s[...] = jnp.zeros_like(dq_s)
    queries, grads, deltas = [], [], []
    for h in range(4):
        at = slice((h // 2) * LANES, (h // 2 + 1) * LANES)
        half = half_lanes(TILE, h % 2)
        pair, grad = q_ref[:, at], do_ref[:, at]
        queries.append(jnp.where(half, pair, jnp.zeros_like(pair)))
        grads.append(jnp.where(half, grad, jnp.zeros_like(grad)))
        product = grads[h].astype(F32) * o_ref[:, at].astype(F32)
        deltas.append(jnp.sum(product, axis=1, keepdims=True))

    def step(t, carry):
        allowed = allowed_pairs(i, t, doc_col, doc_row)
        start = pl.multiple_of(t * TILE, TILE)
        at = pl.ds(start, TILE)
        keys, vals = k_ref[at, :], v_ref[at, :]
        dk, dv = dk_s[at, :], dv_s[at, :]
        for h in range(4):
            logits = jnp.where(allowed, SCORE_MULT * reverse_product(queries[h], keys), MASKED)
            probs = jnp.exp(logits - lse_ref[:, h : h + 1])
            d_probs = reverse_product(grads[h], vals)
            d_logits = (probs * (d_probs - deltas[h])).astype(BF)
            dq_s[h] = dq_s[h] + low_dot(d_logits, keys)
            dk = dk + gradient_product(d_logits, queries[h])
            dv = dv + gradient_product(probs.astype(BF), grads[h])
        dk_s[at, :] = dk
        dv_s[at, :] = dv
        return carry

    lax.fori_loop(first_ref[i], i + 1, step, 0)
    for p in range(2):
        both = jnp.where(half_lanes(TILE, 0), dq_s[2 * p], dq_s[2 * p + 1])
        both = (SCORE_MULT * both).astype(BF).astype(F32)
        dq_ref[:, p * LANES : (p + 1) * LANES] = turn(both, cos_ref[...], -sin_ref[...]).astype(BF)

    @pl.when(i == pl.num_programs(1) - 1)
    def _():
        def finish(t, carry):
            at = pl.ds(pl.multiple_of(t * TILE, TILE), TILE)
            dk, dv = dk_s[at, :], dv_s[at, :]
            dk = (SCORE_MULT * (dk + pltpu.roll(dk, HEAD_WIDTH, 1))).astype(BF).astype(F32)
            dk_ref[at, :] = turn(dk, cos_all[at, :], -sin_all[at, :]).astype(BF)
            dv_ref[at, :] = (dv + pltpu.roll(dv, HEAD_WIDTH, 1)).astype(BF)
            return carry

        lax.fori_loop(0, pl.num_programs(1), finish, 0)


def attention_back_call(
    first, query, keys, values, d_out, out, lse, doc_col, doc_row, cos_tab, sin_tab
):
    rows = query.shape[0]
    group = query.shape[1] // 2
    whole = pl.BlockSpec((rows, LANES), lambda j, i, _: (0, j))
    tile = pl.BlockSpec((TILE, group), lambda j, i, _: (i, j))
    table = pl.BlockSpec((TILE, LANES), lambda j, i, _: (i, 0))
    table_all = pl.BlockSpec((rows, LANES), lambda j, i, _: (0, 0))
    return pl.pallas_call(
        backward_body,
        grid_spec=pltpu.PrefetchScalarGridSpec(
            num_scalar_prefetch=1,
            grid=(2, rows // TILE),
            in_specs=[
                tile,
                whole,
                whole,
                tile,
                tile,
                pl.BlockSpec((TILE, LANES), lambda j, i, _: (i, j)),
                pl.BlockSpec((TILE, 1), lambda j, i, _: (i, 0)),
                pl.BlockSpec((1, rows), lambda j, i, _: (0, 0)),
                table,
                table,
                table_all,
                table_all,
            ],
            out_specs=[tile, whole, whole],
            scratch_shapes=[
                pltpu.VMEM((4, TILE, LANES), F32),
                pltpu.VMEM((rows, LANES), F32),
                pltpu.VMEM((rows, LANES), F32),
            ],
        ),
        out_shape=[
            jax.ShapeDtypeStruct(query.shape, BF),
            jax.ShapeDtypeStruct((rows, 2 * LANES), BF),
            jax.ShapeDtypeStruct((rows, 2 * LANES), BF),
        ],
        name="attention_back",
        cost_estimate=pl.CostEstimate(
            flops=8 * 10 * rows * rows * LANES,
            bytes_accessed=10 << 20,
            transcendentals=8 * rows * rows,
        ),
    )(first, query, keys, values, d_out, out, lse, doc_col, doc_row, cos_tab, sin_tab, cos_tab, sin_tab)


def fast_attention(x, weights, la_q, la_k, la_v, exit_q, exit_k, exit_v, document_line):
    rows = x.shape[0]
    half = HEAD_WIDTH // 2
    cos_tab, sin_tab = rope_tables(jnp.arange(rows, dtype=jnp.int32), HEAD_WIDTH)
    cos_tab = jnp.tile(cos_tab.reshape(rows, half), (1, 4))
    sin_tab = sin_tab.reshape(rows, half)
    sin_tab = jnp.tile(jnp.concatenate([-sin_tab, sin_tab], axis=1), (1, 2))
    first_docs = document_line[::TILE]
    first = jnp.sum((document_line[None, :] < first_docs[:, None]).astype(jnp.int32), axis=1)
    first = first // TILE
    doc_col, doc_row = document_line[:, None], document_line[None, :]
    query, keys, values = qkv_call(
        x, weights, la_q, la_k, la_v, exit_q, jnp.stack([exit_k, exit_v]), cos_tab, sin_tab
    )
    attended, lse = attention_call(first, query, keys, values, doc_col, doc_row)

    def backward(d_heads):
        d_query, d_keys, d_values = attention_back_call(
            first, query, keys, values, d_heads, attended, lse, doc_col, doc_row, cos_tab, sin_tab
        )
        lane = jnp.arange(LANES, dtype=jnp.int32)[None, :] < HEAD_WIDTH
        d_key = jnp.where(lane, d_keys[:, :LANES], d_keys[:, LANES:])
        d_value = jnp.where(lane, d_values[:, :LANES], d_values[:, LANES:])
        return d_query, d_key, d_value

    return attended, backward


def attention_forward(query_heads, key_heads, value_heads, document_line):
    token_length = query_heads.shape[0]
    kv_dev = key_heads.shape[1] // HEAD_WIDTH
    per_kv = query_heads.shape[1] // key_heads.shape[1]
    block_rows = min(512, token_length)
    query_four = query_heads.reshape(token_length, kv_dev, per_kv, HEAD_WIDTH)
    key_three = key_heads.reshape(token_length, kv_dev, HEAD_WIDTH)
    value_three = value_heads.reshape(token_length, kv_dev, HEAD_WIDTH)
    key_pos = jnp.arange(token_length, dtype=jnp.int32)

    def scores_of(first_row):
        query_rows = lax.dynamic_slice_in_dim(query_four, first_row, block_rows, 0)
        row_docs = lax.dynamic_slice_in_dim(document_line, first_row, block_rows, 0)
        row_pos = first_row + jnp.arange(block_rows, dtype=jnp.int32)
        allowed = (row_docs[:, None] == document_line[None, :]) & (
            key_pos[None, :] <= row_pos[:, None]
        )
        raw_scores = jnp.einsum(
            "qkgd,skd->kgqs", query_rows, key_three, preferred_element_type=F32
        )
        return (jnp.where(allowed[None, None], SCORE_MULT * raw_scores, MASKED), query_rows)

    def forward_block(running_totals, block_index):
        logits, query_rows = scores_of(block_index * block_rows)
        row_max = jnp.max(logits, axis=-1, keepdims=True)
        shifted = jnp.exp(logits - row_max)
        row_sum = jnp.sum(shifted, axis=-1, keepdims=True)
        probs_low = (shifted / row_sum).astype(BF)
        mixed_rows = jnp.einsum(
            "kgqs,skd->qkgd", probs_low, value_three, preferred_element_type=F32
        )
        log_total = row_max[..., 0] + jnp.log(row_sum[..., 0])
        return (running_totals, (mixed_rows.reshape(block_rows, -1).astype(BF), log_total))

    block_ids = jnp.arange(token_length // block_rows, dtype=jnp.int32)
    _, (attn_blocks, log_totals) = lax.scan(forward_block, 0, block_ids)

    def backward(d_heads):
        d_heads_four = d_heads.reshape(token_length, kv_dev, per_kv, HEAD_WIDTH)

        def backward_block(running_totals, block_items):
            d_key_sum, d_value_sum = running_totals
            block_index, log_total = block_items
            first_row = block_index * block_rows
            logits, query_rows = scores_of(first_row)
            probs = jnp.exp(logits - log_total[..., None])
            d_rows = lax.dynamic_slice_in_dim(d_heads_four, first_row, block_rows, 0)
            d_probs = jnp.einsum(
                "qkgd,skd->kgqs", d_rows, value_three, preferred_element_type=F32
            )
            inner = jnp.sum(probs * d_probs, axis=-1, keepdims=True)
            d_logits = (probs * (d_probs - inner)).astype(BF)
            d_query_rows = SCORE_MULT * jnp.einsum(
                "kgqs,skd->qkgd", d_logits, key_three, preferred_element_type=F32
            )
            d_key_sum = d_key_sum + SCORE_MULT * jnp.einsum(
                "kgqs,qkgd->skd", d_logits, query_rows, preferred_element_type=F32
            )
            d_value_sum = d_value_sum + jnp.einsum(
                "kgqs,qkgd->skd", probs.astype(BF), d_rows, preferred_element_type=F32
            )
            return (
                (d_key_sum, d_value_sum),
                d_query_rows.astype(BF).reshape(block_rows, -1),
            )

        zero_keys = jnp.zeros((token_length, kv_dev, HEAD_WIDTH), F32)
        (d_key_sum, d_value_sum), d_query_blocks = lax.scan(
            backward_block, (zero_keys, zero_keys), (block_ids, log_totals)
        )
        return (
            d_query_blocks.reshape(token_length, -1),
            d_key_sum.astype(BF).reshape(token_length, -1),
            d_value_sum.astype(BF).reshape(token_length, -1),
        )

    return attn_blocks.reshape(token_length, -1), backward


def rope(values, cos_tab, sin_tab):
    rows, width = values.shape
    heads = values.astype(F32).reshape(rows, width // HEAD_WIDTH, HEAD_WIDTH)
    return rotate(heads, cos_tab, sin_tab).astype(BF).reshape(rows, width)


def plain_attention(x, weights, la_q, la_k, la_v, exit_q, exit_k, exit_v, document_line):
    rows = x.shape[0]
    q_cols, kv_cols = exit_q.shape[1], exit_k.shape[1]
    projected = low_dot(x, weights)
    cos_tab, sin_tab = rope_tables(jnp.arange(rows, dtype=jnp.int32), HEAD_WIDTH)
    query_rot = rope(projected[:, :q_cols] + low_dot(la_q, exit_q), cos_tab, sin_tab)
    key_rot = rope(
        projected[:, q_cols : q_cols + kv_cols] + low_dot(la_k, exit_k), cos_tab, sin_tab
    )
    value_low = (projected[:, q_cols + kv_cols :] + low_dot(la_v, exit_v)).astype(BF)
    attended, attention_back = attention_forward(query_rot, key_rot, value_low, document_line)

    def backward(d_heads):
        d_query, d_key, d_value = attention_back(d_heads)
        return rope(d_query, cos_tab, -sin_tab), rope(d_key, cos_tab, -sin_tab), d_value

    return attended, backward


def layer(mover, args):
    (
        tokens,
        token_document,
        document_adapter,
        attention_norm_gain,
        feedforward_norm_gain,
        query_weight,
        key_weight,
        value_weight,
        output_weight,
        gate_weight,
        up_weight,
        down_weight,
        attention_down_maps,
        query_exit_maps,
        key_value_exit_maps,
        output_entry_maps,
        output_exit_maps,
        feedforward_entry_maps,
        feedforward_exit_maps,
        down_entry_maps,
        down_exit_maps,
        cotangent,
    ) = args
    seq_size, wsh_size, s = mover.seq_size, mover.wsh_size, mover.s
    own_rows = tokens.shape[1]
    width = tokens.shape[2]
    adapters = attention_down_maps.shape[1]
    rank = query_exit_maps.shape[1]
    flat = adapters * rank
    doc_count = document_adapter.shape[1]
    q_cols = query_weight.shape[1] // seq_size
    kv_cols = key_weight.shape[1] // seq_size
    feature = width // seq_size
    row_block = width // wsh_size
    hidden = gate_weight.shape[1]
    hid_block = hidden // (wsh_size * seq_size)
    hid_own = hidden // seq_size

    def owners(docs):
        hot = (docs[:, None] == jnp.arange(doc_count, dtype=jnp.int32)[None, :]).astype(jnp.int32)
        return jnp.sum(hot * document_adapter[0][None, :], axis=1)

    def turned(maps):
        return maps.transpose(1, 2, 0).reshape(-1, maps.shape[0])

    def own_hidden(values, lower=0, upper=hid_own):
        parts, at = [], lower
        while at < upper:
            w = at // hid_block
            stop = min(upper, (w + 1) * hid_block)
            start = (w * seq_size + s) * hid_block + at - w * hid_block
            parts.append(cut(values, start, stop - at, 1))
            at = stop
        return parts

    qkv_local = jnp.concatenate(
        [
            cut(query_weight, s * q_cols, q_cols, 1),
            cut(key_weight, s * kv_cols, kv_cols, 1),
            cut(value_weight, s * kv_cols, kv_cols, 1),
        ],
        axis=1,
    )
    qkv_full = mover.gather_rows(qkv_local)
    local_docs = token_document[0]
    own_owner = owners(local_docs)
    hidden_state = tokens[0].astype(F32)
    first_normed, scale_one = normed(hidden_state, attention_norm_gain)
    first_normed = first_normed.astype(BF)
    input_maps = turned(attention_down_maps)
    picked_first = reverse_product(first_normed, input_maps)
    picked_first = picked_first * adapter_mask(own_owner, 3 * rank, adapters)
    picked_first = fold(picked_first, 3 * rank, 0).astype(BF)
    first_all = mover.gather_tokens(
        jnp.concatenate([mover.to_slots(first_normed, row_block), picked_first], axis=1)
    )
    document_line = mover.gather_tokens(local_docs[None, :].T)[:, 0]
    owner = owners(document_line)
    mask_rank = adapter_mask(owner, rank, adapters)
    output_gradient = cotangent[0].astype(F32)
    d_mlp_local = (RESIDUAL_MULT * output_gradient).astype(BF)
    d_mlp = mover.gather_tokens(d_mlp_local)

    half_width = width // 2
    down_local = cut(down_weight, s * hid_block, hid_block, 0)
    chunk = hid_own // 4
    chunk_bounds = [(0, chunk), (chunk, 2 * chunk), (2 * chunk, 3 * chunk)]
    chunk_bounds += [(3 * chunk, 7 * chunk // 2), (7 * chunk // 2, 4 * chunk)]

    def gate_up(lower, upper):
        return jnp.concatenate(
            own_hidden(gate_weight, lower, upper) + own_hidden(up_weight, lower, upper), axis=1
        )

    out_piece = mover.head_rows(output_weight)
    down_low = mover.gather_rows(down_local[:, :half_width])
    if mover.fast:
        out_full = mover.head_rows_done(mover.gather_rows(out_piece), output_weight.shape[0])
    else:
        out_full = out_piece
    down_high = mover.gather_rows(down_local[:, half_width:])
    chunk_weights = [mover.gather_rows(gate_up(*bounds)) for bounds in chunk_bounds]

    query_exit = cut(query_exit_maps.reshape(flat, -1), s * q_cols, q_cols, 1)
    key_exit = cut(key_value_exit_maps[0].reshape(flat, -1), s * kv_cols, kv_cols, 1)
    value_exit = cut(key_value_exit_maps[1].reshape(flat, -1), s * kv_cols, kv_cols, 1)
    first_slots = first_all[:, :width]
    la_one = first_all[:, width:]
    la_q = spread(la_one, owner, rank, 0, adapters)
    la_k = spread(la_one, owner, rank, rank, adapters)
    la_v = spread(la_one, owner, rank, 2 * rank, adapters)
    token_length = first_all.shape[0]
    attend = fast_attention if mover.fast else plain_attention
    attended, attention_back = attend(
        first_slots, qkv_full, la_q, la_k, la_v, query_exit, key_exit, value_exit, document_line
    )

    out_entry = cut(turned(output_entry_maps), s * q_cols, q_cols, 1)
    out_exit = output_exit_maps.reshape(flat, -1)
    la_out_part = fold(reverse_product(attended, out_entry) * mask_rank, rank, 0)
    attn_sum = mover.scatter_tokens(low_dot(attended, out_full), la_out_part)
    la_out_own = attn_sum[1].astype(BF)
    attention_path = attn_sum[0] + low_dot(
        spread(la_out_own, own_owner, rank, 0, adapters), out_exit
    )
    middle = hidden_state + RESIDUAL_MULT * attention_path

    second_normed, scale_two = normed(middle, feedforward_norm_gain)
    second_normed = second_normed.astype(BF)
    entry_maps = turned(feedforward_entry_maps)
    picked_second = reverse_product(second_normed, entry_maps) * adapter_mask(
        own_owner, 2 * rank, adapters
    )
    picked_second = fold(picked_second, 2 * rank, rank) + la_out_own.astype(F32)
    second_all = mover.gather_tokens(
        jnp.concatenate(
            [mover.to_slots(second_normed, row_block), picked_second.astype(BF)], axis=1
        )
    )
    second_slots = second_all[:, :width]
    la_out = spread(second_all[:, width:], owner, rank, 0, adapters)
    la_gate = spread(second_all[:, width:], owner, rank, rank, adapters)
    la_up = spread(second_all[:, width:], owner, rank, 2 * rank, adapters)

    down_exit = down_exit_maps.reshape(flat, -1)
    d_la_d = (reverse_product(d_mlp, down_exit) * mask_rank).astype(BF)
    d_mixed_slots = reverse_product(d_mlp[:, :half_width], down_low) + reverse_product(
        d_mlp[:, half_width:], down_high
    )
    down_entry = jnp.concatenate(own_hidden(turned(down_entry_maps)), axis=1)
    all_exits = feedforward_exit_maps.reshape(2, flat, -1)
    exits = [jnp.concatenate(own_hidden(all_exits[i]), axis=1) for i in range(2)]
    d_second = jnp.zeros((token_length, width), F32)
    d_la_gate = jnp.zeros((token_length, flat), F32)
    d_la_up = jnp.zeros((token_length, flat), F32)
    mixed_parts, gate_grads, up_grads, entry_grads = [], [], [], []
    for (lower, upper), weights in zip(chunk_bounds, chunk_weights):
        size = upper - lower
        both = low_dot(second_slots, weights)
        gate = both[:, :size] + low_dot(la_gate, exits[0][:, lower:upper])
        up = both[:, size:] + low_dot(la_up, exits[1][:, lower:upper])
        d_parts = []
        at = lower
        while at < upper:
            owner_w = at // hid_block
            stop = min(upper, (owner_w + 1) * hid_block)
            start = mover.slot_of(owner_w) * hid_block + (at - owner_w * hid_block)
            d_parts.append(cut(d_mixed_slots, start, stop - at, 1))
            at = stop
        d_mixed = jnp.concatenate(d_parts, axis=1) + low_dot(d_la_d, down_entry[:, lower:upper])
        sigma = jax.nn.sigmoid(gate)
        swish = gate * sigma
        mixed = (swish * up).astype(BF)
        d_gate = (d_mixed * up * sigma * (1.0 + gate * (1.0 - sigma))).astype(BF)
        d_up = (d_mixed * swish).astype(BF)
        d_second = d_second + reverse_product(jnp.concatenate([d_gate, d_up], axis=1), weights)
        d_la_gate = d_la_gate + reverse_product(d_gate, exits[0][:, lower:upper])
        d_la_up = d_la_up + reverse_product(d_up, exits[1][:, lower:upper])
        mixed_parts.append(mixed)
        gate_grads.append(gradient_product(la_gate, d_gate))
        up_grads.append(gradient_product(la_up, d_up))
        entry_grads.append(gradient_product(d_la_d, mixed))
    d_la_two_part = fold(d_la_gate * mask_rank, rank, 0) + fold(d_la_up * mask_rank, rank, rank)
    d_second_sum = mover.scatter_tokens(d_second, d_la_two_part)
    d_la_two_own = d_second_sum[1].astype(BF)
    d_second_own = mover.from_slots(d_second_sum[0], row_block) + low_dot(
        spread(d_la_two_own, own_owner, 2 * rank, 0, adapters), entry_maps
    )
    grad_middle = output_gradient + normed_back(
        middle, scale_two, feedforward_norm_gain, d_second_own
    )
    d_attn_own = (RESIDUAL_MULT * grad_middle).astype(BF)
    d_attn_all = mover.gather_tokens(jnp.concatenate([d_attn_own, d_la_two_own], axis=1))
    d_attn = d_attn_all[:, :width]
    gate_grad = jnp.concatenate(gate_grads, axis=1)
    up_grad = jnp.concatenate(up_grads, axis=1)
    down_in_grad = jnp.concatenate(entry_grads, axis=1)
    hidden_grads = mover.sum_hidden([gate_grad, up_grad, down_in_grad], hid_block)

    mixed_slots = mover.to_slots(jnp.concatenate(mixed_parts, axis=1), hid_block)
    mixed_all = jnp.concatenate(mixed_parts, axis=1)
    la_down_part = fold(reverse_product(mixed_all, down_entry) * mask_rank, rank, 0)
    mlp_sum = mover.scatter_tokens(
        jnp.concatenate([low_dot(mixed_slots, down_low), low_dot(mixed_slots, down_high)], axis=1),
        la_down_part,
    )
    la_down_own = mlp_sum[1].astype(BF)
    feedforward_path = mlp_sum[0] + low_dot(
        spread(la_down_own, own_owner, rank, 0, adapters), down_exit
    )
    layer_out = (middle + RESIDUAL_MULT * feedforward_path).astype(BF)[None]
    la_down = spread(mover.gather_tokens(la_down_own), owner, rank, 0, adapters)

    def own_features(slots):
        per = wsh_size // seq_size
        parts = [
            cut(slots, mover.slot_of(s * per + i) * row_block, row_block, 1) for i in range(per)
        ]
        return jnp.concatenate(parts, axis=1)

    d_la_two = spread(d_attn_all[:, width:], owner, 2 * rank, 0, adapters)
    entry_grad = gradient_product(d_la_two, own_features(second_slots))
    down_out_grad = gradient_product(la_down, cut(d_mlp, s * feature, feature, 1))
    d_la_o = (reverse_product(d_attn, out_exit) * mask_rank).astype(BF)
    out_in_grad = gradient_product(d_la_o, attended)
    out_out_grad = gradient_product(la_out, cut(d_attn, s * feature, feature, 1))
    feature_grads = mover.sum_features([entry_grad, down_out_grad, out_in_grad, out_out_grad])

    d_attended = (reverse_product(d_attn, out_full) + low_dot(d_la_o, out_entry)).astype(BF)
    d_query, d_key, d_value = attention_back(d_attended)
    d_la_one_part = (
        fold(reverse_product(d_query, query_exit) * mask_rank, rank, 0)
        + fold(reverse_product(d_key, key_exit) * mask_rank, rank, rank)
        + fold(reverse_product(d_value, value_exit) * mask_rank, rank, 2 * rank)
    )
    d_la_one = mover.sum_small(d_la_one_part.astype(BF)).astype(BF)
    d_first_part = reverse_product(jnp.concatenate([d_query, d_key, d_value], axis=1), qkv_full)
    (d_first_sum,) = mover.scatter_tokens(d_first_part)
    d_la_one_own = cut(d_la_one, s * own_rows, own_rows, 0)
    d_first = mover.from_slots(d_first_sum, row_block) + low_dot(
        spread(d_la_one_own, own_owner, 3 * rank, 0, adapters), input_maps
    )
    hidden_gradient = grad_middle + normed_back(
        hidden_state, scale_one, attention_norm_gain, d_first
    )
    attention_in_grad = gradient_product(
        spread(d_la_one, owner, 3 * rank, 0, adapters), own_features(first_slots)
    )
    query_out_grad = gradient_product(la_q, d_query)
    key_out_grad = gradient_product(la_k, d_key)
    value_out_grad = gradient_product(la_v, d_value)
    last_grads = mover.sum_features(
        [attention_in_grad, query_out_grad], key_out_grad, value_out_grad
    )

    def back(values, shape):
        return values.reshape(shape[1], shape[2], shape[0]).transpose(2, 0, 1)

    return (
        layer_out,
        hidden_gradient[None],
        back(last_grads[0], attention_down_maps.shape),
        last_grads[1].reshape(query_exit_maps.shape),
        last_grads[2].reshape(key_value_exit_maps.shape),
        back(feature_grads[2], output_entry_maps.shape),
        feature_grads[3].reshape(output_exit_maps.shape),
        back(feature_grads[0], feedforward_entry_maps.shape),
        hidden_grads[0].reshape(feedforward_exit_maps.shape),
        back(hidden_grads[1], down_entry_maps.shape),
        feature_grads[1].reshape(down_exit_maps.shape),
    )


def solution(mesh):
    seq_size, wsh_size = mesh.shape["seq"], mesh.shape["wsh"]

    def on_device(*args):
        return layer(Mover(seq_size, wsh_size), args)

    rows = P("wsh", None)
    stream = P("wsh", "seq", None)
    in_specs = (stream, P("wsh", "seq"), rows, P(), P()) + (rows,) * 7 + (P(),) * 9 + (stream,)
    out_specs = (stream, stream) + (P(),) * 9
    return jax.shard_map(
        on_device, mesh=mesh, in_specs=in_specs, out_specs=out_specs, check_vma=False
    )
```

time: 2960 us -> 1260 us (0.43)
  waiting for transfers between devices: 2440 us -> 411 us
  starting transfers between devices: 29.7 us -> 188 us
  Pallas kernels: 0 us -> 140 us
  local copies, waits for them, and re-layouts: 83.3 us -> 177 us
  matrix products: 308 us -> 234 us
  other arithmetic: 53.1 us -> 86.2 us
    all_gather x7 -> x0, waiting for transfers between devices: 2070 us -> none  [the longest x1 628 us: on_device(): lax.all_gather(up_weight, 'wsh', axis=0, tiled=True)]
    ppermute x0 -> x121, waiting for transfers between devices: none -> 411 us  [the longest x104 411 us: send(): result = lax.ppermute(values, axis, pairs)]
    psum x1 -> x0, waiting for transfers between devices: 336 us -> none  [on_device(): summed = lax.psum(attn_terms + mlp_terms, ('seq', 'wsh'))]
    ppermute x0 -> x121, starting transfers between devices: none -> 188 us  [the longest x104 186 us: send(): result = lax.ppermute(values, axis, pairs)]
    pallas_call x0 -> x12, Pallas kernels: none -> 140 us  [the longest x9 68.9 us: final_call(): pl.pallas_call(body, grid_spec=pltpu.PrefetchScalarGridSpec(num_scalar_pr...]
    dot_general x32 -> x42, matrix products: 206 us -> 126 us  [low_dot(): return jnp.dot(left, right, preferred_element_type=F32)]
    unnamed x177 -> x440, local copies, waits for them, and re-layouts: 28.9 us -> 105 us
    all_to_all x8 -> x0, waiting for transfers between devices: 33.4 us -> none  [the longest x1 12.3 us: on_device(): lax.all_to_all(d_query_heads, 'seq', split_axis=0, concat_axis=1, tiled=T...]
  transfers between devices with their start and end apart: 16 -> 121, of which waited for: 14 -> 48; matrix products, arithmetic and copies ran while one was open for 7% -> 25% of each run, Pallas kernels for 0% -> 11%
where the time goes in v1:
time: 1260 us; the launch traced here: 1240 us
  waiting for transfers between devices  411 us (33%)
  matrix products  234 us (19%)
  starting transfers between devices  188 us (15%)
  local copies, waits for them, and re-layouts  177 us (14%)
  Pallas kernels  140 us (11%)
  other arithmetic  86.2 us (7%)
    ppermute x104, waiting for transfers between devices, send(): result = lax.ppermute(values, axis, pairs)  411 us
    ppermute x104, starting transfers between devices, send(): result = lax.ppermute(values, axis, pairs)  186 us
    dot_general x42, matrix products, low_dot(): return jnp.dot(left, right, preferred_element_type=F32)  126 us
    unnamed x440, local copies, waits for them, and re-layouts  105 us
    dot_general x19, matrix products, reverse_product(): lax.dot_general(left, right, (((1,), (1,)), ((), ())), preferred_element_...  83.6 us
    pallas_call x9, Pallas kernels, final_call(): pl.pallas_call(body, grid_spec=pltpu.PrefetchScalarGridSpec(num_scalar_pr...  68.9 us
    pallas_call x1, Pallas kernels, attention_call(): pl.pallas_call(forward_body, grid_spec=pltpu.PrefetchScalarGridSpec(num_s...  34 us
    pallas_call x1, Pallas kernels, attention_back_call(): pl.pallas_call(backward_body, grid_spec=pltpu.PrefetchScalarGridSpec(num_...  27.7 us
  transfers between devices with their start and end apart: 121, of which 48 were waited for; matrix products, arithmetic and copies ran while one was open for 25% of the time, Pallas kernels for 11%

profile of v1, /device:TPU:0, one launch (start us, length us, event | category | flops | bytes accessed | tf_op | source)
XLA Modules:
  0.0 1238.8 jit_solution(2913113373264374035)
XLA Ops:
  92.3 10.8 collective-permute-done.17
  103.1 10.7 collective-permute-start.20
  147.8 11.3 collective-permute-done.33
  172.7 18.1 %collective-permute-done.37 = bf16[256,1024]{1,0:T(8,128)(2,1)S(1)} collective-permute-done((bf16[256,1024]{1,0:T(8,128)(2,1)S(1)}, bf16[256,1024]{1,0:T(8,128)(2,1)S(1)}, u32[]{:S(2)}, u32[]{:S(2)}) %collective-permute-start.37) | collective-permute-done | bytes 524320 | tf_op jit(solution)/shard_map/ppermute | solution.py:119
  192.8 22.5 %collective-permute-done.32 = bf16[256,1024]{1,0:T(8,128)(2,1)} collective-permute-done((bf16[256,1024]{1,0:T(8,128)(2,1)S(1)}, bf16[256,1024]{1,0:T(8,128)(2,1)}, u32[]{:S(2)}, u32[]{:S(2)}) %collective-permute-start.32) | collective-permute-done | bytes 524320 | tf_op jit(solution)/shard_map/ppermute | solution.py:119
  241.9 9.1 collective-permute-start.57
  258.1 18.9 %collective-permute-done.55 = bf16[256,1024]{1,0:T(8,128)(2,1)S(1)} collective-permute-done((bf16[256,1024]{1,0:T(8,128)(2,1)S(1)}, bf16[256,1024]{1,0:T(8,128)(2,1)S(1)}, u32[]{:S(2)}, u32[]{:S(2)}) %collective-permute-start.55) | collective-permute-done | bytes 524320 | tf_op jit(solution)/shard_map/ppermute | solution.py:119
  277.5 32.1 %collective-permute-done.57 = bf16[256,1024]{1,0:T(8,128)(2,1)S(1)} collective-permute-done((bf16[256,1024]{1,0:T(8,128)(2,1)S(1)}, bf16[256,1024]{1,0:T(8,128)(2,1)S(1)}, u32[]{:S(2)}, u32[]{:S(2)}) %collective-permute-start.57) | collective-permute-done | bytes 524320 | tf_op jit(solution)/shard_map/ppermute | solution.py:119
  312.0 12.4 %collective-permute-done.44 = bf16[256,1024]{1,0:T(8,128)(2,1)S(1)} collective-permute-done((bf16[256,1024]{1,0:T(8,128)(2,1)S(1)}, bf16[256,1024]{1,0:T(8,128)(2,1)S(1)}, u32[]{:S(2)}, u32[]{:S(2)}) %collective-permute-start.44) | collective-permute-done | bytes 524320 | tf_op jit(solution)/shard_map/ppermute | solution.py:119
  324.4 10.2 collective-permute-done.48
  335.1 14.3 %collective-permute-done.50 = bf16[256,1024]{1,0:T(8,128)(2,1)} collective-permute-done((bf16[256,1024]{1,0:T(8,128)(2,1)S(1)}, bf16[256,1024]{1,0:T(8,128)(2,1)}, u32[]{:S(2)}, u32[]{:S(2)}) %collective-permute-start.50) | collective-permute-done | bytes 524320 | tf_op jit(solution)/shard_map/ppermute | solution.py:119
  422.6 34.0 %attention.1 = (bf16[1024,512]{1,0:T(8,128)(2,1)}, f32[1024,256]{1,0:T(8,128)}) custom-call(s32[4]{0:T(128)} %and_select_fusion.4.first_ref, bf16[1024,512]{1,0:T(8,128)(2,1)} %get-tuple-element.109.q_ref, bf16[1024,256]{1,0:T(8,128)(2,1)} %get-tuple-element.110.k_ref, bf16[1024,256]{1,0:T(8,128)(2,1)} %get-tuple-element.111.v_ref, s32[1024,1]{1,0:T(8,128)} %copy.75.doc_col, ...), custom_call_target="tpu_custom_call" | custom-call | flops 4294967296 | bytes 6291456 | tf_op jit(solution)/shard_map/attention/pallas_call | solution.py:475
  467.8 9.8 collective-permute-start.42
  521.4 10.4 collective-permute-done.58
  531.8 11.2 collective-permute-done.54
  598.8 12.0 collective-permute-done.27
  767.9 16.4 %add_add_fusion = f32[1024,2048]{1,0:T(8,128)} fusion(f32[1024,2048]{1,0:T(8,128)} %fusion.124, f32[1024,2048]{1,0:T(8,128)} %fusion.58, f32[1024,2048]{1,0:T(8,128)} %fusion.50, f32[1024,2048]{1,0:T(8,128)} %fusion.54, bf16[2048,512]{1,0:T(8,128)(2,1)} %constant_dynamic-update-slice_fusion.73, bf16[1024,256]{0,1:T(8,128)(2,1)S(1)} %get-tuple-element.238, ...), kind=kOutput, calls=%fused_computation.1 | convolution fusion | flops 2157969408 | bytes 45088768 | tf_op jit(solution)/shard_map/dot_general | solution.py:44
  801.4 9.2 copy.80
  895.7 15.2 %collective-permute-done.79 = bf16[256,2176]{1,0:T(8,128)(2,1)S(1)} collective-permute-done((bf16[256,2176]{1,0:T(8,128)(2,1)S(1)}, bf16[256,2176]{1,0:T(8,128)(2,1)S(1)}, u32[]{:S(2)}, u32[]{:S(2)}) %collective-permute-start.79) | collective-permute-done | bytes 1114144 | tf_op jit(solution)/shard_map/ppermute | solution.py:119
  913.4 53.9 %collective-permute-done.80 = bf16[256,2176]{1,0:T(8,128)(2,1)} collective-permute-done((bf16[256,2176]{1,0:T(8,128)(2,1)}, bf16[256,2176]{1,0:T(8,128)(2,1)}, u32[]{:S(2)}, u32[]{:S(2)}) %collective-permute-start.80) | collective-permute-done | bytes 1114144 | tf_op jit(solution)/shard_map/ppermute | solution.py:119
  991.7 27.7 %attention_back.1 = (bf16[1024,512]{1,0:T(8,128)(2,1)}, bf16[1024,256]{1,0:T(8,128)(2,1)}, bf16[1024,256]{1,0:T(8,128)(2,1)}) custom-call(s32[4]{0:T(128)} %and_select_fusion.4.first_ref, bf16[1024,512]{1,0:T(8,128)(2,1)} %get-tuple-element.109.q_ref, bf16[1024,256]{1,0:T(8,128)(2,1)} %get-tuple-element.110.k_ref, ...), custom_call_target="tpu_custom_call" | custom-call | flops 10737418240 | bytes 10485760 | tf_op jit(solution)/shard_map/attention_back/pallas_call | solution.py:578
  1135.9 12.9 %collective-permute-done.115.c = bf16[640,512]{1,0:T(8,128)(2,1)} collective-permute-done((bf16[640,512]{1,0:T(8,128)(2,1)S(1)}, bf16[640,512]{1,0:T(8,128)(2,1)}, u32[]{:S(2)}, u32[]{:S(2)}) %collective-permute-start.115) | collective-permute-done | bytes 655392 | tf_op jit(solution)/shard_map/ppermute | solution.py:119
  1152.8 14.5 %finish.16 = f32[1,128,8192]{2,1,0:T(8,128)} custom-call(s32[1]{0:T(128)} %bitcast.134.s_ref, bf16[1536,512]{1,0:T(8,128)(2,1)} %pad_maximum_fusion.12.a, bf16[1536,512]{1,0:T(8,128)(2,1)} %collective-permute-done.119.b, bf16[1536,512]{1,0:T(8,128)(2,1)} %collective-permute-done.91.c, bf16[1536,512]{1,0:T(8,128)(2,1)} %collective-permute-done.120.d), custom_call_target="tpu_custom_call" | custom-call | tf_op jit(solution)/shard_map/finish/pallas_call | solution.py:304
  1167.4 28.5 %finish.15 = f32[2,128,8192]{2,1,0:T(8,128)} custom-call(s32[1]{0:T(128)} %bitcast.134.s_ref, bf16[1536,512]{1,0:T(8,128)(2,1)} %pad_maximum_fusion.12.a, bf16[1536,512]{1,0:T(8,128)(2,1)} %collective-permute-done.119.b, bf16[1536,512]{1,0:T(8,128)(2,1)} %collective-permute-done.91.c, bf16[1536,512]{1,0:T(8,128)(2,1)} %collective-permute-done.120.d), custom_call_target="tpu_custom_call" | custom-call | tf_op jit(solution)/shard_map/finish/pallas_call | solution.py:304
  (925 shorter events, 809.0 us)
Async XLA Ops:
  3.6 83.6 %collective-permute-start.7 = (bf16[256,768]{1,0:T(8,128)(2,1)}, bf16[256,768]{1,0:T(8,128)(2,1)}, u32[]{:S(2)}, u32[]{:S(2)}) collective-permute-start(bf16[256,768]{1,0:T(8,128)(2,1)} %get-tuple-element.335), channel_id=1, source_target_pairs={{0,4},{1,5},{2,6},{3,7},{4,0},{5,1},{6,2},{7,3},{8,12},{9,13},{10,... | collective-permute-start | bytes 1179656 | tf_op jit(solution)/shard_map/ppermute | solution.py:119
  7.7 107.2 %collective-permute-start.4 = (bf16[256,768]{1,0:T(8,128)(2,1)}, bf16[256,768]{1,0:T(8,128)(2,1)}, u32[]{:S(2)}, u32[]{:S(2)}) collective-permute-start(bf16[256,768]{1,0:T(8,128)(2,1)} %get-tuple-element.335), channel_id=1, source_target_pairs={{0,1},{1,0},{2,3},{3,2},{4,5},{5,4},{6,7},{7,6},{8,9},{9,8},{10,11... | collective-permute-start | bytes 1179656 | tf_op jit(solution)/shard_map/ppermute | solution.py:119
  11.2 67.5 %collective-permute-start.11 = (bf16[64,2048]{1,0:T(8,128)(2,1)}, bf16[64,2048]{1,0:T(8,128)(2,1)}, u32[]{:S(2)}, u32[]{:S(2)}) collective-permute-start(bf16[64,2048]{1,0:T(8,128)(2,1)} %get-tuple-element.312), channel_id=1, source_target_pairs={{0,2},{1,3},{10,12},{11,13},{20,22},{21,23},{30,24},{31,25}} | collective-permute-start | bytes 786440 | tf_op jit(solution)/shard_map/ppermute | solution.py:119
  15.5 63.3 %collective-permute-start.12 = (bf16[64,2048]{1,0:T(8,128)(2,1)}, bf16[64,2048]{1,0:T(8,128)(2,1)}, u32[]{:S(2)}, u32[]{:S(2)}) collective-permute-start(bf16[64,2048]{1,0:T(8,128)(2,1)} %get-tuple-element.314), channel_id=1, source_target_pairs={{0,4},{1,5},{10,14},{11,15},{20,16},{21,17},{30,26},{31,27}} | collective-permute-start | bytes 786440 | tf_op jit(solution)/shard_map/ppermute | solution.py:119
  17.5 59.2 %collective-permute-start = (s32[256,1]{0,1:T(1,128)}, s32[256,1]{0,1:T(1,128)}, u32[]{:S(2)}, u32[]{:S(2)}) collective-permute-start(s32[256,1]{0,1:T(1,128)} %bitcast.1), channel_id=1, source_target_pairs={{0,16},{8,24},{16,0},{24,8},{1,17},{9,25},{17,1},{25,9},{2,18},{10... | collective-permute-start | bytes 3080 | tf_op jit(solution)/shard_map/ppermute | solution.py:119
  232.0 78.2 %collective-permute-start.59 = (bf16[256,1024]{1,0:T(8,128)(2,1)S(1)}, bf16[256,1024]{1,0:T(8,128)(2,1)S(1)}, u32[]{:S(2)}, u32[]{:S(2)}) collective-permute-start(bf16[256,1024]{1,0:T(8,128)(2,1)S(1)} %copy-done.66), channel_id=1, source_target_pairs={{0,6},{1,7},{2,0},{3,1},{4,2},{5,3},{6,4},{7,5},{8,14},{9,15},{10,... | collective-permute-start | bytes 1572872 | tf_op jit(solution)/shard_map/ppermute | solution.py:119
  241.9 67.7 %collective-permute-start.57 = (bf16[256,1024]{1,0:T(8,128)(2,1)S(1)}, bf16[256,1024]{1,0:T(8,128)(2,1)S(1)}, u32[]{:S(2)}, u32[]{:S(2)}) collective-permute-start(bf16[256,1024]{1,0:T(8,128)(2,1)S(1)} %copy-done.66), channel_id=1, source_target_pairs={{0,4},{1,5},{2,6},{3,7},{4,0},{5,1},{6,2},{7,3},{8,12},{9,13},{10,... | collective-permute-start | bytes 1572872 | tf_op jit(solution)/shard_map/ppermute | solution.py:119
  276.9 80.6 %collective-permute-start.41 = (bf16[256,1024]{1,0:T(8,128)(2,1)S(1)}, bf16[256,1024]{1,0:T(8,128)(2,1)S(1)}, u32[]{:S(2)}, u32[]{:S(2)}) collective-permute-start(bf16[256,1024]{1,0:T(8,128)(2,1)S(1)} %collective-permute-done.38), channel_id=1, source_target_pairs={{0,1},{1,0},{2,3},{3,2},{4,5},{5,4},{6,7},{7,6},{8,9},{9,8},{10,11... | collective-permute-start | bytes 1572872 | tf_op jit(solution)/shard_map/ppermute | solution.py:119
  335.0 70.3 %collective-permute-start.3 = (bf16[2,256,2176]{2,1,0:T(8,128)(2,1)S(1)}, bf16[2,256,2176]{2,1,0:T(8,128)(2,1)S(1)}, u32[]{:S(2)}, u32[]{:S(2)}) collective-permute-start(bf16[2,256,2176]{2,1,0:T(8,128)(2,1)S(1)} %pad_maximum_fusion.5), channel_id=1, source_target_pairs={{0,8},{8,0},{16,24},{24,16},{1,9},{9,1},{17,25},{25,17},{2,10},{10... | collective-permute-start | bytes 6684680 | tf_op jit(solution)/shard_map/ppermute | solution.py:196
  349.4 118.4 %collective-permute-start.69 = (bf16[256,512]{1,0:T(8,128)(2,1)}, bf16[256,512]{1,0:T(8,128)(2,1)}, u32[]{:S(2)}, u32[]{:S(2)}) collective-permute-start(bf16[256,512]{1,0:T(8,128)(2,1)} %get-tuple-element.168), channel_id=1, source_target_pairs={{0,2},{1,3},{2,4},{3,5},{4,6},{5,7},{6,0},{7,1},{8,10},{9,11},{10,... | collective-permute-start | bytes 786440 | tf_op jit(solution)/shard_map/ppermute | solution.py:119
  371.8 105.7 %collective-permute-start.71 = (bf16[256,512]{1,0:T(8,128)(2,1)}, bf16[256,512]{1,0:T(8,128)(2,1)}, u32[]{:S(2)}, u32[]{:S(2)}) collective-permute-start(bf16[256,512]{1,0:T(8,128)(2,1)} %get-tuple-element.168), channel_id=1, source_target_pairs={{0,4},{1,5},{2,6},{3,7},{4,0},{5,1},{6,2},{7,3},{8,12},{9,13},{10,... | collective-permute-start | bytes 786440 | tf_op jit(solution)/shard_map/ppermute | solution.py:119
  391.4 88.2 %collective-permute-start.51 = (bf16[256,1024]{1,0:T(8,128)(2,1)}, bf16[256,1024]{1,0:T(8,128)(2,1)}, u32[]{:S(2)}, u32[]{:S(2)}) collective-permute-start(bf16[256,1024]{1,0:T(8,128)(2,1)} %collective-permute-done.50), channel_id=1, source_target_pairs={{0,1},{1,0},{2,3},{3,2},{4,5},{5,4},{6,7},{7,6},{8,9},{9,8},{10,11... | collective-permute-start | bytes 1572872 | tf_op jit(solution)/shard_map/ppermute | solution.py:119
  393.6 88.9 %collective-permute-start.62 = (bf16[256,512]{1,0:T(8,128)(2,1)}, bf16[256,512]{1,0:T(8,128)(2,1)}, u32[]{:S(2)}, u32[]{:S(2)}) collective-permute-start(bf16[256,512]{1,0:T(8,128)(2,1)} %get-tuple-element.161), channel_id=1, source_target_pairs={{0,2},{1,3},{2,4},{3,5},{4,6},{5,7},{6,0},{7,1},{8,10},{9,11},{10,... | collective-permute-start | bytes 786440 | tf_op jit(solution)/shard_map/ppermute | solution.py:119
  405.3 77.2 %collective-permute-start.36 = (bf16[256,1024]{1,0:T(8,128)(2,1)}, bf16[256,1024]{1,0:T(8,128)(2,1)}, u32[]{:S(2)}, u32[]{:S(2)}) collective-permute-start(bf16[256,1024]{1,0:T(8,128)(2,1)} %collective-permute-done.32), channel_id=1, source_target_pairs={{0,1},{1,0},{2,3},{3,2},{4,5},{5,4},{6,7},{7,6},{8,9},{9,8},{10,11... | collective-permute-start | bytes 1572872 | tf_op jit(solution)/shard_map/ppermute | solution.py:119
  479.6 77.8 %collective-permute-start.24 = (bf16[2,256,2176]{2,1,0:T(8,128)(2,1)S(1)}, bf16[2,256,2176]{2,1,0:T(8,128)(2,1)S(1)}, u32[]{:S(2)}, u32[]{:S(2)}) collective-permute-start(bf16[2,256,2176]{2,1,0:T(8,128)(2,1)S(1)} %pad_maximum_fusion.6), channel_id=1, source_target_pairs={{0,8},{8,0},{16,24},{24,16},{1,9},{9,1},{17,25},{25,17},{2,10},{10... | collective-permute-start | bytes 6684680 | tf_op jit(solution)/shard_map/ppermute | solution.py:212
  531.8 64.1 %collective-permute-start.76 = (bf16[2,256,2048]{2,1,0:T(8,128)(2,1)}, bf16[2,256,2048]{2,1,0:T(8,128)(2,1)}, u32[]{:S(2)}, u32[]{:S(2)}) collective-permute-start(bf16[2,256,2048]{2,1,0:T(8,128)(2,1)} %pad_maximum_fusion.11), channel_id=1, source_target_pairs={{0,8},{8,0},{16,24},{24,16},{1,9},{9,1},{17,25},{25,17},{2,10},{10... | collective-permute-start | bytes 6291464 | tf_op jit(solution)/shard_map/ppermute | solution.py:196
  893.9 76.3 %collective-permute-start.91 = (bf16[1536,512]{1,0:T(8,128)(2,1)}, bf16[1536,512]{1,0:T(8,128)(2,1)}, u32[]{:S(2)}, u32[]{:S(2)}) collective-permute-start(bf16[1536,512]{1,0:T(8,128)(2,1)} %pad_maximum_fusion.12.a), channel_id=1, source_target_pairs={{0,16},{8,24},{16,0},{24,8},{1,17},{9,25},{17,1},{25,9},{2,18},{10... | collective-permute-start | bytes 4718600 | tf_op jit(solution)/shard_map/ppermute | solution.py:119
  913.3 64.9 %collective-permute-start.81 = (bf16[2,256,2176]{2,1,0:T(8,128)(2,1)}, bf16[2,256,2176]{2,1,0:T(8,128)(2,1)}, u32[]{:S(2)}, u32[]{:S(2)}) collective-permute-start(bf16[2,256,2176]{2,1,0:T(8,128)(2,1)} %pad_maximum_fusion.10), channel_id=1, source_target_pairs={{0,8},{8,0},{16,24},{24,16},{1,9},{9,1},{17,25},{25,17},{2,10},{10... | collective-permute-start | bytes 6684680 | tf_op jit(solution)/shard_map/ppermute | solution.py:196
  975.8 159.5 %collective-permute-start.119 = (bf16[1536,512]{1,0:T(8,128)(2,1)}, bf16[1536,512]{1,0:T(8,128)(2,1)}, u32[]{:S(2)}, u32[]{:S(2)}) collective-permute-start(bf16[1536,512]{1,0:T(8,128)(2,1)} %pad_maximum_fusion.12.a), channel_id=1, source_target_pairs={{0,8},{8,0},{16,24},{24,16},{1,9},{9,1},{17,25},{25,17},{2,10},{10... | collective-permute-start | bytes 4718600 | tf_op jit(solution)/shard_map/ppermute | solution.py:287
  1134.7 87.0 %collective-permute-start.103 = (bf16[256,2048]{1,0:T(8,128)(2,1)}, bf16[256,2048]{1,0:T(8,128)(2,1)}, u32[]{:S(2)}, u32[]{:S(2)}) collective-permute-start(bf16[256,2048]{1,0:T(8,128)(2,1)} %fusion.62), channel_id=1, source_target_pairs={{0,16},{8,24},{16,0},{24,8},{1,17},{9,25},{17,1},{25,9},{2,18},{10... | collective-permute-start | bytes 3145736 | tf_op jit(solution)/shard_map/ppermute | solution.py:119
  1135.3 60.5 %collective-permute-start.117 = (bf16[640,512]{1,0:T(8,128)(2,1)S(1)}, bf16[640,512]{1,0:T(8,128)(2,1)}, u32[]{:S(2)}, u32[]{:S(2)}) collective-permute-start(bf16[640,512]{1,0:T(8,128)(2,1)S(1)} %pad_maximum_fusion.17.a), channel_id=1, source_target_pairs={{0,8},{8,0},{16,24},{24,16},{1,9},{9,1},{17,25},{25,17},{2,10},{10... | collective-permute-start | bytes 1966088 | tf_op jit(solution)/shard_map/ppermute | solution.py:287
  1135.3 60.5 %collective-permute-start.118 = (bf16[640,512]{1,0:T(8,128)(2,1)S(1)}, bf16[640,512]{1,0:T(8,128)(2,1)}, u32[]{:S(2)}, u32[]{:S(2)}) collective-permute-start(bf16[640,512]{1,0:T(8,128)(2,1)S(1)} %collective-permute-done.102.c), channel_id=1, source_target_pairs={{0,8},{8,0},{16,24},{24,16},{1,9},{9,1},{17,25},{25,17},{2,10},{10... | collective-permute-start | bytes 1966088 | tf_op jit(solution)/shard_map/ppermute | solution.py:289
  1135.9 72.7 %collective-permute-start.114 = (bf16[640,512]{1,0:T(8,128)(2,1)S(1)}, bf16[640,512]{1,0:T(8,128)(2,1)}, u32[]{:S(2)}, u32[]{:S(2)}) collective-permute-start(bf16[640,512]{1,0:T(8,128)(2,1)S(1)} %pad_maximum_fusion.18.a), channel_id=1, source_target_pairs={{0,8},{8,0},{16,24},{24,16},{1,9},{9,1},{17,25},{25,17},{2,10},{10... | collective-permute-start | bytes 1966088 | tf_op jit(solution)/shard_map/ppermute | solution.py:287
  1148.9 59.7 %collective-permute-start.116 = (bf16[640,512]{1,0:T(8,128)(2,1)}, bf16[640,512]{1,0:T(8,128)(2,1)}, u32[]{:S(2)}, u32[]{:S(2)}) collective-permute-start(bf16[640,512]{1,0:T(8,128)(2,1)} %collective-permute-done.115.c), channel_id=1, source_target_pairs={{0,8},{8,0},{16,24},{24,16},{1,9},{9,1},{17,25},{25,17},{2,10},{10... | collective-permute-start | bytes 1966088 | tf_op jit(solution)/shard_map/ppermute | solution.py:289
  (264 other events, 4141.0 us)

commit v2 on v1

--- a/solution.py
+++ b/solution.py
@@ -1,5 +1,3 @@
-import functools
-
 import jax
 import jax.numpy as jnp
 from jax import lax
@@ -26,6 +24,8 @@
 CORE_SWAP = [(s, s ^ 1) for s in range(4)]
 Y_SWAP = [(s, s ^ 2) for s in range(4)]
 X_SWAP = [(w, w ^ 1) for w in range(8)]
+NEAR_SWAP = [(w, w ^ 2) for w in range(8)]
+FAR_SWAP = [(w, w ^ 4) for w in range(8)]
 
 
 def z_shift(steps):
@@ -100,6 +100,13 @@
 def pack(values):
     parts = [values[:, i : i + PACK] for i in range(0, values.shape[1], PACK)]
     return jnp.concatenate(parts, axis=0)
+
+
+def after(values, *deps):
+    deps = [d for d in deps if d is not None]
+    if not deps:
+        return values
+    return lax.optimization_barrier((values, tuple(deps)))[0]
 
 
 class Mover:
@@ -109,37 +116,41 @@
         self.s, self.w = lax.axis_index("seq"), lax.axis_index("wsh")
         self.y, self.c = self.s // 2, self.s % 2
         self.z, self.x = self.w // 2, self.w % 2
-        self.lanes = {"x": [], "y": [], "z": []}
-        self.depth = 6
-
-    def send(self, values, axis, pairs, lane, depth=2):
-        sent = self.lanes[lane]
-        if len(sent) >= depth:
-            values, _ = lax.optimization_barrier((values, sent[-depth]))
-        result = lax.ppermute(values, axis, pairs)
-        sent.append(result)
-        return result
-
-    def gather_rows(self, chunk):
+        self.marks = {}
+
+    def far(self, chunk, *deps):
+        chunk = after(chunk, *deps)
         if not self.fast:
-            return lax.all_gather(chunk, "wsh", axis=0, tiled=True)
-        slots = []
-        for r in range(4):
-            held = chunk
-            if r:
-                held = self.send(chunk, "wsh", z_shift(r), "z", self.depth)
-            slots += [held, self.send(held, "wsh", X_SWAP, "x", self.depth)]
-        return jnp.concatenate(slots, axis=0)
+            return chunk
+        return jnp.concatenate([chunk, lax.ppermute(chunk, "wsh", FAR_SWAP)], axis=0)
+
+    def near(self, pair, *deps):
+        pair = after(pair, *deps)
+        if not self.fast:
+            return pair
+        return jnp.concatenate([pair, lax.ppermute(pair, "wsh", NEAR_SWAP)], axis=0)
+
+    def across(self, four, *deps):
+        four = after(four, *deps)
+        if not self.fast:
+            return (lax.all_gather(four, "wsh", axis=0, tiled=True),)
+        return four, lax.ppermute(four, "wsh", X_SWAP)
+
+    def swap_bits(self, d):
+        return d // 2 + 2 * (d % 2)
 
     def slot_owner(self, k):
         if not self.fast:
             return k
-        return 2 * ((self.z - k // 2) % 4) + (self.x ^ (k % 2))
+        return 2 * (self.z ^ self.swap_bits(k % 4)) + (self.x ^ (k // 4))
 
     def slot_of(self, w):
         if not self.fast:
             return w
-        return 2 * ((self.z - w // 2) % 4) + (self.x ^ (w % 2))
+        return self.z_slot(w // 2) + 4 * (self.x ^ (w % 2))
+
+    def z_slot(self, z):
+        return self.swap_bits(self.z ^ z)
 
     def to_slots(self, values, block):
         if not self.fast:
@@ -164,33 +175,42 @@
                 0,
             )
         piece = rows // 4
-        mine = jnp.where(self.z == self.s, cut(weight, self.z * piece, piece, 0), 0)
-        for r in range(1, 4):
-            pairs = [
-                (8 * s + 2 * s + x, 8 * s + 2 * ((s + r) % 4) + x)
+
+        def part(z):
+            return cut(weight, z * piece, piece, 0)
+
+        def pairs(senders, step):
+            return [
+                (8 * s + 2 * (s ^ sender) + x, 8 * s + 2 * (s ^ sender ^ step) + x)
                 for s in range(4)
+                for sender in senders
                 for x in range(2)
             ]
-            out = cut(weight, ((self.z + r) % 4) * piece, piece, 0)
-            mine = mine + self.send(out, ("seq", "wsh"), pairs, "z", self.depth)
-        return mine
-
-    def head_rows_done(self, slots, rows):
-        if not self.fast:
-            return slots
+
+        z, axes = self.z, ("seq", "wsh")
+        away = jnp.concatenate([part(z ^ 2), part(z ^ 3)], axis=0)
+        got = lax.ppermute(away, axes, pairs((0,), 2))
+        first = z == self.s
+        mine = jnp.where(first, part(z), got[:piece])
+        away = jnp.where(first, part(z ^ 1), got[piece:])
+        got = lax.ppermute(away, axes, pairs((0, 2), 1))
+        return jnp.where(first | (z == (self.s ^ 2)), mine, got)
+
+    def head_rows_done(self, halves, rows):
         piece = rows // 4
-        blocks = slots.reshape(4, 2, piece, slots.shape[1])
         out = []
         for shard in range(2):
-            for j in range(4):
-                one = pick(blocks, (self.z - j) % 4, 0)
-                out.append(pick(one, self.x ^ shard, 0))
+            half = jnp.where(self.x == shard, halves[0], halves[1])
+            blocks = half.reshape(4, piece, half.shape[1])
+            out += [pick(blocks, self.z_slot(j), 0) for j in range(4)]
         return jnp.concatenate(out, axis=0)
 
     def gather_tokens(self, values):
         if not self.fast:
             return lax.all_gather(values, "seq", axis=0, tiled=True)
-        other = self.send(values, "seq", Y_SWAP, "y")
+        return self.gather_rest(values, lax.ppermute(values, "seq", Y_SWAP))
+
+    def gather_rest(self, values, other):
         first = self.y == 0
         column = jnp.stack([jnp.where(first, values, other), jnp.where(first, other, values)])
         partner = lax.ppermute(column, "seq", CORE_SWAP)
@@ -200,7 +220,7 @@
         )
         return whole.reshape((4 * values.shape[0],) + values.shape[1:])
 
-    def scatter_tokens(self, *partials):
+    def scatter_tokens(self, *partials, deps=(), late=(), mark=None):
         if not self.fast:
             return [
                 lax.psum_scatter(v.astype(BF), "seq", scatter_dimension=0, tiled=True).astype(F32)
@@ -212,7 +232,9 @@
         got = lax.ppermute(out, "seq", CORE_SWAP).astype(F32)
         mine = jnp.concatenate([pick(v, self.c, 1) for v in blocks], axis=2)
         away = (pick(mine, 1 - self.y, 0) + pick(got, 1 - self.y, 0)).astype(BF)
-        other = self.send(away, "seq", Y_SWAP, "y").astype(F32)
+        other = lax.ppermute(after(away, *deps), "seq", Y_SWAP)
+        self.marks[mark] = other
+        other = after(other, *late).astype(F32)
         total = pick(mine, self.y, 0) + pick(got, self.y, 0) + other
         found, at = [], 0
         for v in partials:
@@ -224,14 +246,14 @@
         if not self.fast:
             return lax.psum(partial, "seq")
         total = partial.astype(F32) + lax.ppermute(partial, "seq", CORE_SWAP).astype(F32)
-        other = self.send(total.astype(BF), "seq", Y_SWAP, "y")
+        other = lax.ppermute(total.astype(BF), "seq", Y_SWAP)
         return total + other.astype(F32)
 
     def sum_plain(self, grad):
         total = lax.psum(grad.astype(BF), "wsh")
         return lax.all_gather(total.astype(BF), "seq", axis=0).astype(F32)
 
-    def sum_hidden(self, grads, hid_block):
+    def sum_hidden(self, grads, hid_block, deps=(), mark=None, early=()):
         if not self.fast:
             found = []
             for grad in grads:
@@ -239,14 +261,14 @@
                 wide = self.sum_plain(grad).reshape(self.seq_size, rows, self.wsh_size, hid_block)
                 found.append(wide.transpose(1, 2, 0, 3).reshape(rows, -1))
             return [jnp.stack(found[:2]), found[2]]
-        parts = self.sum_gather(jnp.concatenate([pack(v) for v in grads], axis=0))
+        parts = self.sum_gather(jnp.concatenate([pack(v) for v in grads], axis=0), deps, (), mark, early)
         s = self.s.astype(jnp.int32)[None]
         return [
             final_hidden(parts, s, 0, 2),
             final_hidden(parts, s, 8 * LANES, 1)[0],
         ]
 
-    def sum_features(self, grads, key=None, value=None):
+    def sum_features(self, grads, key=None, value=None, late=()):
         if not self.fast:
             grads = grads + ([key, value] if key is not None else [])
             found = []
@@ -257,7 +279,7 @@
         if key is not None:
             rest = jnp.zeros((key.shape[0], PACK - 2 * LANES), F32)
             packed.append(jnp.concatenate([key, value, rest], axis=1))
-        parts = self.sum_gather(jnp.concatenate(packed, axis=0))
+        parts = self.sum_gather(jnp.concatenate(packed, axis=0), (), late)
         s = self.s.astype(jnp.int32)[None]
         found, at = [], 0
         for grad in grads:
@@ -267,42 +289,53 @@
             found.append(final_kv(parts, s, at))
         return found
 
-    def sum_gather(self, packed):
+    def sum_gather(self, packed, deps=(), late=(), mark=None, early=()):
         rows = packed.shape[0]
         halves = packed.reshape(2, rows // 2, PACK)
-        got = self.send(pick(halves, 1 - self.x, 0).astype(BF), "wsh", X_SWAP, "x")
+        got = lax.ppermute(pick(halves, 1 - self.x, 0).astype(BF), "wsh", X_SWAP)
         half = pick(halves, self.x, 0) + got.astype(F32)
         blocks = half.reshape(4, rows // 8, PACK)
         total = pick(blocks, self.z, 0)
         for r in range(1, 4):
             out = pick(blocks, (self.z + r) % 4, 0).astype(BF)
-            total = total + self.send(out, "wsh", z_shift(r), "z", 3).astype(F32)
+            total = total + lax.ppermute(out, "wsh", z_shift(r)).astype(F32)
         own = total.astype(BF)
-        got = [own] + [self.send(own, "wsh", z_shift(r), "z", 3) for r in range(1, 4)]
+        got = [own] + [lax.ppermute(own, "wsh", z_shift(r)) for r in range(1, 4)]
         ring = jnp.stack(got)
         half = jnp.concatenate([pick(ring, (self.z - j) % 4, 0) for j in range(4)], axis=0)
-        other = self.send(half, "wsh", X_SWAP, "x")
+        half = after(half, *early)
+        other = lax.ppermute(half, "wsh", X_SWAP)
         first = self.x == 0
         part = jnp.concatenate([jnp.where(first, half, other), jnp.where(first, other, half)])
         core = lax.ppermute(part, "seq", CORE_SWAP)
-        other = self.send(part, "seq", Y_SWAP, "y")
+        if mark is None:
+            other = lax.ppermute(after(part, *deps), "seq", Y_SWAP)
+        else:
+            top = lax.ppermute(after(part[: rows // 2], *deps), "seq", Y_SWAP)
+            rest = lax.ppermute(after(part[rows // 2 :], top), "seq", Y_SWAP)
+            self.marks[mark] = (top, rest)
+            other = jnp.concatenate([top, rest], axis=0)
+        other = after(other, *late)
         return part, core, other, lax.ppermute(other, "seq", CORE_SWAP)
 
 
-def choose_part(s_ref, parts, out_ref, axis):
-    k = s_ref[0] ^ pl.program_id(axis)
-    low = jnp.where(k % 2 == 0, parts[0][...], parts[1][...])
-    high = jnp.where(k % 2 == 0, parts[2][...], parts[3][...])
-    value = jnp.where(k < 2, low, high).astype(F32)
-    out_ref[...] = value.reshape(out_ref.shape)
+def final_body(s_ref, own, core, other, last, out_ref):
+    columns = own.shape[-1]
+    for k in range(4):
+        place = s_ref[0] ^ k
+        low = jnp.where(place % 2 == 0, own[...], core[...])
+        high = jnp.where(place % 2 == 0, other[...], last[...])
+        value = jnp.where(place < 2, low, high).astype(F32)
+        at = slice(k * columns, (k + 1) * columns)
+        if len(out_ref.shape) == 3:
+            out_ref[0, :, at] = value
+        else:
+            out_ref[:, at] = value
 
 
 def final_call(parts, s, grid, part_block, part_map, out_shape, out_block, out_map):
-    def body(s_ref, a, b, c, d, out_ref):
-        choose_part(s_ref, (a, b, c, d), out_ref, len(grid) - 1)
-
     return pl.pallas_call(
-        body,
+        final_body,
         grid_spec=pltpu.PrefetchScalarGridSpec(
             num_scalar_prefetch=1,
             grid=grid,
@@ -319,12 +352,12 @@
     return final_call(
         parts,
         s,
-        (rows // LANES, 4),
+        (rows // LANES,),
         (LANES, PACK),
-        lambda i, j, _: (at + i, 0),
+        lambda i, _: (at + i, 0),
         (rows, 4 * PACK),
-        (LANES, PACK),
-        lambda i, j, _: (i, j),
+        (LANES, 4 * PACK),
+        lambda i, _: (i, 0),
     )
 
 
@@ -333,12 +366,12 @@
     return final_call(
         parts,
         s,
-        (count, 8, 4),
+        (count, 8),
         (LANES, TILE),
-        lambda n, w, j, _: (at + 4 * n + w // 2, w % 2),
+        lambda n, w, _: (at + 4 * n + w // 2, w % 2),
         (count, LANES, 32 * TILE),
-        (1, LANES, TILE),
-        lambda n, w, j, _: (n, 0, 4 * w + j),
+        (1, LANES, 4 * TILE),
+        lambda n, w, _: (n, 0, w),
     )
 
 
@@ -347,12 +380,12 @@
     return final_call(
         parts,
         s,
-        (2, 4),
+        (2,),
         (LANES, LANES),
-        lambda n, j, _: (at, n),
+        lambda n, _: (at, n),
         (2, LANES, 4 * LANES),
-        (1, LANES, LANES),
-        lambda n, j, _: (n, 0, j),
+        (1, LANES, 4 * LANES),
+        lambda n, _: (n, 0, 0),
     )
 
 
@@ -377,9 +410,10 @@
     return jnp.where(first, values, other) if half == 0 else jnp.where(first, other, values)
 
 
-def qkv_body(x_ref, w_ref, la_q, la_k, la_v, exit_q, exit_kv, cos_ref, sin_ref, q_ref, k_ref, v_ref):
+def qkv_body(x_ref, w_own, w_other, la_q, la_k, la_v, exit_q, exit_kv, cos_ref, sin_ref, q_ref, k_ref, v_ref):
     cos_tab, sin_tab = cos_ref[...], sin_ref[...]
-    product = low_dot(x_ref[...], w_ref[...])
+    half = w_own.shape[0]
+    product = low_dot(x_ref[:, :half], w_own[...]) + low_dot(x_ref[:, half:], w_other[...])
     q_cols = q_ref.shape[1]
     query = product[:, :q_cols] + low_dot(la_q[...], exit_q[...])
     for i in range(0, q_cols, LANES):
@@ -393,7 +427,7 @@
 
 
 def qkv_call(x, weights, la_q, la_k, la_v, exit_q, exit_kv, cos_tab, sin_tab):
-    rows, width = x.shape[0], weights.shape[0]
+    rows, width = x.shape[0], 2 * weights[0].shape[0]
     q_cols = exit_q.shape[1]
 
     def tile(columns):
@@ -404,7 +438,8 @@
         grid=(rows // TILE,),
         in_specs=[
             tile(width),
-            pl.BlockSpec(weights.shape, lambda i: (0, 0)),
+            pl.BlockSpec(weights[0].shape, lambda i: (0, 0)),
+            pl.BlockSpec(weights[1].shape, lambda i: (0, 0)),
             tile(LANES),
             tile(LANES),
             tile(LANES),
@@ -421,9 +456,9 @@
         ],
         name="qkv",
         cost_estimate=pl.CostEstimate(
-            flops=2 * rows * width * weights.shape[1], bytes_accessed=12 << 20, transcendentals=0
+            flops=2 * rows * width * weights[0].shape[1], bytes_accessed=12 << 20, transcendentals=0
         ),
-    )(x, weights, la_q, la_k, la_v, exit_q, exit_kv, cos_tab, sin_tab)
+    )(x, *weights, la_q, la_k, la_v, exit_q, exit_kv, cos_tab, sin_tab)
 
 
 def allowed_pairs(i, t, doc_col, doc_row):
@@ -434,7 +469,7 @@
 
 
 def forward_body(first_ref, q_ref, k_ref, v_ref, doc_col, doc_row, o_ref, lse_ref, m_s, l_s, acc_s):
-    i = pl.program_id(1)
+    i = pl.program_id(0)
     m_s[...] = jnp.full_like(m_s, MASKED)
     l_s[...] = jnp.zeros_like(l_s)
     acc_s[...] = jnp.zeros_like(acc_s)
@@ -469,24 +504,24 @@
     lse_ref[...] = total
 
 
-def attention_call(first, query, keys, values, doc_col, doc_row):
+def attention_call(j, first, query, keys, values, doc_col, doc_row):
     rows = query.shape[0]
     group = query.shape[1] // 2
     return pl.pallas_call(
         forward_body,
         grid_spec=pltpu.PrefetchScalarGridSpec(
             num_scalar_prefetch=1,
-            grid=(2, rows // TILE),
+            grid=(rows // TILE,),
             in_specs=[
-                pl.BlockSpec((TILE, group), lambda j, i, _: (i, j)),
-                pl.BlockSpec((rows, LANES), lambda j, i, _: (0, j)),
-                pl.BlockSpec((rows, LANES), lambda j, i, _: (0, j)),
-                pl.BlockSpec((TILE, 1), lambda j, i, _: (i, 0)),
-                pl.BlockSpec((1, rows), lambda j, i, _: (0, 0)),
+                pl.BlockSpec((TILE, group), lambda i, _: (i, j)),
+                pl.BlockSpec((rows, LANES), lambda i, _: (0, j)),
+                pl.BlockSpec((rows, LANES), lambda i, _: (0, j)),
+                pl.BlockSpec((TILE, 1), lambda i, _: (i, 0)),
+                pl.BlockSpec((1, rows), lambda i, _: (0, 0)),
             ],
             out_specs=[
-                pl.BlockSpec((TILE, group), lambda j, i, _: (i, j)),
-                pl.BlockSpec((TILE, LANES), lambda j, i, _: (i, j)),
+                pl.BlockSpec((TILE, group), lambda i, _: (i, 0)),
+                pl.BlockSpec((TILE, LANES), lambda i, _: (i, 0)),
             ],
             scratch_shapes=[
                 pltpu.VMEM((4, TILE, 1), F32),
@@ -495,14 +530,14 @@
             ],
         ),
         out_shape=[
-            jax.ShapeDtypeStruct(query.shape, BF),
-            jax.ShapeDtypeStruct((rows, 2 * LANES), F32),
+            jax.ShapeDtypeStruct((rows, group), BF),
+            jax.ShapeDtypeStruct((rows, LANES), F32),
         ],
         name="attention",
         cost_estimate=pl.CostEstimate(
-            flops=8 * 4 * rows * rows * LANES,
-            bytes_accessed=6 << 20,
-            transcendentals=8 * rows * rows,
+            flops=4 * 4 * rows * rows * LANES,
+            bytes_accessed=3 << 20,
+            transcendentals=4 * rows * rows,
         ),
     )(first, query, keys, values, doc_col, doc_row)
 
@@ -511,7 +546,7 @@
     first_ref, q_ref, k_ref, v_ref, do_ref, o_ref, lse_ref, doc_col, doc_row, cos_ref, sin_ref,
     cos_all, sin_all, dq_ref, dk_ref, dv_ref, dq_s, dk_s, dv_s,
 ):
-    i = pl.program_id(1)
+    i = pl.program_id(0)
 
     @pl.when(i == 0)
     def _():
@@ -553,7 +588,7 @@
         both = (SCORE_MULT * both).astype(BF).astype(F32)
         dq_ref[:, p * LANES : (p + 1) * LANES] = turn(both, cos_ref[...], -sin_ref[...]).astype(BF)
 
-    @pl.when(i == pl.num_programs(1) - 1)
+    @pl.when(i == pl.num_programs(0) - 1)
     def _():
         def finish(t, carry):
             at = pl.ds(pl.multiple_of(t * TILE, TILE), TILE)
@@ -563,38 +598,39 @@
             dv_ref[at, :] = (dv + pltpu.roll(dv, HEAD_WIDTH, 1)).astype(BF)
             return carry
 
-        lax.fori_loop(0, pl.num_programs(1), finish, 0)
+        lax.fori_loop(0, pl.num_programs(0), finish, 0)
 
 
 def attention_back_call(
-    first, query, keys, values, d_out, out, lse, doc_col, doc_row, cos_tab, sin_tab
+    j, first, query, keys, values, d_out, out, lse, doc_col, doc_row, cos_tab, sin_tab
 ):
     rows = query.shape[0]
     group = query.shape[1] // 2
-    whole = pl.BlockSpec((rows, LANES), lambda j, i, _: (0, j))
-    tile = pl.BlockSpec((TILE, group), lambda j, i, _: (i, j))
-    table = pl.BlockSpec((TILE, LANES), lambda j, i, _: (i, 0))
-    table_all = pl.BlockSpec((rows, LANES), lambda j, i, _: (0, 0))
+    whole = pl.BlockSpec((rows, LANES), lambda i, _: (0, j))
+    tile = pl.BlockSpec((TILE, group), lambda i, _: (i, j))
+    table = pl.BlockSpec((TILE, LANES), lambda i, _: (i, 0))
+    table_all = pl.BlockSpec((rows, LANES), lambda i, _: (0, 0))
+    own_tile = pl.BlockSpec((TILE, group), lambda i, _: (i, 0))
     return pl.pallas_call(
         backward_body,
         grid_spec=pltpu.PrefetchScalarGridSpec(
             num_scalar_prefetch=1,
-            grid=(2, rows // TILE),
+            grid=(rows // TILE,),
             in_specs=[
                 tile,
                 whole,
                 whole,
                 tile,
-                tile,
-                pl.BlockSpec((TILE, LANES), lambda j, i, _: (i, j)),
-                pl.BlockSpec((TILE, 1), lambda j, i, _: (i, 0)),
-                pl.BlockSpec((1, rows), lambda j, i, _: (0, 0)),
+                own_tile,
+                table,
+                pl.BlockSpec((TILE, 1), lambda i, _: (i, 0)),
+                pl.BlockSpec((1, rows), lambda i, _: (0, 0)),
                 table,
                 table,
                 table_all,
                 table_all,
             ],
-            out_specs=[tile, whole, whole],
+            out_specs=[own_tile, table_all, table_all],
             scratch_shapes=[
                 pltpu.VMEM((4, TILE, LANES), F32),
                 pltpu.VMEM((rows, LANES), F32),
@@ -602,20 +638,22 @@
             ],
         ),
         out_shape=[
-            jax.ShapeDtypeStruct(query.shape, BF),
-            jax.ShapeDtypeStruct((rows, 2 * LANES), BF),
-            jax.ShapeDtypeStruct((rows, 2 * LANES), BF),
+            jax.ShapeDtypeStruct((rows, group), BF),
+            jax.ShapeDtypeStruct((rows, LANES), BF),
+            jax.ShapeDtypeStruct((rows, LANES), BF),
         ],
         name="attention_back",
         cost_estimate=pl.CostEstimate(
-            flops=8 * 10 * rows * rows * LANES,
-            bytes_accessed=10 << 20,
-            transcendentals=8 * rows * rows,
+            flops=4 * 10 * rows * rows * LANES,
+            bytes_accessed=5 << 20,
+            transcendentals=4 * rows * rows,
         ),
     )(first, query, keys, values, d_out, out, lse, doc_col, doc_row, cos_tab, sin_tab, cos_tab, sin_tab)
 
 
-def fast_attention(x, weights, la_q, la_k, la_v, exit_q, exit_k, exit_v, document_line):
+def fast_attention(
+    x, weights, la_q, la_k, la_v, exit_q, exit_k, exit_v, document_line
+):
     rows = x.shape[0]
     half = HEAD_WIDTH // 2
     cos_tab, sin_tab = rope_tables(jnp.arange(rows, dtype=jnp.int32), HEAD_WIDTH)
@@ -629,18 +667,152 @@
     query, keys, values = qkv_call(
         x, weights, la_q, la_k, la_v, exit_q, jnp.stack([exit_k, exit_v]), cos_tab, sin_tab
     )
-    attended, lse = attention_call(first, query, keys, values, doc_col, doc_row)
-
-    def backward(d_heads):
-        d_query, d_keys, d_values = attention_back_call(
-            first, query, keys, values, d_heads, attended, lse, doc_col, doc_row, cos_tab, sin_tab
+    early = attention_call(0, first, query, keys, values, doc_col, doc_row)
+    found = [early]
+
+    def finish(*deps):
+        query_late = after(query, early[0], *deps)
+        found.append(attention_call(1, first, query_late, keys, values, doc_col, doc_row))
+        return jnp.concatenate([early[0], found[1][0]], axis=1)
+
+    def backward(d_heads, between, behind):
+        back = []
+        for j in range(2):
+            if j:
+                d_heads = after(d_heads, back[0][1], *between)
+            args = (first, query, keys, values, d_heads, *found[j], doc_col, doc_row)
+            back.append(attention_back_call(j, *args, cos_tab, sin_tab))
+        back[1] = after(back[1], *behind)
+        lane = jnp.arange(LANES, dtype=jnp.int32)[None, :] < HEAD_WIDTH
+        d_query = jnp.concatenate([back[0][0], back[1][0]], axis=1)
+        d_key = jnp.where(lane, back[0][1], back[1][1])
+        d_value = jnp.where(lane, back[0][2], back[1][2])
+        return d_query, d_key, d_value
+
+    return early[0], finish, backward
+
+
+def units_rows(at_own, own, other):
+    return jnp.where(at_own, own[...], other[...])
+
+
+def mlp_body(owners, add, sc, n2, w_own, w_other, la_gate, la_up, exit_gate, exit_up, d_mlp,
+             low_own, low_other, high_own, high_other, d_la_d, entry, *rest):
+    if add:
+        sum_in, la_in, mixed_ref, gate_ref, up_ref, sum_ref, la_ref = rest
+    else:
+        mixed_ref, gate_ref, up_ref, sum_ref, la_ref = rest
+    half = w_own.shape[0]
+    size = TILE * len(owners)
+    both = low_dot(n2[:, :half], w_own[...]) + low_dot(n2[:, half:], w_other[...])
+    gate = both[:, :size] + low_dot(la_gate[...], exit_gate[...])
+    up = both[:, size:] + low_dot(la_up[...], exit_up[...])
+    parts = []
+    for w in owners:
+        at_own = sc[1] == w % 2
+        parts.append(
+            reverse_product(d_mlp[:, :half], units_rows(at_own, low_own, low_other))
+            + reverse_product(d_mlp[:, half:], units_rows(at_own, high_own, high_other))
         )
-        lane = jnp.arange(LANES, dtype=jnp.int32)[None, :] < HEAD_WIDTH
-        d_key = jnp.where(lane, d_keys[:, :LANES], d_keys[:, LANES:])
-        d_value = jnp.where(lane, d_values[:, :LANES], d_values[:, LANES:])
-        return d_query, d_key, d_value
-
-    return attended, backward
+    d_mixed = jnp.concatenate(parts, axis=1) + low_dot(d_la_d[...], entry[...])
+    sigma = jax.nn.sigmoid(gate)
+    swish = gate * sigma
+    mixed_ref[...] = (swish * up).astype(BF)
+    d_gate = (d_mixed * up * sigma * (1.0 + gate * (1.0 - sigma))).astype(BF)
+    d_up = (d_mixed * swish).astype(BF)
+    gate_ref[...] = d_gate
+    up_ref[...] = d_up
+    d_both = jnp.concatenate([d_gate, d_up], axis=1)
+    sum_own, sum_other = reverse_product(d_both, w_own[...]), reverse_product(d_both, w_other[...])
+    back_gate, back_up = reverse_product(d_gate, exit_gate[...]), reverse_product(d_up, exit_up[...])
+    if add:
+        sum_own, sum_other = sum_own + sum_in[:, :half], sum_other + sum_in[:, half:]
+        back_gate, back_up = back_gate + la_in[:, :LANES], back_up + la_in[:, LANES:]
+    sum_ref[:, :half] = sum_own
+    sum_ref[:, half:] = sum_other
+    la_ref[:, :LANES] = back_gate
+    la_ref[:, LANES:] = back_up
+
+
+def mlp_call(owners, block, x, n2, weights, la_gate, la_up, exit_gate, exit_up, d_mlp, low, high,
+             d_la_d, entry, sums):
+    rows = d_mlp.shape[0]
+    half = weights[0].shape[0]
+    size = TILE * len(owners)
+
+    def tile(columns):
+        return pl.BlockSpec((TILE, columns), lambda t, _: (t, 0))
+
+    def whole(array):
+        return pl.BlockSpec(array.shape, lambda t, _: (0, 0))
+
+    units = pl.BlockSpec((TILE, half), lambda t, sc: (sc[0], 0))
+    args = [n2, *weights, la_gate, la_up, exit_gate, exit_up, d_mlp, *low, *high, d_la_d, entry]
+    in_specs = [tile(2 * half), whole(weights[0]), whole(weights[1]), tile(LANES), tile(LANES)]
+    in_specs += [whole(exit_gate), whole(exit_up), tile(2 * half)] + [units] * 4
+    in_specs += [tile(LANES), whole(entry)]
+    aliases = {}
+    if sums is not None:
+        aliases = {1 + len(args): 3, 2 + len(args): 4}
+        args += sums
+        in_specs += [tile(2 * half), tile(2 * LANES)]
+    return pl.pallas_call(
+        lambda *refs: mlp_body(owners, sums is not None, *refs),
+        grid_spec=pltpu.PrefetchScalarGridSpec(
+            num_scalar_prefetch=1,
+            grid=(rows // TILE,),
+            in_specs=in_specs,
+            out_specs=[tile(size)] * 3 + [tile(2 * half), tile(2 * LANES)],
+        ),
+        out_shape=[jax.ShapeDtypeStruct((rows, size), BF)] * 3
+        + [
+            jax.ShapeDtypeStruct((rows, 2 * half), F32),
+            jax.ShapeDtypeStruct((rows, 2 * LANES), F32),
+        ],
+        input_output_aliases=aliases,
+        name="units",
+        cost_estimate=pl.CostEstimate(
+            flops=20 * rows * half * size, bytes_accessed=32 << 20, transcendentals=rows * size
+        ),
+    )(jnp.stack([block, x]).astype(jnp.int32), *args)
+
+
+def mlp_out_body(chunks, sc, *refs):
+    mixed = refs[: len(chunks)]
+    low_own, low_other, high_own, high_other, out_ref = refs[len(chunks) :]
+    half = low_own.shape[1]
+    low = high = None
+    for (owners, ref) in zip(chunks, mixed):
+        for n, w in enumerate(owners):
+            at = pl.ds(pl.multiple_of(sc[w // 2] * TILE, TILE), TILE)
+            at_own = sc[4] == w % 2
+            part = ref[:, n * TILE : (n + 1) * TILE]
+            more_low = low_dot(part, jnp.where(at_own, low_own[at, :], low_other[at, :]))
+            more_high = low_dot(part, jnp.where(at_own, high_own[at, :], high_other[at, :]))
+            low = more_low if low is None else low + more_low
+            high = more_high if high is None else high + more_high
+    out_ref[:, :half] = low
+    out_ref[:, half:] = high
+
+
+def mlp_out_call(chunks, z_slots, x, mixed, low, high):
+    rows, half = mixed[0].shape[0], low[0].shape[1]
+    places = jnp.stack([*z_slots, x]).astype(jnp.int32)
+    return pl.pallas_call(
+        lambda *refs: mlp_out_body(chunks, *refs),
+        grid_spec=pltpu.PrefetchScalarGridSpec(
+            num_scalar_prefetch=1,
+            grid=(rows // TILE,),
+            in_specs=[pl.BlockSpec((TILE, m.shape[1]), lambda t, _: (t, 0)) for m in mixed]
+            + [pl.BlockSpec(low[0].shape, lambda t, _: (0, 0))] * 4,
+            out_specs=pl.BlockSpec((TILE, 2 * half), lambda t, _: (t, 0)),
+        ),
+        out_shape=jax.ShapeDtypeStruct((rows, 2 * half), F32),
+        name="units_out",
+        cost_estimate=pl.CostEstimate(
+            flops=4 * rows * half * 8 * TILE, bytes_accessed=20 << 20, transcendentals=0
+        ),
+    )(places, *mixed, *low, *high)
 
 
 def attention_forward(query_heads, key_heads, value_heads, document_line):
@@ -728,10 +900,12 @@
     return rotate(heads, cos_tab, sin_tab).astype(BF).reshape(rows, width)
 
 
-def plain_attention(x, weights, la_q, la_k, la_v, exit_q, exit_k, exit_v, document_line):
+def plain_attention(
+    x, weights, la_q, la_k, la_v, exit_q, exit_k, exit_v, document_line, *_
+):
     rows = x.shape[0]
     q_cols, kv_cols = exit_q.shape[1], exit_k.shape[1]
-    projected = low_dot(x, weights)
+    projected = low_dot(x[:, : weights[0].shape[0]], weights[0])
     cos_tab, sin_tab = rope_tables(jnp.arange(rows, dtype=jnp.int32), HEAD_WIDTH)
     query_rot = rope(projected[:, :q_cols] + low_dot(la_q, exit_q), cos_tab, sin_tab)
     key_rot = rope(
@@ -740,11 +914,11 @@
     value_low = (projected[:, q_cols + kv_cols :] + low_dot(la_v, exit_v)).astype(BF)
     attended, attention_back = attention_forward(query_rot, key_rot, value_low, document_line)
 
-    def backward(d_heads):
+    def backward(d_heads, *_):
         d_query, d_key, d_value = attention_back(d_heads)
         return rope(d_query, cos_tab, -sin_tab), rope(d_key, cos_tab, -sin_tab), d_value
 
-    return attended, backward
+    return attended, lambda: attended, backward
 
 
 def layer(mover, args):
@@ -812,7 +986,6 @@
         ],
         axis=1,
     )
-    qkv_full = mover.gather_rows(qkv_local)
     local_docs = token_document[0]
     own_owner = owners(local_docs)
     hidden_state = tokens[0].astype(F32)
@@ -821,50 +994,105 @@
     input_maps = turned(attention_down_maps)
     picked_first = reverse_product(first_normed, input_maps)
     picked_first = picked_first * adapter_mask(own_owner, 3 * rank, adapters)
-    picked_first = fold(picked_first, 3 * rank, 0).astype(BF)
-    first_all = mover.gather_tokens(
-        jnp.concatenate([mover.to_slots(first_normed, row_block), picked_first], axis=1)
-    )
-    document_line = mover.gather_tokens(local_docs[None, :].T)[:, 0]
+    picked_first = fold(picked_first, 3 * rank, 0)
+    last_lane = jnp.arange(LANES, dtype=jnp.int32)[None, :] == LANES - 1
+    picked_first = jnp.where(last_lane, local_docs.astype(F32)[:, None], picked_first).astype(BF)
+
+    half_width = width // 2
+    down_local = cut(down_weight, s * hid_block, hid_block, 0)
+    if mover.fast:
+        chunks = [(0, 1), (2, 3), (4, 5), (6,), (7,)]
+    else:
+        chunks = [tuple(range(wsh_size))]
+    chunk_bounds = [(c[0] * hid_block, (c[-1] + 1) * hid_block) for c in chunks]
+
+    def gate_up_far(i, *deps):
+        gate_late, up_late = after((gate_weight, up_weight), *deps)
+        parts = own_hidden(gate_late, *chunk_bounds[i]) + own_hidden(up_late, *chunk_bounds[i])
+        return mover.far(jnp.concatenate(parts, axis=1))
+
+    output_gradient = cotangent[0].astype(F32)
+    d_mlp_local = (RESIDUAL_MULT * output_gradient).astype(BF)
+    first_cols = jnp.concatenate([mover.to_slots(first_normed, row_block), picked_first], axis=1)
+    qkv_pair = mover.far(qkv_local)
+    if mover.fast:
+        d_mlp_other = lax.ppermute(d_mlp_local, "seq", Y_SWAP)
+        first_other = after(lax.ppermute(first_cols, "seq", Y_SWAP), d_mlp_other)
+        out_piece = mover.head_rows(output_weight)
+        qkv_four = mover.near(qkv_pair)
+        out_pair = mover.far(out_piece, qkv_pair)
+        qkv_full = mover.across(qkv_four)
+        first_all = mover.gather_rest(first_cols, first_other)
+        out_four = mover.near(out_pair, qkv_four)
+        low_pair = mover.far(down_local[:, :half_width], qkv_four)
+        out_swapped = mover.across(out_four, qkv_full[1])
+        out_full = mover.head_rows_done(out_swapped, output_weight.shape[0])
+        d_mlp = mover.gather_rest(d_mlp_local, after(d_mlp_other, first_all))
+        low_four = mover.near(low_pair, out_four)
+        high_pair = mover.far(down_local[:, half_width:], low_pair, qkv_full[1])
+        first_all = after(first_all, d_mlp)
+    else:
+        qkv_full = mover.across(qkv_pair)
+        first_all = mover.gather_tokens(first_cols)
+        d_mlp = mover.gather_tokens(d_mlp_local)
+        out_full = mover.head_rows(output_weight)
+        down_full = mover.across(down_local)[0]
+    document_line = first_all[:, width + LANES - 1].astype(jnp.int32)
     owner = owners(document_line)
     mask_rank = adapter_mask(owner, rank, adapters)
-    output_gradient = cotangent[0].astype(F32)
-    d_mlp_local = (RESIDUAL_MULT * output_gradient).astype(BF)
-    d_mlp = mover.gather_tokens(d_mlp_local)
-
-    half_width = width // 2
-    down_local = cut(down_weight, s * hid_block, hid_block, 0)
-    chunk = hid_own // 4
-    chunk_bounds = [(0, chunk), (chunk, 2 * chunk), (2 * chunk, 3 * chunk)]
-    chunk_bounds += [(3 * chunk, 7 * chunk // 2), (7 * chunk // 2, 4 * chunk)]
-
-    def gate_up(lower, upper):
-        return jnp.concatenate(
-            own_hidden(gate_weight, lower, upper) + own_hidden(up_weight, lower, upper), axis=1
-        )
-
-    out_piece = mover.head_rows(output_weight)
-    down_low = mover.gather_rows(down_local[:, :half_width])
-    if mover.fast:
-        out_full = mover.head_rows_done(mover.gather_rows(out_piece), output_weight.shape[0])
-    else:
-        out_full = out_piece
-    down_high = mover.gather_rows(down_local[:, half_width:])
-    chunk_weights = [mover.gather_rows(gate_up(*bounds)) for bounds in chunk_bounds]
-
+
+    (
+        query_exit_maps,
+        key_value_exit_maps,
+    ) = after((query_exit_maps, key_value_exit_maps), first_normed)
     query_exit = cut(query_exit_maps.reshape(flat, -1), s * q_cols, q_cols, 1)
     key_exit = cut(key_value_exit_maps[0].reshape(flat, -1), s * kv_cols, kv_cols, 1)
     value_exit = cut(key_value_exit_maps[1].reshape(flat, -1), s * kv_cols, kv_cols, 1)
-    first_slots = first_all[:, :width]
     la_one = first_all[:, width:]
     la_q = spread(la_one, owner, rank, 0, adapters)
     la_k = spread(la_one, owner, rank, rank, adapters)
     la_v = spread(la_one, owner, rank, 2 * rank, adapters)
     token_length = first_all.shape[0]
     attend = fast_attention if mover.fast else plain_attention
-    attended, attention_back = attend(
-        first_slots, qkv_full, la_q, la_k, la_v, query_exit, key_exit, value_exit, document_line
-    )
+    early, attend_rest, attention_back = attend(
+        first_all, qkv_full, la_q, la_k, la_v, query_exit, key_exit, value_exit, document_line,
+    )
+
+    (
+        feedforward_entry_maps,
+        feedforward_exit_maps,
+        down_entry_maps,
+        down_exit_maps,
+        output_entry_maps,
+        output_exit_maps,
+    ) = after(
+        (
+            feedforward_entry_maps,
+            feedforward_exit_maps,
+            down_entry_maps,
+            down_exit_maps,
+            output_entry_maps,
+            output_exit_maps,
+        ),
+        early,
+    )
+    if mover.fast:
+        low_rows = low_four.shape[0] // 2
+        low_early = after(low_four[:low_rows], out_swapped[1], early)
+        low_other = [
+            lax.ppermute(low_early, "wsh", X_SWAP),
+            lax.ppermute(low_four[low_rows:], "wsh", X_SWAP),
+        ]
+        down_low = (low_four, jnp.concatenate(low_other, axis=0))
+        high_four = mover.near(high_pair, low_four, early)
+        attended = attend_rest(out_full, high_pair)
+        chunk_pairs = [gate_up_far(0, high_four)]
+        attended = after(attended, high_four, low_other[0])
+        down_high = mover.across(high_four)
+        chunk_fours = [mover.near(chunk_pairs[0], high_four)]
+        chunk_pairs.append(gate_up_far(1, chunk_pairs[0]))
+    else:
+        attended = attend_rest()
 
     out_entry = cut(turned(output_entry_maps), s * q_cols, q_cols, 1)
     out_exit = output_exit_maps.reshape(flat, -1)
@@ -875,6 +1103,8 @@
         spread(la_out_own, own_owner, rank, 0, adapters), out_exit
     )
     middle = hidden_state + RESIDUAL_MULT * attention_path
+    if mover.fast:
+        middle = after(middle, low_other[1], chunk_pairs[0])
 
     second_normed, scale_two = normed(middle, feedforward_norm_gain)
     second_normed = second_normed.astype(BF)
@@ -883,50 +1113,76 @@
         own_owner, 2 * rank, adapters
     )
     picked_second = fold(picked_second, 2 * rank, rank) + la_out_own.astype(F32)
-    second_all = mover.gather_tokens(
-        jnp.concatenate(
-            [mover.to_slots(second_normed, row_block), picked_second.astype(BF)], axis=1
+    second_cols = jnp.concatenate(
+        [mover.to_slots(second_normed, row_block), picked_second.astype(BF)], axis=1
+    )
+    if mover.fast:
+        second_other = lax.ppermute(second_cols, "seq", Y_SWAP)
+        second_all = mover.gather_rest(
+            second_cols, after(second_other, down_high[1], chunk_fours[0], chunk_pairs[1])
         )
-    )
-    second_slots = second_all[:, :width]
+    else:
+        second_all = mover.gather_tokens(second_cols)
     la_out = spread(second_all[:, width:], owner, rank, 0, adapters)
     la_gate = spread(second_all[:, width:], owner, rank, rank, adapters)
     la_up = spread(second_all[:, width:], owner, rank, 2 * rank, adapters)
 
     down_exit = down_exit_maps.reshape(flat, -1)
     d_la_d = (reverse_product(d_mlp, down_exit) * mask_rank).astype(BF)
-    d_mixed_slots = reverse_product(d_mlp[:, :half_width], down_low) + reverse_product(
-        d_mlp[:, half_width:], down_high
-    )
     down_entry = jnp.concatenate(own_hidden(turned(down_entry_maps)), axis=1)
     all_exits = feedforward_exit_maps.reshape(2, flat, -1)
     exits = [jnp.concatenate(own_hidden(all_exits[i]), axis=1) for i in range(2)]
-    d_second = jnp.zeros((token_length, width), F32)
-    d_la_gate = jnp.zeros((token_length, flat), F32)
-    d_la_up = jnp.zeros((token_length, flat), F32)
     mixed_parts, gate_grads, up_grads, entry_grads = [], [], [], []
-    for (lower, upper), weights in zip(chunk_bounds, chunk_weights):
-        size = upper - lower
-        both = low_dot(second_slots, weights)
-        gate = both[:, :size] + low_dot(la_gate, exits[0][:, lower:upper])
-        up = both[:, size:] + low_dot(la_up, exits[1][:, lower:upper])
-        d_parts = []
-        at = lower
-        while at < upper:
-            owner_w = at // hid_block
-            stop = min(upper, (owner_w + 1) * hid_block)
-            start = mover.slot_of(owner_w) * hid_block + (at - owner_w * hid_block)
-            d_parts.append(cut(d_mixed_slots, start, stop - at, 1))
-            at = stop
-        d_mixed = jnp.concatenate(d_parts, axis=1) + low_dot(d_la_d, down_entry[:, lower:upper])
+    if mover.fast:
+        chunk_weights = [mover.across(chunk_fours[0])]
+        sums = None
+        for i, units in enumerate(chunks):
+            if i + 1 < len(chunks):
+                deps = [chunk_fours[i]] + ([] if sums is None else [sums[0]])
+                chunk_fours.append(mover.near(chunk_pairs[i + 1], *deps))
+                chunk_weights.append(mover.across(chunk_fours[i + 1]))
+            if i + 2 < len(chunks):
+                deps = [chunk_pairs[i + 1], down_high[1] if sums is None else sums[0]]
+                chunk_pairs.append(gate_up_far(i + 2, *deps))
+            lower, upper = chunk_bounds[i]
+            units_in = after(second_all, *chunk_fours[i + 1 : i + 2], *chunk_pairs[i + 2 : i + 3])
+            mixed, d_gate, d_up, *sums = mlp_call(
+                units,
+                mover.z_slot(units[0] // 2),
+                mover.x,
+                units_in,
+                chunk_weights[i],
+                la_gate,
+                la_up,
+                exits[0][:, lower:upper],
+                exits[1][:, lower:upper],
+                d_mlp,
+                down_low,
+                down_high,
+                d_la_d,
+                down_entry[:, lower:upper],
+                sums,
+            )
+            mixed_parts.append(mixed)
+            gate_grads.append(gradient_product(la_gate, d_gate))
+            up_grads.append(gradient_product(la_up, d_up))
+            entry_grads.append(gradient_product(d_la_d, mixed))
+        d_second, d_la_both = sums
+        d_la_gate, d_la_up = d_la_both[:, :flat], d_la_both[:, flat:]
+    else:
+        weights = mover.across(gate_up_far(0))[0]
+        both = low_dot(second_all[:, :width], weights)
+        gate = both[:, :hid_own] + low_dot(la_gate, exits[0])
+        up = both[:, hid_own:] + low_dot(la_up, exits[1])
+        d_mixed = reverse_product(d_mlp, down_full) + low_dot(d_la_d, down_entry)
         sigma = jax.nn.sigmoid(gate)
         swish = gate * sigma
         mixed = (swish * up).astype(BF)
         d_gate = (d_mixed * up * sigma * (1.0 + gate * (1.0 - sigma))).astype(BF)
         d_up = (d_mixed * swish).astype(BF)
-        d_second = d_second + reverse_product(jnp.concatenate([d_gate, d_up], axis=1), weights)
-        d_la_gate = d_la_gate + reverse_product(d_gate, exits[0][:, lower:upper])
-        d_la_up = d_la_up + reverse_product(d_up, exits[1][:, lower:upper])
+        d_second = reverse_product(jnp.concatenate([d_gate, d_up], axis=1), weights)
+        d_la_gate = reverse_product(d_gate, exits[0])
+        d_la_up = reverse_product(d_up, exits[1])
         mixed_parts.append(mixed)
         gate_grads.append(gradient_product(la_gate, d_gate))
         up_grads.append(gradient_product(la_up, d_up))
@@ -946,15 +1202,20 @@
     gate_grad = jnp.concatenate(gate_grads, axis=1)
     up_grad = jnp.concatenate(up_grads, axis=1)
     down_in_grad = jnp.concatenate(entry_grads, axis=1)
-    hidden_grads = mover.sum_hidden([gate_grad, up_grad, down_in_grad], hid_block)
-
-    mixed_slots = mover.to_slots(jnp.concatenate(mixed_parts, axis=1), hid_block)
+
     mixed_all = jnp.concatenate(mixed_parts, axis=1)
     la_down_part = fold(reverse_product(mixed_all, down_entry) * mask_rank, rank, 0)
-    mlp_sum = mover.scatter_tokens(
-        jnp.concatenate([low_dot(mixed_slots, down_low), low_dot(mixed_slots, down_high)], axis=1),
-        la_down_part,
-    )
+    if mover.fast:
+        mlp_part = mlp_out_call(
+            chunks, [mover.z_slot(i) for i in range(4)], mover.x, mixed_parts, down_low, down_high
+        )
+    else:
+        mlp_part = low_dot(mixed_all, down_full)
+    mlp_sum = mover.scatter_tokens(mlp_part, la_down_part, deps=(d_attn_all,), mark="mlp")
+    hidden_grads = mover.sum_hidden(
+        [gate_grad, up_grad, down_in_grad], hid_block, (mover.marks.get("mlp"),), "hidden", (d_attn_all,)
+    )
+    hidden_sent = mover.marks.get("hidden", (None, None))
     la_down_own = mlp_sum[1].astype(BF)
     feedforward_path = mlp_sum[0] + low_dot(
         spread(la_down_own, own_owner, rank, 0, adapters), down_exit
@@ -970,23 +1231,32 @@
         return jnp.concatenate(parts, axis=1)
 
     d_la_two = spread(d_attn_all[:, width:], owner, 2 * rank, 0, adapters)
-    entry_grad = gradient_product(d_la_two, own_features(second_slots))
+    entry_grad = gradient_product(d_la_two, own_features(second_all))
     down_out_grad = gradient_product(la_down, cut(d_mlp, s * feature, feature, 1))
     d_la_o = (reverse_product(d_attn, out_exit) * mask_rank).astype(BF)
     out_in_grad = gradient_product(d_la_o, attended)
     out_out_grad = gradient_product(la_out, cut(d_attn, s * feature, feature, 1))
-    feature_grads = mover.sum_features([entry_grad, down_out_grad, out_in_grad, out_out_grad])
 
     d_attended = (reverse_product(d_attn, out_full) + low_dot(d_la_o, out_entry)).astype(BF)
-    d_query, d_key, d_value = attention_back(d_attended)
+    d_query, d_key, d_value = attention_back(
+        d_attended, (mover.marks.get("mlp"),), hidden_sent[:1]
+    )
     d_la_one_part = (
         fold(reverse_product(d_query, query_exit) * mask_rank, rank, 0)
         + fold(reverse_product(d_key, key_exit) * mask_rank, rank, rank)
         + fold(reverse_product(d_value, value_exit) * mask_rank, rank, 2 * rank)
     )
     d_la_one = mover.sum_small(d_la_one_part.astype(BF)).astype(BF)
-    d_first_part = reverse_product(jnp.concatenate([d_query, d_key, d_value], axis=1), qkv_full)
-    (d_first_sum,) = mover.scatter_tokens(d_first_part)
+    d_qkv = jnp.concatenate([d_query, d_key, d_value], axis=1)
+    d_qkv = after(d_qkv, d_la_one_part)
+    d_first_sum = jnp.concatenate(
+        mover.scatter_tokens(
+            *[reverse_product(d_qkv, half) for half in qkv_full],
+            deps=(d_la_one, hidden_sent[1]),
+            late=hidden_grads,
+        ),
+        axis=1,
+    )
     d_la_one_own = cut(d_la_one, s * own_rows, own_rows, 0)
     d_first = mover.from_slots(d_first_sum, row_block) + low_dot(
         spread(d_la_one_own, own_owner, 3 * rank, 0, adapters), input_maps
@@ -995,13 +1265,16 @@
         hidden_state, scale_one, attention_norm_gain, d_first
     )
     attention_in_grad = gradient_product(
-        spread(d_la_one, owner, 3 * rank, 0, adapters), own_features(first_slots)
+        spread(d_la_one, owner, 3 * rank, 0, adapters), own_features(first_all)
     )
     query_out_grad = gradient_product(la_q, d_query)
     key_out_grad = gradient_product(la_k, d_key)
     value_out_grad = gradient_product(la_v, d_value)
     last_grads = mover.sum_features(
-        [attention_in_grad, query_out_grad], key_out_grad, value_out_grad
+        [attention_in_grad, query_out_grad, down_out_grad, entry_grad, out_in_grad, out_out_grad],
+        key_out_grad,
+        value_out_grad,
+        (d_first_sum,),
     )
 
     def back(values, shape):
@@ -1012,13 +1285,13 @@
         hidden_gradient[None],
         back(last_grads[0], attention_down_maps.shape),
         last_grads[1].reshape(query_exit_maps.shape),
-        last_grads[2].reshape(key_value_exit_maps.shape),
-        back(feature_grads[2], output_entry_maps.shape),
-        feature_grads[3].reshape(output_exit_maps.shape),
-        back(feature_grads[0], feedforward_entry_maps.shape),
+        last_grads[6].reshape(key_value_exit_maps.shape),
+        back(last_grads[4], output_entry_maps.shape),
+        last_grads[5].reshape(output_exit_maps.shape),
+        back(last_grads[3], feedforward_entry_maps.shape),
         hidden_grads[0].reshape(feedforward_exit_maps.shape),
         back(hidden_grads[1], down_entry_maps.shape),
-        feature_grads[1].reshape(down_exit_maps.shape),
+        last_grads[2].reshape(down_exit_maps.shape),
     )
 
 

time: 1260 us -> 932 us (0.74)
  matrix products: 234 us -> 85 us
  waiting for transfers between devices: 411 us -> 272 us
  starting transfers between devices: 188 us -> 72.5 us
  Pallas kernels: 140 us -> 239 us
  local copies, waits for them, and re-layouts: 177 us -> 157 us
    ppermute x110 -> x64, waiting for transfers between devices: 411 us -> 272 us  [the longest x9 73.9 us: far(): lax.ppermute(chunk, 'wsh', FAR_SWAP)]
    ppermute x110 -> x64, starting transfers between devices: 186 us -> 71.6 us  [the longest x9 15.6 us: far(): lax.ppermute(chunk, 'wsh', FAR_SWAP)]
    pallas_call x9 -> x15, Pallas kernels: 68.9 us -> 147 us  [the longest x5 97 us: mlp_call(): pl.pallas_call(lambda *refs: mlp_body(owners, sums is not None, *refs), g...]
    dot_general x42 -> x20, matrix products: 126 us -> 49.5 us  [low_dot(): return jnp.dot(left, right, preferred_element_type=F32)]
    dot_general x19 -> x5, matrix products: 83.6 us -> 11.4 us  [reverse_product(): lax.dot_general(left, right, (((1,), (1,)), ((), ())), preferred_element_...]
    unnamed x440 -> x351, local copies, waits for them, and re-layouts: 105 us -> 82.5 us
    pallas_call x1 -> x2, Pallas kernels: 34 us -> 45.7 us  [attention_call(): pl.pallas_call(forward_body, grid_spec=pltpu.PrefetchScalarGridSpec(num_s...]
    pallas_call x1 -> x2, Pallas kernels: 27.7 us -> 36.7 us  [attention_back_call(): pl.pallas_call(backward_body, grid_spec=pltpu.PrefetchScalarGridSpec(num_...]
  transfers between devices with their start and end apart: 121 -> 73, of which waited for: 48 -> 34; matrix products, arithmetic and copies ran while one was open for 25% -> 29% of each run, Pallas kernels for 11% -> 22%
where the time goes in v2:
time: 932 us; the launch traced here: 918 us
  waiting for transfers between devices  272 us (29%)
  Pallas kernels  239 us (26%)
  local copies, waits for them, and re-layouts  157 us (17%)
  other arithmetic  89 us (10%)
  matrix products  85 us (9%)
  starting transfers between devices  72.5 us (8%)
    pallas_call x5, Pallas kernels, mlp_call(): pl.pallas_call(lambda *refs: mlp_body(owners, sums is not None, *refs), g...  97 us
    unnamed x351, local copies, waits for them, and re-layouts  82.5 us
    ppermute x9, waiting for transfers between devices, far(): lax.ppermute(chunk, 'wsh', FAR_SWAP)  73.9 us
    dot_general x20, matrix products, low_dot(): return jnp.dot(left, right, preferred_element_type=F32)  49.5 us
    ppermute x9, waiting for transfers between devices, near(): return jnp.concatenate([pair, lax.ppermute(pair, 'wsh', NEAR_SWAP)], axis=0)  47.4 us
    pallas_call x2, Pallas kernels, attention_call(): pl.pallas_call(forward_body, grid_spec=pltpu.PrefetchScalarGridSpec(num_s...  45.7 us
    pallas_call x2, Pallas kernels, attention_back_call(): pl.pallas_call(backward_body, grid_spec=pltpu.PrefetchScalarGridSpec(num_...  36.7 us
    pallas_call x9, Pallas kernels, final_call(): pl.pallas_call(final_body, grid_spec=pltpu.PrefetchScalarGridSpec(num_sca...  34.3 us
  transfers between devices with their start and end apart: 73, of which 34 were waited for; matrix products, arithmetic and copies ran while one was open for 29% of the time, Pallas kernels for 22%

profile of v2, /device:TPU:0, one launch (start us, length us, event | category | flops | bytes accessed | tf_op | source)
XLA Modules:
  0.0 918.3 jit_solution(14890800645517157516)
XLA Ops:
  46.3 15.5 %collective-permute-done = bf16[256,2176]{1,0:T(8,128)(2,1)} collective-permute-done((bf16[256,2176]{1,0:T(8,128)(2,1)}, bf16[256,2176]{1,0:T(8,128)(2,1)}, u32[]{:S(2)}, u32[]{:S(2)}) %collective-permute-start) | collective-permute-done | bytes 1114144 | tf_op jit(solution)/shard_map/ppermute | solution.py:1020
  79.2 14.7 %collective-permute-done.12 = bf16[256,1024]{1,0:T(8,128)(2,1)} collective-permute-done((bf16[256,1024]{1,0:T(8,128)(2,1)}, bf16[256,1024]{1,0:T(8,128)(2,1)}, u32[]{:S(2)}, u32[]{:S(2)}) %collective-permute-start.12) | collective-permute-done | bytes 524320 | tf_op jit(solution)/shard_map/ppermute | solution.py:125
  100.7 12.0 %collective-permute-done.6.w_other = bf16[1024,768]{1,0:T(8,128)(2,1)S(1)} collective-permute-done((bf16[1024,768]{1,0:T(8,128)(2,1)}, bf16[1024,768]{1,0:T(8,128)(2,1)S(1)}, u32[]{:S(2)}, u32[]{:S(2)}) %collective-permute-start.6) | collective-permute-done | bytes 1572896 | tf_op jit(solution)/shard_map/ppermute | solution.py:137
  115.7 11.4 %collective-permute-done.14 = bf16[512,1024]{1,0:T(8,128)(2,1)} collective-permute-done((bf16[512,1024]{1,0:T(8,128)(2,1)S(1)}, bf16[512,1024]{1,0:T(8,128)(2,1)}, u32[]{:S(2)}, u32[]{:S(2)}) %collective-permute-start.14) | collective-permute-done | bytes 1048608 | tf_op jit(solution)/shard_map/ppermute | solution.py:131
  154.0 9.2 %qkv.1 = (bf16[1024,512]{1,0:T(8,128)(2,1)}, bf16[1024,256]{1,0:T(8,128)(2,1)}, bf16[1024,256]{1,0:T(8,128)(2,1)}) custom-call(bf16[1024,2176]{1,0:T(8,128)(2,1)} %bitcast.415, bf16[1024,768]{1,0:T(8,128)(2,1)} %pad_maximum_fusion.12.w_own, bf16[1024,768]{1,0:T(8,128)(2,1)} %copy-done.138, bf16[1024,128]{1,0:T(8,128)(2,1)} %fusion.54.la_q, ...), custom_call_target="tpu_custom_call" | custom-call | flops 3221225472 | bytes 12582912 | tf_op jit(solution)/shard_map/qkv/pallas_call | solution.py:436
  163.2 22.8 %attention.2 = (bf16[1024,256]{1,0:T(8,128)(2,1)}, f32[1024,128]{1,0:T(8,128)}) custom-call(s32[4]{0:T(128)} %and_select_fusion.4.first_ref, bf16[1024,512]{1,0:T(8,128)(2,1)} %get-tuple-element.117.q_ref, bf16[1024,256]{1,0:T(8,128)(2,1)} %get-tuple-element.109.k_ref, bf16[1024,256]{1,0:T(8,128)(2,1)} %get-tuple-element.110.v_ref, ...), custom_call_target="tpu_custom_call" | custom-call | flops 2147483648 | bytes 3145728 | tf_op jit(solution)/shard_map/attention/pallas_call | solution.py:510
  195.1 22.9 %attention.3 = (bf16[1024,256]{1,0:T(8,128)(2,1)}, f32[1024,128]{1,0:T(8,128)}) custom-call(s32[4]{0:T(128)} %and_select_fusion.4.first_ref, bf16[1024,512]{1,0:T(8,128)(2,1)} %get-tuple-element.117.q_ref, bf16[1024,256]{1,0:T(8,128)(2,1)} %get-tuple-element.109.k_ref, bf16[1024,256]{1,0:T(8,128)(2,1)} %get-tuple-element.110.v_ref, ...), custom_call_target="tpu_custom_call" | custom-call | flops 2147483648 | bytes 3145728 | tf_op jit(solution)/shard_map/attention/pallas_call | solution.py:510
  249.6 18.3 %collective-permute-done.20 = bf16[256,1024]{1,0:T(8,128)(2,1)S(1)} collective-permute-done((bf16[256,1024]{1,0:T(8,128)(2,1)S(1)}, bf16[256,1024]{1,0:T(8,128)(2,1)S(1)}, u32[]{:S(2)}, u32[]{:S(2)}) %collective-permute-start.20) | collective-permute-done | bytes 524320 | tf_op jit(solution)/shard_map/ppermute | solution.py:125
  296.7 15.5 %collective-permute-done.24 = bf16[256,1024]{1,0:T(8,128)(2,1)S(1)} collective-permute-done((bf16[256,1024]{1,0:T(8,128)(2,1)S(1)}, bf16[256,1024]{1,0:T(8,128)(2,1)S(1)}, u32[]{:S(2)}, u32[]{:S(2)}) %collective-permute-start.24) | collective-permute-done | bytes 524320 | tf_op jit(solution)/shard_map/ppermute | solution.py:125
  334.0 24.7 %collective-permute-done.26 = bf16[512,1024]{1,0:T(8,128)(2,1)S(1)} collective-permute-done((bf16[512,1024]{1,0:T(8,128)(2,1)S(1)}, bf16[512,1024]{1,0:T(8,128)(2,1)S(1)}, u32[]{:S(2)}, u32[]{:S(2)}) %collective-permute-start.26) | collective-permute-done | bytes 1048608 | tf_op jit(solution)/shard_map/ppermute | solution.py:131
  366.8 13.3 %collective-permute-done.28.refs_3_ = bf16[1024,1024]{1,0:T(8,128)(2,1)} collective-permute-done((bf16[1024,1024]{1,0:T(8,128)(2,1)S(1)}, bf16[1024,1024]{1,0:T(8,128)(2,1)}, u32[]{:S(2)}, u32[]{:S(2)}) %collective-permute-start.28) | collective-permute-done | bytes 2097184 | tf_op jit(solution)/shard_map/ppermute | solution.py:137
  380.1 20.3 %units.5 = (bf16[1024,512]{1,0:T(8,128)(2,1)}, bf16[1024,512]{1,0:T(8,128)(2,1)}, bf16[1024,512]{1,0:T(8,128)(2,1)}, f32[1024,2048]{1,0:T(8,128)}, f32[1024,256]{1,0:T(8,128)}) custom-call(s32[2]{0:T(128)} %pad_add_fusion.refs_0_, bf16[1024,2176]{1,0:T(8,128)(2,1)} %bitcast.391, bf16[1024,1024]{1,0:T(8,128)(2,1)} %copy-done.95, ...), custom_call_target="tpu_custom_call" | custom-call | flops 10737418240 | bytes 33554432 | tf_op jit(solution)/shard_map/units/pallas_call | solution.py:759
  409.7 17.8 %collective-permute-done.30 = bf16[256,512]{1,0:T(8,128)(2,1)S(1)} collective-permute-done((bf16[256,512]{1,0:T(8,128)(2,1)S(1)}, bf16[256,512]{1,0:T(8,128)(2,1)S(1)}, u32[]{:S(2)}, u32[]{:S(2)}) %collective-permute-start.30) | collective-permute-done | bytes 262176 | tf_op jit(solution)/shard_map/ppermute | solution.py:125
  431.9 21.2 %units.6 = (bf16[1024,512]{1,0:T(8,128)(2,1)}, bf16[1024,512]{1,0:T(8,128)(2,1)}, bf16[1024,512]{1,0:T(8,128)(2,1)}, f32[1024,2048]{1,0:T(8,128)}, f32[1024,256]{1,0:T(8,128)}) custom-call(s32[2]{0:T(128)} %pad_add_fusion.1.refs_0_, bf16[1024,2176]{1,0:T(8,128)(2,1)} %bitcast.392, ...), custom_call_target="tpu_custom_call", output_to_operand_aliasing={{3}: (15, {}), {4}: (16, {})} | custom-call | flops 10737418240 | bytes 33554432 | tf_op jit(solution)/shard_map/units/pallas_call | solution.py:759
  477.5 21.3 %units.7 = (bf16[1024,512]{1,0:T(8,128)(2,1)}, bf16[1024,512]{1,0:T(8,128)(2,1)}, bf16[1024,512]{1,0:T(8,128)(2,1)}, f32[1024,2048]{1,0:T(8,128)}, f32[1024,256]{1,0:T(8,128)}) custom-call(s32[2]{0:T(128)} %pad_add_fusion.2.refs_0_, bf16[1024,2176]{1,0:T(8,128)(2,1)} %bitcast.393, ...), custom_call_target="tpu_custom_call", output_to_operand_aliasing={{3}: (15, {}), {4}: (16, {})} | custom-call | flops 10737418240 | bytes 33554432 | tf_op jit(solution)/shard_map/units/pallas_call | solution.py:759
  511.3 17.2 %units.8 = (bf16[1024,256]{1,0:T(8,128)(2,1)}, bf16[1024,256]{1,0:T(8,128)(2,1)}, bf16[1024,256]{1,0:T(8,128)(2,1)}, f32[1024,2048]{1,0:T(8,128)}, f32[1024,256]{1,0:T(8,128)}) custom-call(s32[2]{0:T(128)} %pad_add_fusion.3.refs_0_, bf16[1024,2176]{1,0:T(8,128)(2,1)} %bitcast.394, ...), custom_call_target="tpu_custom_call", output_to_operand_aliasing={{3}: (15, {}), {4}: (16, {})} | custom-call | flops 5368709120 | bytes 33554432 | tf_op jit(solution)/shard_map/units/pallas_call | solution.py:759
  533.8 16.9 %units.9 = (bf16[1024,256]{1,0:T(8,128)(2,1)}, bf16[1024,256]{1,0:T(8,128)(2,1)}, bf16[1024,256]{1,0:T(8,128)(2,1)}, f32[1024,2048]{1,0:T(8,128)}, f32[1024,256]{1,0:T(8,128)}) custom-call(s32[2]{0:T(128)} %pad_add_fusion.3.refs_0_, bf16[1024,2176]{1,0:T(8,128)(2,1)} %bitcast.395, ...), custom_call_target="tpu_custom_call", output_to_operand_aliasing={{3}: (15, {}), {4}: (16, {})} | custom-call | flops 5368709120 | bytes 33554432 | tf_op jit(solution)/shard_map/units/pallas_call | solution.py:759
  571.9 15.8 %units_out.1 = f32[1024,2048]{1,0:T(8,128)} custom-call(s32[5]{0:T(128)} %stack.190.refs_0_, bf16[1024,512]{1,0:T(8,128)(2,1)} %get-tuple-element.140.refs_1_, bf16[1024,512]{1,0:T(8,128)(2,1)} %get-tuple-element.147.refs_2_, bf16[1024,512]{1,0:T(8,128)(2,1)} %get-tuple-element.154.refs_3_, bf16[1024,256]{1,0:T(8,128)(2,1)} %get-tuple-element.159.refs_4_, ...), custom_call_target="tpu_custom_call" | custom-call | flops 8589934592 | bytes 20971520 | tf_op jit(solution)/shard_map/units_out/pallas_call | solution.py:801
  621.7 16.9 %collective-permute-done.41 = bf16[256,2176]{1,0:T(8,128)(2,1)S(1)} collective-permute-done((bf16[256,2176]{1,0:T(8,128)(2,1)}, bf16[256,2176]{1,0:T(8,128)(2,1)S(1)}, u32[]{:S(2)}, u32[]{:S(2)}) %collective-permute-start.41) | collective-permute-done | bytes 1114144 | tf_op jit(solution)/shard_map/ppermute | solution.py:211
  696.8 18.4 %attention_back.2 = (bf16[1024,256]{1,0:T(8,128)(2,1)}, bf16[1024,128]{1,0:T(8,128)(2,1)}, bf16[1024,128]{1,0:T(8,128)(2,1)}) custom-call(s32[4]{0:T(128)} %and_select_fusion.4.first_ref, bf16[1024,512]{1,0:T(8,128)(2,1)} %get-tuple-element.117.q_ref, bf16[1024,256]{1,0:T(8,128)(2,1)} %get-tuple-element.109.k_ref, ...), custom_call_target="tpu_custom_call" | custom-call | flops 5368709120 | bytes 5242880 | tf_op jit(solution)/shard_map/attention_back/pallas_call | solution.py:614
  724.6 18.2 %attention_back.3 = (bf16[1024,256]{1,0:T(8,128)(2,1)}, bf16[1024,128]{1,0:T(8,128)(2,1)}, bf16[1024,128]{1,0:T(8,128)(2,1)}) custom-call(s32[4]{0:T(128)} %and_select_fusion.4.first_ref, bf16[1024,512]{1,0:T(8,128)(2,1)} %get-tuple-element.117.q_ref, bf16[1024,256]{1,0:T(8,128)(2,1)} %get-tuple-element.109.k_ref, ...), custom_call_target="tpu_custom_call" | custom-call | flops 5368709120 | bytes 5242880 | tf_op jit(solution)/shard_map/attention_back/pallas_call | solution.py:614
  794.3 10.3 %collective-permute-done.62 = bf16[640,512]{1,0:T(8,128)(2,1)S(1)} collective-permute-done((bf16[640,512]{1,0:T(8,128)(2,1)S(1)}, bf16[640,512]{1,0:T(8,128)(2,1)S(1)}, u32[]{:S(2)}, u32[]{:S(2)}) %collective-permute-start.62) | collective-permute-done | bytes 655392 | tf_op jit(solution)/shard_map/ppermute | solution.py:295
  858.0 11.1 %finish.9 = f32[2,128,8192]{2,1,0:T(8,128)} custom-call(s32[1]{0:T(128)} %bitcast.111.s_ref, bf16[1536,512]{1,0:T(8,128)(2,1)} %pad_maximum_fusion.14.own, bf16[1536,512]{1,0:T(8,128)(2,1)} %collective-permute-done.58.core, bf16[1536,512]{1,0:T(8,128)(2,1)} %constant_dynamic-update-slice_fusion.54.other, bf16[1536,512]{1,0:T(8,128)(2,1)} %collective-permute-done.59.last), custom_call_target="tpu_custom_call" | custom-call | tf_op jit(solution)/shard_map/finish/pallas_call | solution.py:337
  877.2 14.5 %collective-permute-done.71.other = bf16[1280,512]{1,0:T(8,128)(2,1)} collective-permute-done((bf16[1280,512]{1,0:T(8,128)(2,1)S(1)}, bf16[1280,512]{1,0:T(8,128)(2,1)}, u32[]{:S(2)}, u32[]{:S(2)}) %collective-permute-start.71) | collective-permute-done | bytes 1310752 | tf_op jit(solution)/shard_map/ppermute | solution.py:312
  (744 shorter events, 514.7 us)
Async XLA Ops:
  4.2 37.9 %collective-permute-start.4 = (bf16[256,768]{1,0:T(8,128)(2,1)}, bf16[256,768]{1,0:T(8,128)(2,1)S(1)}, u32[]{:S(2)}, u32[]{:S(2)}) collective-permute-start(bf16[256,768]{1,0:T(8,128)(2,1)} %pad_maximum_fusion.33), channel_id=1, source_target_pairs={{0,4},{1,5},{2,6},{3,7},{4,0},{5,1},{6,2},{7,3},{8,12},{9,13},{10,... | collective-permute-start | bytes 1179656 | tf_op jit(solution)/shard_map/ppermute | solution.py:125
  14.2 32.1 %collective-permute-start.1 = (bf16[256,2048]{1,0:T(8,128)(2,1)}, bf16[256,2048]{1,0:T(8,128)(2,1)}, u32[]{:S(2)}, u32[]{:S(2)}) collective-permute-start(bf16[256,2048]{1,0:T(8,128)(2,1)} %fusion.38), channel_id=1, source_target_pairs={{0,16},{8,24},{16,0},{24,8},{1,17},{9,25},{17,1},{25,9},{2,18},{10... | collective-permute-start | bytes 3145736 | tf_op jit(solution)/shard_map/ppermute | solution.py:1019
  65.7 65.2 %collective-permute-start.2 = (bf16[2,256,2176]{2,1,0:T(8,128)(2,1)}, bf16[2,256,2176]{2,1,0:T(8,128)(2,1)}, u32[]{:S(2)}, u32[]{:S(2)}) collective-permute-start(bf16[2,256,2176]{2,1,0:T(8,128)(2,1)} %pad_maximum_fusion.4), channel_id=1, source_target_pairs={{0,8},{8,0},{16,24},{24,16},{1,9},{9,1},{17,25},{25,17},{2,10},{10... | collective-permute-start | bytes 6684680 | tf_op jit(solution)/shard_map/ppermute | solution.py:216
  75.5 37.2 %collective-permute-start.6 = (bf16[1024,768]{1,0:T(8,128)(2,1)}, bf16[1024,768]{1,0:T(8,128)(2,1)S(1)}, u32[]{:S(2)}, u32[]{:S(2)}) collective-permute-start(bf16[1024,768]{1,0:T(8,128)(2,1)} %pad_maximum_fusion.12.w_own), channel_id=1, source_target_pairs={{0,1},{1,0},{2,3},{3,2},{4,5},{5,4},{6,7},{7,6},{8,9},{9,8},{10,11... | collective-permute-start | bytes 4718600 | tf_op jit(solution)/shard_map/ppermute | solution.py:137
  127.1 148.2 %collective-permute-start.19 = (bf16[512,1024]{1,0:T(8,128)(2,1)}, bf16[512,1024]{1,0:T(8,128)(2,1)}, u32[]{:S(2)}, u32[]{:S(2)}) collective-permute-start(bf16[512,1024]{1,0:T(8,128)(2,1)} %collective-permute-done.14), channel_id=1, source_target_pairs={{0,1},{1,0},{2,3},{3,2},{4,5},{5,4},{6,7},{7,6},{8,9},{9,8},{10,11... | collective-permute-start | bytes 3145736 | tf_op jit(solution)/shard_map/ppermute | solution.py:1084
  186.0 33.3 %collective-permute-start.15 = (bf16[512,1024]{1,0:T(8,128)(2,1)}, bf16[512,1024]{1,0:T(8,128)(2,1)}, u32[]{:S(2)}, u32[]{:S(2)}) collective-permute-start(bf16[512,1024]{1,0:T(8,128)(2,1)} %copy-done.55), channel_id=1, source_target_pairs={{0,2},{1,3},{2,0},{3,1},{4,6},{5,7},{6,4},{7,5},{8,10},{9,11},{10,... | collective-permute-start | bytes 3145736 | tf_op jit(solution)/shard_map/ppermute | solution.py:131
  188.0 34.0 %collective-permute-start.16 = (bf16[512,1024]{1,0:T(8,128)(2,1)}, bf16[512,1024]{1,0:T(8,128)(2,1)}, u32[]{:S(2)}, u32[]{:S(2)}) collective-permute-start(bf16[512,1024]{1,0:T(8,128)(2,1)} %copy-done.54), channel_id=1, source_target_pairs={{0,1},{1,0},{2,3},{3,2},{4,5},{5,4},{6,7},{7,6},{8,9},{9,8},{10,11... | collective-permute-start | bytes 3145736 | tf_op jit(solution)/shard_map/ppermute | solution.py:1083
  237.7 32.2 %collective-permute-start.18 = (bf16[256,2176]{1,0:T(8,128)(2,1)S(1)}, bf16[256,2176]{1,0:T(8,128)(2,1)S(1)}, u32[]{:S(2)}, u32[]{:S(2)}) collective-permute-start(bf16[256,2176]{1,0:T(8,128)(2,1)S(1)} %fusion.87), channel_id=1, source_target_pairs={{0,16},{8,24},{16,0},{24,8},{1,17},{9,25},{17,1},{25,9},{2,18},{10... | collective-permute-start | bytes 3342344 | tf_op jit(solution)/shard_map/ppermute | solution.py:235
  248.1 65.5 %collective-permute-start.22 = (bf16[1024,1024]{1,0:T(8,128)(2,1)}, bf16[1024,1024]{1,0:T(8,128)(2,1)}, u32[]{:S(2)}, u32[]{:S(2)}) collective-permute-start(bf16[1024,1024]{1,0:T(8,128)(2,1)} %constant_dynamic-update-slice_fusion.17.refs_11_.refs_8_), channel_id=1, source_target_pairs={{0,1},{1,0},{2,3},{3,2},{4,5},{5,4},{6,7},{7,6},{8,9},{9,8},{10,11... | collective-permute-start | bytes 6291464 | tf_op jit(solution)/shard_map/ppermute | solution.py:137
  269.0 43.3 %collective-permute-start.23 = (bf16[512,1024]{1,0:T(8,128)(2,1)}, bf16[512,1024]{1,0:T(8,128)(2,1)}, u32[]{:S(2)}, u32[]{:S(2)}) collective-permute-start(bf16[512,1024]{1,0:T(8,128)(2,1)} %pad_maximum_fusion.18), channel_id=1, source_target_pairs={{0,2},{1,3},{2,0},{3,1},{4,6},{5,7},{6,4},{7,5},{8,10},{9,11},{10,... | collective-permute-start | bytes 3145736 | tf_op jit(solution)/shard_map/ppermute | solution.py:131
  316.1 46.2 %collective-permute-start.25 = (bf16[2,256,2176]{2,1,0:T(8,128)(2,1)S(1)}, bf16[2,256,2176]{2,1,0:T(8,128)(2,1)S(1)}, u32[]{:S(2)}, u32[]{:S(2)}) collective-permute-start(bf16[2,256,2176]{2,1,0:T(8,128)(2,1)S(1)} %pad_maximum_fusion.6), channel_id=1, source_target_pairs={{0,8},{8,0},{16,24},{24,16},{1,9},{9,1},{17,25},{25,17},{2,10},{10... | collective-permute-start | bytes 6684680 | tf_op jit(solution)/shard_map/ppermute | solution.py:216
  321.9 36.8 %collective-permute-start.26 = (bf16[512,1024]{1,0:T(8,128)(2,1)S(1)}, bf16[512,1024]{1,0:T(8,128)(2,1)S(1)}, u32[]{:S(2)}, u32[]{:S(2)}) collective-permute-start(bf16[512,1024]{1,0:T(8,128)(2,1)S(1)} %pad_maximum_fusion.19), channel_id=1, source_target_pairs={{0,2},{1,3},{2,0},{3,1},{4,6},{5,7},{6,4},{7,5},{8,10},{9,11},{10,... | collective-permute-start | bytes 3145736 | tf_op jit(solution)/shard_map/ppermute | solution.py:131
  326.0 35.3 %collective-permute-start.27 = (bf16[256,1024]{1,0:T(8,128)(2,1)S(1)}, bf16[256,1024]{1,0:T(8,128)(2,1)S(1)}, u32[]{:S(2)}, u32[]{:S(2)}) collective-permute-start(bf16[256,1024]{1,0:T(8,128)(2,1)S(1)} %pad_maximum_fusion.30), channel_id=1, source_target_pairs={{0,4},{1,5},{2,6},{3,7},{4,0},{5,1},{6,2},{7,3},{8,12},{9,13},{10,... | collective-permute-start | bytes 1572872 | tf_op jit(solution)/shard_map/ppermute | solution.py:125
  331.4 48.7 %collective-permute-start.28 = (bf16[1024,1024]{1,0:T(8,128)(2,1)S(1)}, bf16[1024,1024]{1,0:T(8,128)(2,1)}, u32[]{:S(2)}, u32[]{:S(2)}) collective-permute-start(bf16[1024,1024]{1,0:T(8,128)(2,1)S(1)} %constant_dynamic-update-slice_fusion.27.refs_2_), channel_id=1, source_target_pairs={{0,1},{1,0},{2,3},{3,2},{4,5},{5,4},{6,7},{7,6},{8,9},{9,8},{10,11... | collective-permute-start | bytes 6291464 | tf_op jit(solution)/shard_map/ppermute | solution.py:137
  359.8 72.2 %collective-permute-start.31 = (bf16[1024,1024]{1,0:T(8,128)(2,1)}, bf16[1024,1024]{1,0:T(8,128)(2,1)}, u32[]{:S(2)}, u32[]{:S(2)}) collective-permute-start(bf16[1024,1024]{1,0:T(8,128)(2,1)} %constant_dynamic-update-slice_fusion.29.refs_2_), channel_id=1, source_target_pairs={{0,1},{1,0},{2,3},{3,2},{4,5},{5,4},{6,7},{7,6},{8,9},{9,8},{10,11... | collective-permute-start | bytes 6291464 | tf_op jit(solution)/shard_map/ppermute | solution.py:137
  430.4 47.0 %collective-permute-start.34 = (bf16[1024,1024]{1,0:T(8,128)(2,1)}, bf16[1024,1024]{1,0:T(8,128)(2,1)}, u32[]{:S(2)}, u32[]{:S(2)}) collective-permute-start(bf16[1024,1024]{1,0:T(8,128)(2,1)} %constant_dynamic-update-slice_fusion.33.refs_2_), channel_id=1, source_target_pairs={{0,1},{1,0},{2,3},{3,2},{4,5},{5,4},{6,7},{7,6},{8,9},{9,8},{10,11... | collective-permute-start | bytes 6291464 | tf_op jit(solution)/shard_map/ppermute | solution.py:137
  473.4 38.0 %collective-permute-start.36 = (bf16[1024,512]{1,0:T(8,128)(2,1)}, bf16[1024,512]{1,0:T(8,128)(2,1)}, u32[]{:S(2)}, u32[]{:S(2)}) collective-permute-start(bf16[1024,512]{1,0:T(8,128)(2,1)} %constant_dynamic-update-slice_fusion.35.refs_2_), channel_id=1, source_target_pairs={{0,1},{1,0},{2,3},{3,2},{4,5},{5,4},{6,7},{7,6},{8,9},{9,8},{10,11... | collective-permute-start | bytes 3145736 | tf_op jit(solution)/shard_map/ppermute | solution.py:137
  571.0 68.8 %collective-permute-start.44 = (bf16[768,512]{1,0:T(8,128)(2,1)}, bf16[768,512]{1,0:T(8,128)(2,1)}, u32[]{:S(2)}, u32[]{:S(2)}) collective-permute-start(bf16[768,512]{1,0:T(8,128)(2,1)} %fusion.109), channel_id=1, source_target_pairs={{0,1},{1,0},{2,3},{3,2},{4,5},{5,4},{6,7},{7,6},{8,9},{9,8},{10,11... | collective-permute-start | bytes 2359304 | tf_op jit(solution)/shard_map/ppermute | solution.py:295
  621.6 58.9 %collective-permute-start.38 = (bf16[2,256,2176]{2,1,0:T(8,128)(2,1)S(1)}, bf16[2,256,2176]{2,1,0:T(8,128)(2,1)S(1)}, u32[]{:S(2)}, u32[]{:S(2)}) collective-permute-start(bf16[2,256,2176]{2,1,0:T(8,128)(2,1)S(1)} %pad_maximum_fusion.7), channel_id=1, source_target_pairs={{0,8},{8,0},{16,24},{24,16},{1,9},{9,1},{17,25},{25,17},{2,10},{10... | collective-permute-start | bytes 6684680 | tf_op jit(solution)/shard_map/ppermute | solution.py:232
  639.2 44.1 %collective-permute-start.42 = (bf16[2,256,2176]{2,1,0:T(8,128)(2,1)S(1)}, bf16[2,256,2176]{2,1,0:T(8,128)(2,1)S(1)}, u32[]{:S(2)}, u32[]{:S(2)}) collective-permute-start(bf16[2,256,2176]{2,1,0:T(8,128)(2,1)S(1)} %pad_maximum_fusion.9), channel_id=1, source_target_pairs={{0,8},{8,0},{16,24},{24,16},{1,9},{9,1},{17,25},{25,17},{2,10},{10... | collective-permute-start | bytes 6684680 | tf_op jit(solution)/shard_map/ppermute | solution.py:216
  790.7 46.1 %collective-permute-start.53 = (bf16[2,256,2048]{2,1,0:T(8,128)(2,1)S(1)}, bf16[2,256,2048]{2,1,0:T(8,128)(2,1)S(1)}, u32[]{:S(2)}, u32[]{:S(2)}) collective-permute-start(bf16[2,256,2048]{2,1,0:T(8,128)(2,1)S(1)} %pad_maximum_fusion.11), channel_id=1, source_target_pairs={{0,8},{8,0},{16,24},{24,16},{1,9},{9,1},{17,25},{25,17},{2,10},{10... | collective-permute-start | bytes 6291464 | tf_op jit(solution)/shard_map/ppermute | solution.py:232
  793.4 31.0 %collective-permute-start.56 = (bf16[768,512]{1,0:T(8,128)(2,1)S(1)}, bf16[768,512]{1,0:T(8,128)(2,1)S(1)}, u32[]{:S(2)}, u32[]{:S(2)}) collective-permute-start(bf16[768,512]{1,0:T(8,128)(2,1)S(1)} %copy-done.47), channel_id=1, source_target_pairs={{0,16},{8,24},{16,0},{24,8},{1,17},{9,25},{17,1},{25,9},{2,18},{10... | collective-permute-start | bytes 2359304 | tf_op jit(solution)/shard_map/ppermute | solution.py:315
  851.0 40.7 %collective-permute-start.71 = (bf16[1280,512]{1,0:T(8,128)(2,1)S(1)}, bf16[1280,512]{1,0:T(8,128)(2,1)}, u32[]{:S(2)}, u32[]{:S(2)}) collective-permute-start(bf16[1280,512]{1,0:T(8,128)(2,1)S(1)} %pad_maximum_fusion.15.own), channel_id=1, source_target_pairs={{0,16},{8,24},{16,0},{24,8},{1,17},{9,25},{17,1},{25,9},{2,18},{10... | collective-permute-start | bytes 3932168 | tf_op jit(solution)/shard_map/ppermute | solution.py:312
  851.8 49.2 %collective-permute-start.70 = (bf16[1280,512]{1,0:T(8,128)(2,1)S(1)}, bf16[1280,512]{1,0:T(8,128)(2,1)}, u32[]{:S(2)}, u32[]{:S(2)}) collective-permute-start(bf16[1280,512]{1,0:T(8,128)(2,1)S(1)} %pad_maximum_fusion.15.own), channel_id=1, source_target_pairs={{0,8},{8,0},{16,24},{24,16},{1,9},{9,1},{17,25},{25,17},{2,10},{10... | collective-permute-start | bytes 3932168 | tf_op jit(solution)/shard_map/ppermute | solution.py:310
  (194 other events, 2392.7 us)

commit v3 on v2

--- a/solution.py
+++ b/solution.py
@@ -135,6 +135,12 @@
         if not self.fast:
             return (lax.all_gather(four, "wsh", axis=0, tiled=True),)
         return four, lax.ppermute(four, "wsh", X_SWAP)
+
+    def across_parts(self, four, *deps):
+        rows = four.shape[0] // 2
+        parts = [four[:rows], four[rows:]]
+        parts = [lax.ppermute(after(v, *deps), "wsh", X_SWAP) for v in parts]
+        return (four, jnp.concatenate(parts, axis=0)), parts
 
     def swap_bits(self, d):
         return d // 2 + 2 * (d % 2)
@@ -234,6 +240,8 @@
         away = (pick(mine, 1 - self.y, 0) + pick(got, 1 - self.y, 0)).astype(BF)
         other = lax.ppermute(after(away, *deps), "seq", Y_SWAP)
         self.marks[mark] = other
+        if mark is not None:
+            self.marks[mark + "_away"] = away
         other = after(other, *late).astype(F32)
         total = pick(mine, self.y, 0) + pick(got, self.y, 0) + other
         found, at = [], 0
@@ -242,33 +250,34 @@
             at += v.shape[1]
         return found
 
-    def sum_small(self, partial):
+    def sum_small(self, partial, deps=()):
         if not self.fast:
             return lax.psum(partial, "seq")
         total = partial.astype(F32) + lax.ppermute(partial, "seq", CORE_SWAP).astype(F32)
-        other = lax.ppermute(total.astype(BF), "seq", Y_SWAP)
+        other = lax.ppermute(after(total.astype(BF), *deps), "seq", Y_SWAP)
         return total + other.astype(F32)
 
     def sum_plain(self, grad):
         total = lax.psum(grad.astype(BF), "wsh")
         return lax.all_gather(total.astype(BF), "seq", axis=0).astype(F32)
 
-    def sum_hidden(self, grads, hid_block, deps=(), mark=None, early=()):
-        if not self.fast:
-            found = []
-            for grad in grads:
-                rows = grad.shape[0]
-                wide = self.sum_plain(grad).reshape(self.seq_size, rows, self.wsh_size, hid_block)
-                found.append(wide.transpose(1, 2, 0, 3).reshape(rows, -1))
-            return [jnp.stack(found[:2]), found[2]]
-        parts = self.sum_gather(jnp.concatenate([pack(v) for v in grads], axis=0), deps, (), mark, early)
+    def plain_hidden(self, grads, hid_block):
+        found = []
+        for grad in grads:
+            rows = grad.shape[0]
+            wide = self.sum_plain(grad).reshape(self.seq_size, rows, self.wsh_size, hid_block)
+            found.append(wide.transpose(1, 2, 0, 3).reshape(rows, -1))
+        return [jnp.stack(found[:2]), found[2]]
+
+    def sum_hidden(self, half, deps, mark, early):
+        parts = self.sum_end(half, deps, mark, early)
         s = self.s.astype(jnp.int32)[None]
         return [
             final_hidden(parts, s, 0, 2),
             final_hidden(parts, s, 8 * LANES, 1)[0],
         ]
 
-    def sum_features(self, grads, key=None, value=None, late=()):
+    def sum_features(self, grads, key=None, value=None, mid=(), deps=()):
         if not self.fast:
             grads = grads + ([key, value] if key is not None else [])
             found = []
@@ -279,7 +288,7 @@
         if key is not None:
             rest = jnp.zeros((key.shape[0], PACK - 2 * LANES), F32)
             packed.append(jnp.concatenate([key, value, rest], axis=1))
-        parts = self.sum_gather(jnp.concatenate(packed, axis=0), (), late)
+        parts = self.sum_end(self.sum_start(jnp.concatenate(packed, axis=0), mid), deps)
         s = self.s.astype(jnp.int32)[None]
         found, at = [], 0
         for grad in grads:
@@ -289,12 +298,12 @@
             found.append(final_kv(parts, s, at))
         return found
 
-    def sum_gather(self, packed, deps=(), late=(), mark=None, early=()):
+    def sum_start(self, packed, mid=()):
         rows = packed.shape[0]
         halves = packed.reshape(2, rows // 2, PACK)
         got = lax.ppermute(pick(halves, 1 - self.x, 0).astype(BF), "wsh", X_SWAP)
         half = pick(halves, self.x, 0) + got.astype(F32)
-        blocks = half.reshape(4, rows // 8, PACK)
+        blocks = after(half, *mid).reshape(4, rows // 8, PACK)
         total = pick(blocks, self.z, 0)
         for r in range(1, 4):
             out = pick(blocks, (self.z + r) % 4, 0).astype(BF)
@@ -302,7 +311,10 @@
         own = total.astype(BF)
         got = [own] + [lax.ppermute(own, "wsh", z_shift(r)) for r in range(1, 4)]
         ring = jnp.stack(got)
-        half = jnp.concatenate([pick(ring, (self.z - j) % 4, 0) for j in range(4)], axis=0)
+        return jnp.concatenate([pick(ring, (self.z - j) % 4, 0) for j in range(4)], axis=0)
+
+    def sum_end(self, half, deps=(), mark=None, early=()):
+        rows = 2 * half.shape[0]
         half = after(half, *early)
         other = lax.ppermute(half, "wsh", X_SWAP)
         first = self.x == 0
@@ -315,7 +327,6 @@
             rest = lax.ppermute(after(part[rows // 2 :], top), "seq", Y_SWAP)
             self.marks[mark] = (top, rest)
             other = jnp.concatenate([top, rest], axis=0)
-        other = after(other, *late)
         return part, core, other, lax.ppermute(other, "seq", CORE_SWAP)
 
 
@@ -1030,7 +1041,6 @@
         d_mlp = mover.gather_rest(d_mlp_local, after(d_mlp_other, first_all))
         low_four = mover.near(low_pair, out_four)
         high_pair = mover.far(down_local[:, half_width:], low_pair, qkv_full[1])
-        first_all = after(first_all, d_mlp)
     else:
         qkv_full = mover.across(qkv_pair)
         first_all = mover.gather_tokens(first_cols)
@@ -1085,11 +1095,13 @@
         ]
         down_low = (low_four, jnp.concatenate(low_other, axis=0))
         high_four = mover.near(high_pair, low_four, early)
-        attended = attend_rest(out_full, high_pair)
-        chunk_pairs = [gate_up_far(0, high_four)]
+        attended = attend_rest(out_full, high_pair, d_mlp)
+        chunk_pairs = [gate_up_far(0, high_pair, early)]
         attended = after(attended, high_four, low_other[0])
-        down_high = mover.across(high_four)
+        down_high, high_parts = mover.across_parts(high_four)
         chunk_fours = [mover.near(chunk_pairs[0], high_four)]
+        chunk_weights, chunk_parts = mover.across_parts(chunk_fours[0])
+        chunk_weights = [chunk_weights]
         chunk_pairs.append(gate_up_far(1, chunk_pairs[0]))
     else:
         attended = attend_rest()
@@ -1097,14 +1109,16 @@
     out_entry = cut(turned(output_entry_maps), s * q_cols, q_cols, 1)
     out_exit = output_exit_maps.reshape(flat, -1)
     la_out_part = fold(reverse_product(attended, out_entry) * mask_rank, rank, 0)
-    attn_sum = mover.scatter_tokens(low_dot(attended, out_full), la_out_part)
+    attn_sum = mover.scatter_tokens(
+        low_dot(attended, out_full), la_out_part, deps=chunk_pairs[:1] if mover.fast else ()
+    )
     la_out_own = attn_sum[1].astype(BF)
     attention_path = attn_sum[0] + low_dot(
         spread(la_out_own, own_owner, rank, 0, adapters), out_exit
     )
     middle = hidden_state + RESIDUAL_MULT * attention_path
     if mover.fast:
-        middle = after(middle, low_other[1], chunk_pairs[0])
+        middle = after(middle, low_other[1], high_parts[0], chunk_fours[0])
 
     second_normed, scale_two = normed(middle, feedforward_norm_gain)
     second_normed = second_normed.astype(BF)
@@ -1119,7 +1133,7 @@
     if mover.fast:
         second_other = lax.ppermute(second_cols, "seq", Y_SWAP)
         second_all = mover.gather_rest(
-            second_cols, after(second_other, down_high[1], chunk_fours[0], chunk_pairs[1])
+            second_cols, after(second_other, high_parts[1], chunk_parts[0], chunk_pairs[1])
         )
     else:
         second_all = mover.gather_tokens(second_cols)
@@ -1132,9 +1146,8 @@
     down_entry = jnp.concatenate(own_hidden(turned(down_entry_maps)), axis=1)
     all_exits = feedforward_exit_maps.reshape(2, flat, -1)
     exits = [jnp.concatenate(own_hidden(all_exits[i]), axis=1) for i in range(2)]
-    mixed_parts, gate_grads, up_grads, entry_grads = [], [], [], []
+    units_found = []
     if mover.fast:
-        chunk_weights = [mover.across(chunk_fours[0])]
         sums = None
         for i, units in enumerate(chunks):
             if i + 1 < len(chunks):
@@ -1163,10 +1176,7 @@
                 down_entry[:, lower:upper],
                 sums,
             )
-            mixed_parts.append(mixed)
-            gate_grads.append(gradient_product(la_gate, d_gate))
-            up_grads.append(gradient_product(la_up, d_up))
-            entry_grads.append(gradient_product(d_la_d, mixed))
+            units_found.append((mixed, d_gate, d_up))
         d_second, d_la_both = sums
         d_la_gate, d_la_up = d_la_both[:, :flat], d_la_both[:, flat:]
     else:
@@ -1183,12 +1193,14 @@
         d_second = reverse_product(jnp.concatenate([d_gate, d_up], axis=1), weights)
         d_la_gate = reverse_product(d_gate, exits[0])
         d_la_up = reverse_product(d_up, exits[1])
-        mixed_parts.append(mixed)
-        gate_grads.append(gradient_product(la_gate, d_gate))
-        up_grads.append(gradient_product(la_up, d_up))
-        entry_grads.append(gradient_product(d_la_d, mixed))
+        units_found.append((mixed, d_gate, d_up))
     d_la_two_part = fold(d_la_gate * mask_rank, rank, 0) + fold(d_la_up * mask_rank, rank, rank)
-    d_second_sum = mover.scatter_tokens(d_second, d_la_two_part)
+    d_second_sum = mover.scatter_tokens(d_second, d_la_two_part, mark="second")
+    units_found[-1] = after(units_found[-1], mover.marks.get("second_away"))
+    mixed_parts = [found[0] for found in units_found]
+    gate_grads = [gradient_product(la_gate, found[1]) for found in units_found]
+    up_grads = [gradient_product(la_up, found[2]) for found in units_found]
+    entry_grads = [gradient_product(d_la_d, found[0]) for found in units_found]
     d_la_two_own = d_second_sum[1].astype(BF)
     d_second_own = mover.from_slots(d_second_sum[0], row_block) + low_dot(
         spread(d_la_two_own, own_owner, 2 * rank, 0, adapters), entry_maps
@@ -1197,11 +1209,18 @@
         middle, scale_two, feedforward_norm_gain, d_second_own
     )
     d_attn_own = (RESIDUAL_MULT * grad_middle).astype(BF)
-    d_attn_all = mover.gather_tokens(jnp.concatenate([d_attn_own, d_la_two_own], axis=1))
-    d_attn = d_attn_all[:, :width]
     gate_grad = jnp.concatenate(gate_grads, axis=1)
     up_grad = jnp.concatenate(up_grads, axis=1)
     down_in_grad = jnp.concatenate(entry_grads, axis=1)
+    d_attn_cols = jnp.concatenate([d_attn_own, d_la_two_own], axis=1)
+    if mover.fast:
+        packed = jnp.concatenate([pack(v) for v in (gate_grad, up_grad, down_in_grad)], axis=0)
+        hidden_half = mover.sum_start(packed)
+        d_attn_other = lax.ppermute(d_attn_cols, "seq", Y_SWAP)
+        d_attn_all = mover.gather_rest(d_attn_cols, after(d_attn_other, hidden_half))
+    else:
+        d_attn_all = mover.gather_tokens(d_attn_cols)
+    d_attn = d_attn_all[:, :width]
 
     mixed_all = jnp.concatenate(mixed_parts, axis=1)
     la_down_part = fold(reverse_product(mixed_all, down_entry) * mask_rank, rank, 0)
@@ -1212,9 +1231,12 @@
     else:
         mlp_part = low_dot(mixed_all, down_full)
     mlp_sum = mover.scatter_tokens(mlp_part, la_down_part, deps=(d_attn_all,), mark="mlp")
-    hidden_grads = mover.sum_hidden(
-        [gate_grad, up_grad, down_in_grad], hid_block, (mover.marks.get("mlp"),), "hidden", (d_attn_all,)
-    )
+    if mover.fast:
+        hidden_grads = mover.sum_hidden(
+            hidden_half, (mover.marks["mlp"],), "hidden", (d_attn_all,)
+        )
+    else:
+        hidden_grads = mover.plain_hidden([gate_grad, up_grad, down_in_grad], hid_block)
     hidden_sent = mover.marks.get("hidden", (None, None))
     la_down_own = mlp_sum[1].astype(BF)
     feedforward_path = mlp_sum[0] + low_dot(
@@ -1246,14 +1268,15 @@
         + fold(reverse_product(d_key, key_exit) * mask_rank, rank, rank)
         + fold(reverse_product(d_value, value_exit) * mask_rank, rank, 2 * rank)
     )
-    d_la_one = mover.sum_small(d_la_one_part.astype(BF)).astype(BF)
+    d_la_one = mover.sum_small(d_la_one_part.astype(BF), hidden_sent[1:]).astype(BF)
     d_qkv = jnp.concatenate([d_query, d_key, d_value], axis=1)
     d_qkv = after(d_qkv, d_la_one_part)
     d_first_sum = jnp.concatenate(
         mover.scatter_tokens(
             *[reverse_product(d_qkv, half) for half in qkv_full],
-            deps=(d_la_one, hidden_sent[1]),
+            deps=(d_la_one,),
             late=hidden_grads,
+            mark="first",
         ),
         axis=1,
     )
@@ -1274,7 +1297,8 @@
         [attention_in_grad, query_out_grad, down_out_grad, entry_grad, out_in_grad, out_out_grad],
         key_out_grad,
         value_out_grad,
-        (d_first_sum,),
+        (mover.marks.get("first_away"),),
+        (mover.marks.get("first"),),
     )
 
     def back(values, shape):

time: 932 us -> 1010 us (1.084)
  waiting for transfers between devices: 272 us -> 336 us
  other arithmetic: 89 us -> 106 us
    ppermute x24 -> x29, waiting for transfers between devices: 84.1 us -> 118 us  [the longest x4 34.2 us: across_parts(): parts = [lax.ppermute(after(v, *deps), 'wsh', X_SWAP) for v in parts]]
    ppermute x9, waiting for transfers between devices: 47.4 us -> 76.6 us  [near(): return jnp.concatenate([pair, lax.ppermute(pair, 'wsh', NEAR_SWAP)], axis=0)]
    ppermute x9, waiting for transfers between devices: 73.9 us -> 96.5 us  [far(): lax.ppermute(chunk, 'wsh', FAR_SWAP)]
    ppermute x2 -> x1, waiting for transfers between devices: 16.9 us -> 0.01 us  [gather_tokens(): return self.gather_rest(values, lax.ppermute(values, 'seq', Y_SWAP))]
    ppermute x24 -> x29, starting transfers between devices: 20.2 us -> 30.6 us  [the longest x6 8.51 us: sum_start(): total = total + lax.ppermute(out, 'wsh', z_shift(r)).astype(F32)]
    ppermute x8 -> x6, waiting for transfers between devices: 29.4 us -> 19 us  [across(): return (four, lax.ppermute(four, 'wsh', X_SWAP))]
    unnamed x351 -> x358, local copies, waits for them, and re-layouts: 82.5 us -> 83.5 us
  transfers between devices with their start and end apart: 73 -> 75, of which waited for: 34 -> 33; matrix products, arithmetic and copies ran while one was open for 29% -> 27% of each run, Pallas kernels for 22% -> 18%
where the time goes in v3:
time: 1010 us; the launch traced here: 1000 us
  waiting for transfers between devices  336 us (33%)
  Pallas kernels  239 us (24%)
  local copies, waits for them, and re-layouts  160 us (16%)
  other arithmetic  106 us (10%)
  matrix products  81.8 us (8%)
  starting transfers between devices  76.9 us (8%)
    pallas_call x5, Pallas kernels, mlp_call(): pl.pallas_call(lambda *refs: mlp_body(owners, sums is not None, *refs), g...  96.9 us
    ppermute x9, waiting for transfers between devices, far(): lax.ppermute(chunk, 'wsh', FAR_SWAP)  96.5 us
    unnamed x358, local copies, waits for them, and re-layouts  83.5 us
    ppermute x9, waiting for transfers between devices, near(): return jnp.concatenate([pair, lax.ppermute(pair, 'wsh', NEAR_SWAP)], axis=0)  76.6 us
    dot_general x20, matrix products, low_dot(): return jnp.dot(left, right, preferred_element_type=F32)  49.3 us
    pallas_call x2, Pallas kernels, attention_call(): pl.pallas_call(forward_body, grid_spec=pltpu.PrefetchScalarGridSpec(num_s...  45.8 us
    pallas_call x2, Pallas kernels, attention_back_call(): pl.pallas_call(backward_body, grid_spec=pltpu.PrefetchScalarGridSpec(num_...  36.6 us
    pallas_call x9, Pallas kernels, final_call(): pl.pallas_call(final_body, grid_spec=pltpu.PrefetchScalarGridSpec(num_sca...  34.6 us
  transfers between devices with their start and end apart: 75, of which 33 were waited for; matrix products, arithmetic and copies ran while one was open for 27% of the time, Pallas kernels for 18%

profile of v3, /device:TPU:0, one launch (start us, length us, event | category | flops | bytes accessed | tf_op | source)
XLA Modules:
  0.0 1003.0 jit_solution(1889604645618138220)
XLA Ops:
  43.9 17.3 %collective-permute-done = bf16[256,2176]{1,0:T(8,128)(2,1)} collective-permute-done((bf16[256,2176]{1,0:T(8,128)(2,1)}, bf16[256,2176]{1,0:T(8,128)(2,1)}, u32[]{:S(2)}, u32[]{:S(2)}) %collective-permute-start) | collective-permute-done | bytes 1114144 | tf_op jit(solution)/shard_map/ppermute | solution.py:1031
  72.5 20.8 %collective-permute-done.11 = bf16[256,1024]{1,0:T(8,128)(2,1)S(1)} collective-permute-done((bf16[256,1024]{1,0:T(8,128)(2,1)S(1)}, bf16[256,1024]{1,0:T(8,128)(2,1)S(1)}, u32[]{:S(2)}, u32[]{:S(2)}) %collective-permute-start.11) | collective-permute-done | bytes 524320 | tf_op jit(solution)/shard_map/ppermute | solution.py:125
  112.7 18.0 %collective-permute-done.14 = bf16[512,1024]{1,0:T(8,128)(2,1)} collective-permute-done((bf16[512,1024]{1,0:T(8,128)(2,1)}, bf16[512,1024]{1,0:T(8,128)(2,1)}, u32[]{:S(2)}, u32[]{:S(2)}) %collective-permute-start.14) | collective-permute-done | bytes 1048608 | tf_op jit(solution)/shard_map/ppermute | solution.py:131
  158.2 22.8 %attention.2 = (bf16[1024,256]{1,0:T(8,128)(2,1)}, f32[1024,128]{1,0:T(8,128)}) custom-call(s32[4]{0:T(128)} %and_select_fusion.4.first_ref, bf16[1024,512]{1,0:T(8,128)(2,1)} %get-tuple-element.122.q_ref, bf16[1024,256]{1,0:T(8,128)(2,1)} %get-tuple-element.113.k_ref, bf16[1024,256]{1,0:T(8,128)(2,1)} %get-tuple-element.114.v_ref, ...), custom_call_target="tpu_custom_call" | custom-call | flops 2147483648 | bytes 3145728 | tf_op jit(solution)/shard_map/attention/pallas_call | solution.py:521
  187.8 16.7 %collective-permute-done.15 = bf16[512,1024]{1,0:T(8,128)(2,1)S(1)} collective-permute-done((bf16[512,1024]{1,0:T(8,128)(2,1)}, bf16[512,1024]{1,0:T(8,128)(2,1)S(1)}, u32[]{:S(2)}, u32[]{:S(2)}) %collective-permute-start.15) | collective-permute-done | bytes 1048608 | tf_op jit(solution)/shard_map/ppermute | solution.py:131
  208.9 23.1 %attention.3 = (bf16[1024,256]{1,0:T(8,128)(2,1)}, f32[1024,128]{1,0:T(8,128)}) custom-call(s32[4]{0:T(128)} %and_select_fusion.4.first_ref, bf16[1024,512]{1,0:T(8,128)(2,1)} %get-tuple-element.122.q_ref, bf16[1024,256]{1,0:T(8,128)(2,1)} %get-tuple-element.113.k_ref, bf16[1024,256]{1,0:T(8,128)(2,1)} %get-tuple-element.114.v_ref, ...), custom_call_target="tpu_custom_call" | custom-call | flops 2147483648 | bytes 3145728 | tf_op jit(solution)/shard_map/attention/pallas_call | solution.py:521
  250.5 25.1 %collective-permute-done.18 = bf16[256,1024]{1,0:T(8,128)(2,1)} collective-permute-done((bf16[256,1024]{1,0:T(8,128)(2,1)}, bf16[256,1024]{1,0:T(8,128)(2,1)}, u32[]{:S(2)}, u32[]{:S(2)}) %collective-permute-start.18) | collective-permute-done | bytes 524320 | tf_op jit(solution)/shard_map/ppermute | solution.py:125
  320.2 16.4 %collective-permute-done.21 = bf16[512,1024]{1,0:T(8,128)(2,1)} collective-permute-done((bf16[512,1024]{1,0:T(8,128)(2,1)}, bf16[512,1024]{1,0:T(8,128)(2,1)}, u32[]{:S(2)}, u32[]{:S(2)}) %collective-permute-start.21) | collective-permute-done | bytes 1048608 | tf_op jit(solution)/shard_map/ppermute | solution.py:142
  362.9 16.2 %collective-permute-done.26 = bf16[256,1024]{1,0:T(8,128)(2,1)S(1)} collective-permute-done((bf16[256,1024]{1,0:T(8,128)(2,1)S(1)}, bf16[256,1024]{1,0:T(8,128)(2,1)S(1)}, u32[]{:S(2)}, u32[]{:S(2)}) %collective-permute-start.26) | collective-permute-done | bytes 524320 | tf_op jit(solution)/shard_map/ppermute | solution.py:125
  379.2 17.7 %collective-permute-done.24 = bf16[512,1024]{1,0:T(8,128)(2,1)S(1)} collective-permute-done((bf16[512,1024]{1,0:T(8,128)(2,1)S(1)}, bf16[512,1024]{1,0:T(8,128)(2,1)S(1)}, u32[]{:S(2)}, u32[]{:S(2)}) %collective-permute-start.24) | collective-permute-done | bytes 1048608 | tf_op jit(solution)/shard_map/ppermute | solution.py:142
  416.9 24.0 %collective-permute-done.29 = bf16[256,1024]{1,0:T(8,128)(2,1)S(1)} collective-permute-done((bf16[256,1024]{1,0:T(8,128)(2,1)S(1)}, bf16[256,1024]{1,0:T(8,128)(2,1)S(1)}, u32[]{:S(2)}, u32[]{:S(2)}) %collective-permute-start.29) | collective-permute-done | bytes 524320 | tf_op jit(solution)/shard_map/ppermute | solution.py:125
  449.9 19.9 %units.5 = (bf16[1024,512]{1,0:T(8,128)(2,1)}, bf16[1024,512]{1,0:T(8,128)(2,1)}, bf16[1024,512]{1,0:T(8,128)(2,1)}, f32[1024,2048]{1,0:T(8,128)}, f32[1024,256]{1,0:T(8,128)}) custom-call(s32[2]{0:T(128)} %pad_add_fusion.refs_0_, bf16[1024,2176]{1,0:T(8,128)(2,1)} %bitcast.391, bf16[1024,1024]{1,0:T(8,128)(2,1)} %constant_dynamic-update-slice_fusion.19.refs_2_, ...), custom_call_target="tpu_custom_call" | custom-call | flops 10737418240 | bytes 33554432 | tf_op jit(solution)/shard_map/units/pallas_call | solution.py:770
  481.4 20.0 %collective-permute-done.31 = bf16[512,1024]{1,0:T(8,128)(2,1)S(1)} collective-permute-done((bf16[512,1024]{1,0:T(8,128)(2,1)S(1)}, bf16[512,1024]{1,0:T(8,128)(2,1)S(1)}, u32[]{:S(2)}, u32[]{:S(2)}) %collective-permute-start.31) | collective-permute-done | bytes 1048608 | tf_op jit(solution)/shard_map/ppermute | solution.py:131
  504.7 21.4 %units.6 = (bf16[1024,512]{1,0:T(8,128)(2,1)}, bf16[1024,512]{1,0:T(8,128)(2,1)}, bf16[1024,512]{1,0:T(8,128)(2,1)}, f32[1024,2048]{1,0:T(8,128)}, f32[1024,256]{1,0:T(8,128)}) custom-call(s32[2]{0:T(128)} %pad_add_fusion.1.refs_0_, bf16[1024,2176]{1,0:T(8,128)(2,1)} %bitcast.392, ...), custom_call_target="tpu_custom_call", output_to_operand_aliasing={{3}: (15, {}), {4}: (16, {})} | custom-call | flops 10737418240 | bytes 33554432 | tf_op jit(solution)/shard_map/units/pallas_call | solution.py:770
  531.6 10.3 %collective-permute-done.35 = bf16[256,512]{1,0:T(8,128)(2,1)S(1)} collective-permute-done((bf16[256,512]{1,0:T(8,128)(2,1)S(1)}, bf16[256,512]{1,0:T(8,128)(2,1)S(1)}, u32[]{:S(2)}, u32[]{:S(2)}) %collective-permute-start.35) | collective-permute-done | bytes 262176 | tf_op jit(solution)/shard_map/ppermute | solution.py:125
  549.1 21.4 %units.7 = (bf16[1024,512]{1,0:T(8,128)(2,1)}, bf16[1024,512]{1,0:T(8,128)(2,1)}, bf16[1024,512]{1,0:T(8,128)(2,1)}, f32[1024,2048]{1,0:T(8,128)}, f32[1024,256]{1,0:T(8,128)}) custom-call(s32[2]{0:T(128)} %pad_add_fusion.2.refs_0_, bf16[1024,2176]{1,0:T(8,128)(2,1)} %bitcast.393, ...), custom_call_target="tpu_custom_call", output_to_operand_aliasing={{3}: (15, {}), {4}: (16, {})} | custom-call | flops 10737418240 | bytes 33554432 | tf_op jit(solution)/shard_map/units/pallas_call | solution.py:770
  596.8 17.1 %units.8 = (bf16[1024,256]{1,0:T(8,128)(2,1)}, bf16[1024,256]{1,0:T(8,128)(2,1)}, bf16[1024,256]{1,0:T(8,128)(2,1)}, f32[1024,2048]{1,0:T(8,128)}, f32[1024,256]{1,0:T(8,128)}) custom-call(s32[2]{0:T(128)} %pad_add_fusion.3.refs_0_, bf16[1024,2176]{1,0:T(8,128)(2,1)} %bitcast.394, ...), custom_call_target="tpu_custom_call", output_to_operand_aliasing={{3}: (15, {}), {4}: (16, {})} | custom-call | flops 5368709120 | bytes 33554432 | tf_op jit(solution)/shard_map/units/pallas_call | solution.py:770
  616.2 17.1 %units.9 = (bf16[1024,256]{1,0:T(8,128)(2,1)}, bf16[1024,256]{1,0:T(8,128)(2,1)}, bf16[1024,256]{1,0:T(8,128)(2,1)}, f32[1024,2048]{1,0:T(8,128)}, f32[1024,256]{1,0:T(8,128)}) custom-call(s32[2]{0:T(128)} %pad_add_fusion.3.refs_0_, bf16[1024,2176]{1,0:T(8,128)(2,1)} %bitcast.395, ...), custom_call_target="tpu_custom_call", output_to_operand_aliasing={{3}: (15, {}), {4}: (16, {})} | custom-call | flops 5368709120 | bytes 33554432 | tf_op jit(solution)/shard_map/units/pallas_call | solution.py:770
  658.8 15.8 %units_out.1 = f32[1024,2048]{1,0:T(8,128)} custom-call(s32[5]{0:T(128)} %stack.190.refs_0_, bf16[1024,512]{1,0:T(8,128)(2,1)} %get-tuple-element.146.refs_1_, bf16[1024,512]{1,0:T(8,128)(2,1)} %get-tuple-element.153.refs_2_, bf16[1024,512]{1,0:T(8,128)(2,1)} %get-tuple-element.160.refs_3_, bf16[1024,256]{1,0:T(8,128)(2,1)} %get-tuple-element.165.refs_4_, ...), custom_call_target="tpu_custom_call" | custom-call | flops 8589934592 | bytes 20971520 | tf_op jit(solution)/shard_map/units_out/pallas_call | solution.py:812
  718.7 10.4 %collective-permute-done.49 = bf16[192,512]{1,0:T(8,128)(2,1)S(1)} collective-permute-done((bf16[192,512]{1,0:T(8,128)(2,1)S(1)}, bf16[192,512]{1,0:T(8,128)(2,1)S(1)}, u32[]{:S(2)}, u32[]{:S(2)}) %collective-permute-start.49) | collective-permute-done | bytes 196640 | tf_op jit(solution)/shard_map/ppermute | solution.py:312
  764.3 18.4 %attention_back.2 = (bf16[1024,256]{1,0:T(8,128)(2,1)}, bf16[1024,128]{1,0:T(8,128)(2,1)}, bf16[1024,128]{1,0:T(8,128)(2,1)}) custom-call(s32[4]{0:T(128)} %and_select_fusion.4.first_ref, bf16[1024,512]{1,0:T(8,128)(2,1)} %get-tuple-element.122.q_ref, bf16[1024,256]{1,0:T(8,128)(2,1)} %get-tuple-element.113.k_ref, ...), custom_call_target="tpu_custom_call" | custom-call | flops 5368709120 | bytes 5242880 | tf_op jit(solution)/shard_map/attention_back/pallas_call | solution.py:625
  792.0 18.2 %attention_back.3 = (bf16[1024,256]{1,0:T(8,128)(2,1)}, bf16[1024,128]{1,0:T(8,128)(2,1)}, bf16[1024,128]{1,0:T(8,128)(2,1)}) custom-call(s32[4]{0:T(128)} %and_select_fusion.4.first_ref, bf16[1024,512]{1,0:T(8,128)(2,1)} %get-tuple-element.122.q_ref, bf16[1024,256]{1,0:T(8,128)(2,1)} %get-tuple-element.113.k_ref, ...), custom_call_target="tpu_custom_call" | custom-call | flops 5368709120 | bytes 5242880 | tf_op jit(solution)/shard_map/attention_back/pallas_call | solution.py:625
  932.2 11.2 %finish.9 = f32[2,128,8192]{2,1,0:T(8,128)} custom-call(s32[1]{0:T(128)} %bitcast.111.s_ref, bf16[1536,512]{1,0:T(8,128)(2,1)} %copy-done.20, bf16[1536,512]{1,0:T(8,128)(2,1)} %collective-permute-done.60.core, bf16[1536,512]{1,0:T(8,128)(2,1)} %constant_dynamic-update-slice_fusion.56.other, bf16[1536,512]{1,0:T(8,128)(2,1)} %collective-permute-done.61.last), custom_call_target="tpu_custom_call" | custom-call | tf_op jit(solution)/shard_map/finish/pallas_call | solution.py:348
  953.9 22.5 %collective-permute-done.73.other = bf16[1280,512]{1,0:T(8,128)(2,1)} collective-permute-done((bf16[1280,512]{1,0:T(8,128)(2,1)S(1)}, bf16[1280,512]{1,0:T(8,128)(2,1)}, u32[]{:S(2)}, u32[]{:S(2)}) %collective-permute-start.73) | collective-permute-done | bytes 1310752 | tf_op jit(solution)/shard_map/ppermute | solution.py:324
  (755 shorter events, 557.8 us)
Async XLA Ops:
  3.6 35.9 %collective-permute-start.3 = (bf16[256,768]{1,0:T(8,128)(2,1)}, bf16[256,768]{1,0:T(8,128)(2,1)S(1)}, u32[]{:S(2)}, u32[]{:S(2)}) collective-permute-start(bf16[256,768]{1,0:T(8,128)(2,1)} %pad_maximum_fusion.34), channel_id=1, source_target_pairs={{0,4},{1,5},{2,6},{3,7},{4,0},{5,1},{6,2},{7,3},{8,12},{9,13},{10,... | collective-permute-start | bytes 1179656 | tf_op jit(solution)/shard_map/ppermute | solution.py:125
  65.1 70.0 %collective-permute-start.2 = (bf16[2,256,2176]{2,1,0:T(8,128)(2,1)}, bf16[2,256,2176]{2,1,0:T(8,128)(2,1)}, u32[]{:S(2)}, u32[]{:S(2)}) collective-permute-start(bf16[2,256,2176]{2,1,0:T(8,128)(2,1)} %pad_maximum_fusion.4), channel_id=1, source_target_pairs={{0,8},{8,0},{16,24},{24,16},{1,9},{9,1},{17,25},{25,17},{2,10},{10... | collective-permute-start | bytes 6684680 | tf_op jit(solution)/shard_map/ppermute | solution.py:222
  65.8 36.6 %collective-permute-start.5 = (bf16[1024,768]{1,0:T(8,128)(2,1)S(1)}, bf16[1024,768]{1,0:T(8,128)(2,1)S(1)}, u32[]{:S(2)}, u32[]{:S(2)}) collective-permute-start(bf16[1024,768]{1,0:T(8,128)(2,1)S(1)} %pad_maximum_fusion.13.w_own), channel_id=1, source_target_pairs={{0,1},{1,0},{2,3},{3,2},{4,5},{5,4},{6,7},{7,6},{8,9},{9,8},{10,11... | collective-permute-start | bytes 4718600 | tf_op jit(solution)/shard_map/ppermute | solution.py:137
  95.0 35.8 %collective-permute-start.14 = (bf16[512,1024]{1,0:T(8,128)(2,1)}, bf16[512,1024]{1,0:T(8,128)(2,1)}, u32[]{:S(2)}, u32[]{:S(2)}) collective-permute-start(bf16[512,1024]{1,0:T(8,128)(2,1)} %constant_dynamic-update-slice_fusion.11), channel_id=1, source_target_pairs={{0,2},{1,3},{2,0},{3,1},{4,6},{5,7},{6,4},{7,5},{8,10},{9,11},{10,... | collective-permute-start | bytes 3145736 | tf_op jit(solution)/shard_map/ppermute | solution.py:131
  110.1 75.2 %collective-permute-start.10 = (bf16[256,2048]{1,0:T(8,128)(2,1)}, bf16[256,2048]{1,0:T(8,128)(2,1)}, u32[]{:S(2)}, u32[]{:S(2)}) collective-permute-start(bf16[256,2048]{1,0:T(8,128)(2,1)} %constant_dynamic-update-slice_fusion.9), channel_id=1, source_target_pairs={{0,1},{1,0},{2,3},{3,2},{4,5},{5,4},{6,7},{7,6},{8,9},{9,8},{10,11... | collective-permute-start | bytes 3145736 | tf_op jit(solution)/shard_map/ppermute | solution.py:137
  185.4 47.9 %collective-permute-start.16 = (bf16[512,1024]{1,0:T(8,128)(2,1)}, bf16[512,1024]{1,0:T(8,128)(2,1)}, u32[]{:S(2)}, u32[]{:S(2)}) collective-permute-start(bf16[512,1024]{1,0:T(8,128)(2,1)} %constant_dynamic-update-slice_fusion.11), channel_id=1, source_target_pairs={{0,1},{1,0},{2,3},{3,2},{4,5},{5,4},{6,7},{7,6},{8,9},{9,8},{10,11... | collective-permute-start | bytes 3145736 | tf_op jit(solution)/shard_map/ppermute | solution.py:1093
  245.4 34.9 %collective-permute-start.17 = (bf16[2,256,2176]{2,1,0:T(8,128)(2,1)}, bf16[2,256,2176]{2,1,0:T(8,128)(2,1)}, u32[]{:S(2)}, u32[]{:S(2)}) collective-permute-start(bf16[2,256,2176]{2,1,0:T(8,128)(2,1)} %pad_maximum_fusion.5), channel_id=1, source_target_pairs={{0,8},{8,0},{16,24},{24,16},{1,9},{9,1},{17,25},{25,17},{2,10},{10... | collective-permute-start | bytes 6684680 | tf_op jit(solution)/shard_map/ppermute | solution.py:238
  289.5 47.1 %collective-permute-start.21 = (bf16[512,1024]{1,0:T(8,128)(2,1)}, bf16[512,1024]{1,0:T(8,128)(2,1)}, u32[]{:S(2)}, u32[]{:S(2)}) collective-permute-start(bf16[512,1024]{1,0:T(8,128)(2,1)} %copy-done.52), channel_id=1, source_target_pairs={{0,1},{1,0},{2,3},{3,2},{4,5},{5,4},{6,7},{7,6},{8,9},{9,8},{10,11... | collective-permute-start | bytes 3145736 | tf_op jit(solution)/shard_map/ppermute | solution.py:142
  347.2 49.8 %collective-permute-start.23 = (bf16[256,2176]{1,0:T(8,128)(2,1)}, bf16[256,2176]{1,0:T(8,128)(2,1)S(1)}, u32[]{:S(2)}, u32[]{:S(2)}) collective-permute-start(bf16[256,2176]{1,0:T(8,128)(2,1)} %fusion.81), channel_id=1, source_target_pairs={{0,16},{8,24},{16,0},{24,8},{1,17},{9,25},{17,1},{25,9},{2,18},{10... | collective-permute-start | bytes 3342344 | tf_op jit(solution)/shard_map/ppermute | solution.py:1134
  350.7 46.2 %collective-permute-start.25 = (bf16[512,1024]{1,0:T(8,128)(2,1)}, bf16[512,1024]{1,0:T(8,128)(2,1)S(1)}, u32[]{:S(2)}, u32[]{:S(2)}) collective-permute-start(bf16[512,1024]{1,0:T(8,128)(2,1)} %pad_maximum_fusion.19), channel_id=1, source_target_pairs={{0,1},{1,0},{2,3},{3,2},{4,5},{5,4},{6,7},{7,6},{8,9},{9,8},{10,11... | collective-permute-start | bytes 3145736 | tf_op jit(solution)/shard_map/ppermute | solution.py:142
  351.3 45.7 %collective-permute-start.24 = (bf16[512,1024]{1,0:T(8,128)(2,1)S(1)}, bf16[512,1024]{1,0:T(8,128)(2,1)S(1)}, u32[]{:S(2)}, u32[]{:S(2)}) collective-permute-start(bf16[512,1024]{1,0:T(8,128)(2,1)S(1)} %copy-done.81), channel_id=1, source_target_pairs={{0,1},{1,0},{2,3},{3,2},{4,5},{5,4},{6,7},{7,6},{8,9},{9,8},{10,11... | collective-permute-start | bytes 3145736 | tf_op jit(solution)/shard_map/ppermute | solution.py:142
  398.6 46.5 %collective-permute-start.27 = (bf16[2,256,2176]{2,1,0:T(8,128)(2,1)S(1)}, bf16[2,256,2176]{2,1,0:T(8,128)(2,1)S(1)}, u32[]{:S(2)}, u32[]{:S(2)}) collective-permute-start(bf16[2,256,2176]{2,1,0:T(8,128)(2,1)S(1)} %pad_maximum_fusion.6), channel_id=1, source_target_pairs={{0,8},{8,0},{16,24},{24,16},{1,9},{9,1},{17,25},{25,17},{2,10},{10... | collective-permute-start | bytes 6684680 | tf_op jit(solution)/shard_map/ppermute | solution.py:222
  405.1 36.9 %collective-permute-start.28 = (bf16[512,1024]{1,0:T(8,128)(2,1)S(1)}, bf16[512,1024]{1,0:T(8,128)(2,1)S(1)}, u32[]{:S(2)}, u32[]{:S(2)}) collective-permute-start(bf16[512,1024]{1,0:T(8,128)(2,1)S(1)} %pad_maximum_fusion.20), channel_id=1, source_target_pairs={{0,2},{1,3},{2,0},{3,1},{4,6},{5,7},{6,4},{7,5},{8,10},{9,11},{10,... | collective-permute-start | bytes 3145736 | tf_op jit(solution)/shard_map/ppermute | solution.py:131
  407.6 35.9 %collective-permute-start.30 = (bf16[512,1024]{1,0:T(8,128)(2,1)}, bf16[512,1024]{1,0:T(8,128)(2,1)S(1)}, u32[]{:S(2)}, u32[]{:S(2)}) collective-permute-start(bf16[512,1024]{1,0:T(8,128)(2,1)} %collective-permute-done.22), channel_id=1, source_target_pairs={{0,1},{1,0},{2,3},{3,2},{4,5},{5,4},{6,7},{7,6},{8,9},{9,8},{10,11... | collective-permute-start | bytes 3145736 | tf_op jit(solution)/shard_map/ppermute | solution.py:142
  409.3 31.7 %collective-permute-start.29 = (bf16[256,1024]{1,0:T(8,128)(2,1)S(1)}, bf16[256,1024]{1,0:T(8,128)(2,1)S(1)}, u32[]{:S(2)}, u32[]{:S(2)}) collective-permute-start(bf16[256,1024]{1,0:T(8,128)(2,1)S(1)} %pad_maximum_fusion.31), channel_id=1, source_target_pairs={{0,4},{1,5},{2,6},{3,7},{4,0},{5,1},{6,2},{7,3},{8,12},{9,13},{10,... | collective-permute-start | bytes 1572872 | tf_op jit(solution)/shard_map/ppermute | solution.py:125
  443.0 61.6 %collective-permute-start.33 = (bf16[1024,1024]{1,0:T(8,128)(2,1)}, bf16[1024,1024]{1,0:T(8,128)(2,1)}, u32[]{:S(2)}, u32[]{:S(2)}) collective-permute-start(bf16[1024,1024]{1,0:T(8,128)(2,1)} %constant_dynamic-update-slice_fusion.29.refs_2_), channel_id=1, source_target_pairs={{0,1},{1,0},{2,3},{3,2},{4,5},{5,4},{6,7},{7,6},{8,9},{9,8},{10,11... | collective-permute-start | bytes 6291464 | tf_op jit(solution)/shard_map/ppermute | solution.py:137
  469.8 31.6 %collective-permute-start.31 = (bf16[512,1024]{1,0:T(8,128)(2,1)S(1)}, bf16[512,1024]{1,0:T(8,128)(2,1)S(1)}, u32[]{:S(2)}, u32[]{:S(2)}) collective-permute-start(bf16[512,1024]{1,0:T(8,128)(2,1)S(1)} %pad_maximum_fusion.21), channel_id=1, source_target_pairs={{0,2},{1,3},{2,0},{3,1},{4,6},{5,7},{6,4},{7,5},{8,10},{9,11},{10,... | collective-permute-start | bytes 3145736 | tf_op jit(solution)/shard_map/ppermute | solution.py:131
  502.4 46.6 %collective-permute-start.36 = (bf16[1024,1024]{1,0:T(8,128)(2,1)}, bf16[1024,1024]{1,0:T(8,128)(2,1)}, u32[]{:S(2)}, u32[]{:S(2)}) collective-permute-start(bf16[1024,1024]{1,0:T(8,128)(2,1)} %constant_dynamic-update-slice_fusion.35.refs_2_), channel_id=1, source_target_pairs={{0,1},{1,0},{2,3},{3,2},{4,5},{5,4},{6,7},{7,6},{8,9},{9,8},{10,11... | collective-permute-start | bytes 6291464 | tf_op jit(solution)/shard_map/ppermute | solution.py:137
  583.2 33.1 %collective-permute-start.39 = (bf16[1024,512]{1,0:T(8,128)(2,1)}, bf16[1024,512]{1,0:T(8,128)(2,1)}, u32[]{:S(2)}, u32[]{:S(2)}) collective-permute-start(bf16[1024,512]{1,0:T(8,128)(2,1)} %constant_dynamic-update-slice_fusion.39.refs_2_), channel_id=1, source_target_pairs={{0,1},{1,0},{2,3},{3,2},{4,5},{5,4},{6,7},{7,6},{8,9},{9,8},{10,11... | collective-permute-start | bytes 3145736 | tf_op jit(solution)/shard_map/ppermute | solution.py:137
  650.7 39.2 %collective-permute-start.42 = (bf16[256,2176]{1,0:T(8,128)(2,1)}, bf16[256,2176]{1,0:T(8,128)(2,1)}, u32[]{:S(2)}, u32[]{:S(2)}) collective-permute-start(bf16[256,2176]{1,0:T(8,128)(2,1)} %fusion.88), channel_id=1, source_target_pairs={{0,16},{8,24},{16,0},{24,8},{1,17},{9,25},{17,1},{25,9},{2,18},{10... | collective-permute-start | bytes 3342344 | tf_op jit(solution)/shard_map/ppermute | solution.py:241
  844.0 38.8 %collective-permute-start.55 = (bf16[2,256,2048]{2,1,0:T(8,128)(2,1)}, bf16[2,256,2048]{2,1,0:T(8,128)(2,1)}, u32[]{:S(2)}, u32[]{:S(2)}) collective-permute-start(bf16[2,256,2048]{2,1,0:T(8,128)(2,1)} %pad_maximum_fusion.12), channel_id=1, source_target_pairs={{0,8},{8,0},{16,24},{24,16},{1,9},{9,1},{17,25},{25,17},{2,10},{10... | collective-permute-start | bytes 6291464 | tf_op jit(solution)/shard_map/ppermute | solution.py:238
  870.5 55.3 %collective-permute-start.60 = (bf16[1536,512]{1,0:T(8,128)(2,1)S(1)}, bf16[1536,512]{1,0:T(8,128)(2,1)}, u32[]{:S(2)}, u32[]{:S(2)}) collective-permute-start(bf16[1536,512]{1,0:T(8,128)(2,1)S(1)} %pad_maximum_fusion.15.own), channel_id=1, source_target_pairs={{0,8},{8,0},{16,24},{24,16},{1,9},{9,1},{17,25},{25,17},{2,10},{10... | collective-permute-start | bytes 4718600 | tf_op jit(solution)/shard_map/ppermute | solution.py:322
  892.9 32.9 %collective-permute-start.61 = (bf16[1536,512]{1,0:T(8,128)(2,1)}, bf16[1536,512]{1,0:T(8,128)(2,1)}, u32[]{:S(2)}, u32[]{:S(2)}) collective-permute-start(bf16[1536,512]{1,0:T(8,128)(2,1)} %constant_dynamic-update-slice_fusion.56.other), channel_id=1, source_target_pairs={{0,8},{8,0},{16,24},{24,16},{1,9},{9,1},{17,25},{25,17},{2,10},{10... | collective-permute-start | bytes 4718600 | tf_op jit(solution)/shard_map/ppermute | solution.py:330
  945.0 40.7 %collective-permute-start.72 = (bf16[1280,512]{1,0:T(8,128)(2,1)S(1)}, bf16[1280,512]{1,0:T(8,128)(2,1)}, u32[]{:S(2)}, u32[]{:S(2)}) collective-permute-start(bf16[1280,512]{1,0:T(8,128)(2,1)S(1)} %pad_maximum_fusion.16.own), channel_id=1, source_target_pairs={{0,8},{8,0},{16,24},{24,16},{1,9},{9,1},{17,25},{25,17},{2,10},{10... | collective-permute-start | bytes 3932168 | tf_op jit(solution)/shard_map/ppermute | solution.py:322
  (199 other events, 2303.1 us)

commit v4 on v3

--- a/solution.py
+++ b/solution.py
@@ -135,12 +135,6 @@
         if not self.fast:
             return (lax.all_gather(four, "wsh", axis=0, tiled=True),)
         return four, lax.ppermute(four, "wsh", X_SWAP)
-
-    def across_parts(self, four, *deps):
-        rows = four.shape[0] // 2
-        parts = [four[:rows], four[rows:]]
-        parts = [lax.ppermute(after(v, *deps), "wsh", X_SWAP) for v in parts]
-        return (four, jnp.concatenate(parts, axis=0)), parts
 
     def swap_bits(self, d):
         return d // 2 + 2 * (d % 2)
@@ -277,7 +271,7 @@
             final_hidden(parts, s, 8 * LANES, 1)[0],
         ]
 
-    def sum_features(self, grads, key=None, value=None, mid=(), deps=()):
+    def sum_features(self, grads, key=None, value=None, mid=(), deps=(), late=(), mark=None):
         if not self.fast:
             grads = grads + ([key, value] if key is not None else [])
             found = []
@@ -288,7 +282,9 @@
         if key is not None:
             rest = jnp.zeros((key.shape[0], PACK - 2 * LANES), F32)
             packed.append(jnp.concatenate([key, value, rest], axis=1))
-        parts = self.sum_end(self.sum_start(jnp.concatenate(packed, axis=0), mid), deps)
+        half = self.sum_start(jnp.concatenate(packed, axis=0), mid)
+        parts = self.sum_end(half, deps, late=late)
+        self.marks[mark] = parts[2]
         s = self.s.astype(jnp.int32)[None]
         found, at = [], 0
         for grad in grads:
@@ -313,7 +309,7 @@
         ring = jnp.stack(got)
         return jnp.concatenate([pick(ring, (self.z - j) % 4, 0) for j in range(4)], axis=0)
 
-    def sum_end(self, half, deps=(), mark=None, early=()):
+    def sum_end(self, half, deps=(), mark=None, early=(), late=()):
         rows = 2 * half.shape[0]
         half = after(half, *early)
         other = lax.ppermute(half, "wsh", X_SWAP)
@@ -321,7 +317,7 @@
         part = jnp.concatenate([jnp.where(first, half, other), jnp.where(first, other, half)])
         core = lax.ppermute(part, "seq", CORE_SWAP)
         if mark is None:
-            other = lax.ppermute(after(part, *deps), "seq", Y_SWAP)
+            other = after(lax.ppermute(after(part, *deps), "seq", Y_SWAP), *late)
         else:
             top = lax.ppermute(after(part[: rows // 2], *deps), "seq", Y_SWAP)
             rest = lax.ppermute(after(part[rows // 2 :], top), "seq", Y_SWAP)
@@ -1041,6 +1037,7 @@
         d_mlp = mover.gather_rest(d_mlp_local, after(d_mlp_other, first_all))
         low_four = mover.near(low_pair, out_four)
         high_pair = mover.far(down_local[:, half_width:], low_pair, qkv_full[1])
+        first_all = after(first_all, d_mlp)
     else:
         qkv_full = mover.across(qkv_pair)
         first_all = mover.gather_tokens(first_cols)
@@ -1095,13 +1092,11 @@
         ]
         down_low = (low_four, jnp.concatenate(low_other, axis=0))
         high_four = mover.near(high_pair, low_four, early)
-        attended = attend_rest(out_full, high_pair, d_mlp)
-        chunk_pairs = [gate_up_far(0, high_pair, early)]
+        attended = attend_rest(out_full, high_pair)
+        chunk_pairs = [gate_up_far(0, high_four)]
         attended = after(attended, high_four, low_other[0])
-        down_high, high_parts = mover.across_parts(high_four)
+        down_high = mover.across(high_four)
         chunk_fours = [mover.near(chunk_pairs[0], high_four)]
-        chunk_weights, chunk_parts = mover.across_parts(chunk_fours[0])
-        chunk_weights = [chunk_weights]
         chunk_pairs.append(gate_up_far(1, chunk_pairs[0]))
     else:
         attended = attend_rest()
@@ -1109,16 +1104,14 @@
     out_entry = cut(turned(output_entry_maps), s * q_cols, q_cols, 1)
     out_exit = output_exit_maps.reshape(flat, -1)
     la_out_part = fold(reverse_product(attended, out_entry) * mask_rank, rank, 0)
-    attn_sum = mover.scatter_tokens(
-        low_dot(attended, out_full), la_out_part, deps=chunk_pairs[:1] if mover.fast else ()
-    )
+    attn_sum = mover.scatter_tokens(low_dot(attended, out_full), la_out_part)
     la_out_own = attn_sum[1].astype(BF)
     attention_path = attn_sum[0] + low_dot(
         spread(la_out_own, own_owner, rank, 0, adapters), out_exit
     )
     middle = hidden_state + RESIDUAL_MULT * attention_path
     if mover.fast:
-        middle = after(middle, low_other[1], high_parts[0], chunk_fours[0])
+        middle = after(middle, low_other[1], chunk_pairs[0])
 
     second_normed, scale_two = normed(middle, feedforward_norm_gain)
     second_normed = second_normed.astype(BF)
@@ -1133,7 +1126,7 @@
     if mover.fast:
         second_other = lax.ppermute(second_cols, "seq", Y_SWAP)
         second_all = mover.gather_rest(
-            second_cols, after(second_other, high_parts[1], chunk_parts[0], chunk_pairs[1])
+            second_cols, after(second_other, down_high[1], chunk_fours[0], chunk_pairs[1])
         )
     else:
         second_all = mover.gather_tokens(second_cols)
@@ -1148,6 +1141,7 @@
     exits = [jnp.concatenate(own_hidden(all_exits[i]), axis=1) for i in range(2)]
     units_found = []
     if mover.fast:
+        chunk_weights = [mover.across(chunk_fours[0])]
         sums = None
         for i, units in enumerate(chunks):
             if i + 1 < len(chunks):
@@ -1293,12 +1287,19 @@
     query_out_grad = gradient_product(la_q, d_query)
     key_out_grad = gradient_product(la_k, d_key)
     value_out_grad = gradient_product(la_v, d_value)
-    last_grads = mover.sum_features(
-        [attention_in_grad, query_out_grad, down_out_grad, entry_grad, out_in_grad, out_out_grad],
+    first_sent = mover.marks.get("first")
+    early_grads = mover.sum_features(
+        [query_out_grad, down_out_grad, entry_grad, out_in_grad, out_out_grad],
         key_out_grad,
         value_out_grad,
-        (mover.marks.get("first_away"),),
-        (mover.marks.get("first"),),
+        deps=(first_sent,),
+        mark="features",
+    )
+    (last_grad,) = mover.sum_features(
+        [attention_in_grad],
+        mid=(mover.marks.get("first_away"),),
+        deps=(mover.marks.get("features"),),
+        late=early_grads,
     )
 
     def back(values, shape):
@@ -1307,15 +1308,15 @@
     return (
         layer_out,
         hidden_gradient[None],
-        back(last_grads[0], attention_down_maps.shape),
-        last_grads[1].reshape(query_exit_maps.shape),
-        last_grads[6].reshape(key_value_exit_maps.shape),
-        back(last_grads[4], output_entry_maps.shape),
-        last_grads[5].reshape(output_exit_maps.shape),
-        back(last_grads[3], feedforward_entry_maps.shape),
+        back(last_grad, attention_down_maps.shape),
+        early_grads[0].reshape(query_exit_maps.shape),
+        early_grads[5].reshape(key_value_exit_maps.shape),
+        back(early_grads[3], output_entry_maps.shape),
+        early_grads[4].reshape(output_exit_maps.shape),
+        back(early_grads[2], feedforward_entry_maps.shape),
         hidden_grads[0].reshape(feedforward_exit_maps.shape),
         back(hidden_grads[1], down_entry_maps.shape),
-        last_grads[2].reshape(down_exit_maps.shape),
+        early_grads[1].reshape(down_exit_maps.shape),
     )
 
 

time: 1010 us -> 942 us (0.933)
  waiting for transfers between devices: 336 us -> 257 us
    ppermute x9, waiting for transfers between devices: 96.5 us -> 51.8 us  [far(): lax.ppermute(chunk, 'wsh', FAR_SWAP)]
    ppermute x5 -> x2, waiting for transfers between devices: 56.7 us -> 18.3 us  [sum_end(): other = after(lax.ppermute(after(part, *deps), 'seq', Y_SWAP), *late)]
    ppermute x9, waiting for transfers between devices: 76.6 us -> 98.5 us  [near(): return jnp.concatenate([pair, lax.ppermute(pair, 'wsh', NEAR_SWAP)], axis=0)]
    ppermute x6 -> x8, waiting for transfers between devices: 19 us -> 32.4 us  [across(): return (four, lax.ppermute(four, 'wsh', X_SWAP))]
    unnamed x358 -> x371, local copies, waits for them, and re-layouts: 83.5 us -> 75.3 us
    ppermute x6 -> x9, waiting for transfers between devices: 22.5 us -> 15.4 us  [sum_start(): got = [own] + [lax.ppermute(own, 'wsh', z_shift(r)) for r in range(1, 4)]]
  transfers between devices with their start and end apart: 75 -> 84, of which waited for: 33 -> 34; matrix products, arithmetic and copies ran while one was open for 27% -> 28% of each run, Pallas kernels for 18% -> 18%
where the time goes in v4:
time: 942 us; the launch traced here: 930 us
  waiting for transfers between devices  257 us (27%)
  Pallas kernels  239 us (25%)
  local copies, waits for them, and re-layouts  151 us (16%)
  other arithmetic  114 us (12%)
  matrix products  85 us (9%)
  starting transfers between devices  81.9 us (9%)
    ppermute x9, waiting for transfers between devices, near(): return jnp.concatenate([pair, lax.ppermute(pair, 'wsh', NEAR_SWAP)], axis=0)  98.5 us
    pallas_call x5, Pallas kernels, mlp_call(): pl.pallas_call(lambda *refs: mlp_body(owners, sums is not None, *refs), g...  96.8 us
    unnamed x371, local copies, waits for them, and re-layouts  75.3 us
    ppermute x9, waiting for transfers between devices, far(): lax.ppermute(chunk, 'wsh', FAR_SWAP)  51.8 us
    dot_general x20, matrix products, low_dot(): return jnp.dot(left, right, preferred_element_type=F32)  48.6 us
    pallas_call x2, Pallas kernels, attention_call(): pl.pallas_call(forward_body, grid_spec=pltpu.PrefetchScalarGridSpec(num_s...  45.6 us
    pallas_call x2, Pallas kernels, attention_back_call(): pl.pallas_call(backward_body, grid_spec=pltpu.PrefetchScalarGridSpec(num_...  36.6 us
    pallas_call x9, Pallas kernels, final_call(): pl.pallas_call(final_body, grid_spec=pltpu.PrefetchScalarGridSpec(num_sca...  34.6 us
  transfers between devices with their start and end apart: 84, of which 34 were waited for; matrix products, arithmetic and copies ran while one was open for 28% of the time, Pallas kernels for 18%

profile of v4, /device:TPU:0, one launch (start us, length us, event | category | flops | bytes accessed | tf_op | source)
XLA Modules:
  0.0 930.3 jit_solution(17697664991750216718)
XLA Ops:
  42.9 18.3 %collective-permute-done = bf16[256,2176]{1,0:T(8,128)(2,1)} collective-permute-done((bf16[256,2176]{1,0:T(8,128)(2,1)}, bf16[256,2176]{1,0:T(8,128)(2,1)}, u32[]{:S(2)}, u32[]{:S(2)}) %collective-permute-start) | collective-permute-done | bytes 1114144 | tf_op jit(solution)/shard_map/ppermute | solution.py:1027
  76.5 17.6 %collective-permute-done.9 = bf16[64,2048]{1,0:T(8,128)(2,1)} collective-permute-done((bf16[64,2048]{1,0:T(8,128)(2,1)}, bf16[64,2048]{1,0:T(8,128)(2,1)}, u32[]{:S(2)}, u32[]{:S(2)}) %collective-permute-start.9) | collective-permute-done | bytes 262176 | tf_op jit(solution)/shard_map/ppermute | solution.py:125
  106.0 10.0 %collective-permute-done.10 = bf16[128,2048]{1,0:T(8,128)(2,1)} collective-permute-done((bf16[128,2048]{1,0:T(8,128)(2,1)}, bf16[128,2048]{1,0:T(8,128)(2,1)}, u32[]{:S(2)}, u32[]{:S(2)}) %collective-permute-start.10) | collective-permute-done | bytes 524320 | tf_op jit(solution)/shard_map/ppermute | solution.py:131
  127.2 26.3 %collective-permute-done.14 = bf16[512,1024]{1,0:T(8,128)(2,1)S(1)} collective-permute-done((bf16[512,1024]{1,0:T(8,128)(2,1)S(1)}, bf16[512,1024]{1,0:T(8,128)(2,1)S(1)}, u32[]{:S(2)}, u32[]{:S(2)}) %collective-permute-start.14) | collective-permute-done | bytes 1048608 | tf_op jit(solution)/shard_map/ppermute | solution.py:131
  169.7 9.2 qkv.1
  178.9 22.8 %attention.2 = (bf16[1024,256]{1,0:T(8,128)(2,1)}, f32[1024,128]{1,0:T(8,128)}) custom-call(s32[4]{0:T(128)} %and_select_fusion.4.first_ref, bf16[1024,512]{1,0:T(8,128)(2,1)} %get-tuple-element.125.q_ref, bf16[1024,256]{1,0:T(8,128)(2,1)} %get-tuple-element.117.k_ref, bf16[1024,256]{1,0:T(8,128)(2,1)} %get-tuple-element.118.v_ref, ...), custom_call_target="tpu_custom_call" | custom-call | flops 2147483648 | bytes 3145728 | tf_op jit(solution)/shard_map/attention/pallas_call | solution.py:517
  209.3 22.9 %attention.3 = (bf16[1024,256]{1,0:T(8,128)(2,1)}, f32[1024,128]{1,0:T(8,128)}) custom-call(s32[4]{0:T(128)} %and_select_fusion.4.first_ref, bf16[1024,512]{1,0:T(8,128)(2,1)} %get-tuple-element.125.q_ref, bf16[1024,256]{1,0:T(8,128)(2,1)} %get-tuple-element.117.k_ref, bf16[1024,256]{1,0:T(8,128)(2,1)} %get-tuple-element.118.v_ref, ...), custom_call_target="tpu_custom_call" | custom-call | flops 2147483648 | bytes 3145728 | tf_op jit(solution)/shard_map/attention/pallas_call | solution.py:517
  264.8 21.6 %collective-permute-done.20 = bf16[256,1024]{1,0:T(8,128)(2,1)} collective-permute-done((bf16[256,1024]{1,0:T(8,128)(2,1)S(1)}, bf16[256,1024]{1,0:T(8,128)(2,1)}, u32[]{:S(2)}, u32[]{:S(2)}) %collective-permute-start.20) | collective-permute-done | bytes 524320 | tf_op jit(solution)/shard_map/ppermute | solution.py:125
  318.6 9.3 collective-permute-done.23
  355.3 26.1 %collective-permute-done.26 = bf16[512,1024]{1,0:T(8,128)(2,1)S(1)} collective-permute-done((bf16[512,1024]{1,0:T(8,128)(2,1)S(1)}, bf16[512,1024]{1,0:T(8,128)(2,1)S(1)}, u32[]{:S(2)}, u32[]{:S(2)}) %collective-permute-start.26) | collective-permute-done | bytes 1048608 | tf_op jit(solution)/shard_map/ppermute | solution.py:131
  387.4 15.3 %collective-permute-done.28.refs_3_ = bf16[1024,1024]{1,0:T(8,128)(2,1)} collective-permute-done((bf16[1024,1024]{1,0:T(8,128)(2,1)S(1)}, bf16[1024,1024]{1,0:T(8,128)(2,1)}, u32[]{:S(2)}, u32[]{:S(2)}) %collective-permute-start.28) | collective-permute-done | bytes 2097184 | tf_op jit(solution)/shard_map/ppermute | solution.py:137
  402.7 19.9 %units.5 = (bf16[1024,512]{1,0:T(8,128)(2,1)}, bf16[1024,512]{1,0:T(8,128)(2,1)}, bf16[1024,512]{1,0:T(8,128)(2,1)}, f32[1024,2048]{1,0:T(8,128)}, f32[1024,256]{1,0:T(8,128)}) custom-call(s32[2]{0:T(128)} %pad_add_fusion.refs_0_, bf16[1024,2176]{1,0:T(8,128)(2,1)} %bitcast.423, bf16[1024,1024]{1,0:T(8,128)(2,1)} %copy-done.96, ...), custom_call_target="tpu_custom_call" | custom-call | flops 10737418240 | bytes 33554432 | tf_op jit(solution)/shard_map/units/pallas_call | solution.py:766
  433.0 17.9 %collective-permute-done.29 = bf16[512,1024]{1,0:T(8,128)(2,1)S(1)} collective-permute-done((bf16[512,1024]{1,0:T(8,128)(2,1)S(1)}, bf16[512,1024]{1,0:T(8,128)(2,1)S(1)}, u32[]{:S(2)}, u32[]{:S(2)}) %collective-permute-start.29) | collective-permute-done | bytes 1048608 | tf_op jit(solution)/shard_map/ppermute | solution.py:131
  453.2 21.4 %units.6 = (bf16[1024,512]{1,0:T(8,128)(2,1)}, bf16[1024,512]{1,0:T(8,128)(2,1)}, bf16[1024,512]{1,0:T(8,128)(2,1)}, f32[1024,2048]{1,0:T(8,128)}, f32[1024,256]{1,0:T(8,128)}) custom-call(s32[2]{0:T(128)} %pad_add_fusion.1.refs_0_, bf16[1024,2176]{1,0:T(8,128)(2,1)} %bitcast.424, ...), custom_call_target="tpu_custom_call", output_to_operand_aliasing={{3}: (15, {}), {4}: (16, {})} | custom-call | flops 10737418240 | bytes 33554432 | tf_op jit(solution)/shard_map/units/pallas_call | solution.py:766
  480.4 8.5 collective-permute-done.33
  496.4 21.3 %units.7 = (bf16[1024,512]{1,0:T(8,128)(2,1)}, bf16[1024,512]{1,0:T(8,128)(2,1)}, bf16[1024,512]{1,0:T(8,128)(2,1)}, f32[1024,2048]{1,0:T(8,128)}, f32[1024,256]{1,0:T(8,128)}) custom-call(s32[2]{0:T(128)} %pad_add_fusion.2.refs_0_, bf16[1024,2176]{1,0:T(8,128)(2,1)} %bitcast.425, ...), custom_call_target="tpu_custom_call", output_to_operand_aliasing={{3}: (15, {}), {4}: (16, {})} | custom-call | flops 10737418240 | bytes 33554432 | tf_op jit(solution)/shard_map/units/pallas_call | solution.py:766
  544.1 17.1 %units.8 = (bf16[1024,256]{1,0:T(8,128)(2,1)}, bf16[1024,256]{1,0:T(8,128)(2,1)}, bf16[1024,256]{1,0:T(8,128)(2,1)}, f32[1024,2048]{1,0:T(8,128)}, f32[1024,256]{1,0:T(8,128)}) custom-call(s32[2]{0:T(128)} %pad_add_fusion.3.refs_0_, bf16[1024,2176]{1,0:T(8,128)(2,1)} %bitcast.426, ...), custom_call_target="tpu_custom_call", output_to_operand_aliasing={{3}: (15, {}), {4}: (16, {})} | custom-call | flops 5368709120 | bytes 33554432 | tf_op jit(solution)/shard_map/units/pallas_call | solution.py:766
  561.4 17.0 %units.9 = (bf16[1024,256]{1,0:T(8,128)(2,1)}, bf16[1024,256]{1,0:T(8,128)(2,1)}, bf16[1024,256]{1,0:T(8,128)(2,1)}, f32[1024,2048]{1,0:T(8,128)}, f32[1024,256]{1,0:T(8,128)}) custom-call(s32[2]{0:T(128)} %pad_add_fusion.3.refs_0_, bf16[1024,2176]{1,0:T(8,128)(2,1)} %bitcast.427, ...), custom_call_target="tpu_custom_call", output_to_operand_aliasing={{3}: (15, {}), {4}: (16, {})} | custom-call | flops 5368709120 | bytes 33554432 | tf_op jit(solution)/shard_map/units/pallas_call | solution.py:766
  604.0 15.8 %units_out.1 = f32[1024,2048]{1,0:T(8,128)} custom-call(s32[5]{0:T(128)} %stack.205.refs_0_, bf16[1024,512]{1,0:T(8,128)(2,1)} %get-tuple-element.148.refs_1_, bf16[1024,512]{1,0:T(8,128)(2,1)} %get-tuple-element.155.refs_2_, bf16[1024,512]{1,0:T(8,128)(2,1)} %get-tuple-element.162.refs_3_, bf16[1024,256]{1,0:T(8,128)(2,1)} %get-tuple-element.167.refs_4_, ...), custom_call_target="tpu_custom_call" | custom-call | flops 8589934592 | bytes 20971520 | tf_op jit(solution)/shard_map/units_out/pallas_call | solution.py:808
  664.1 10.3 %collective-permute-done.47 = bf16[192,512]{1,0:T(8,128)(2,1)S(1)} collective-permute-done((bf16[192,512]{1,0:T(8,128)(2,1)S(1)}, bf16[192,512]{1,0:T(8,128)(2,1)S(1)}, u32[]{:S(2)}, u32[]{:S(2)}) %collective-permute-start.47) | collective-permute-done | bytes 196640 | tf_op jit(solution)/shard_map/ppermute | solution.py:308
  709.0 18.4 %attention_back.2 = (bf16[1024,256]{1,0:T(8,128)(2,1)}, bf16[1024,128]{1,0:T(8,128)(2,1)}, bf16[1024,128]{1,0:T(8,128)(2,1)}) custom-call(s32[4]{0:T(128)} %and_select_fusion.4.first_ref, bf16[1024,512]{1,0:T(8,128)(2,1)} %get-tuple-element.125.q_ref, bf16[1024,256]{1,0:T(8,128)(2,1)} %get-tuple-element.117.k_ref, ...), custom_call_target="tpu_custom_call" | custom-call | flops 5368709120 | bytes 5242880 | tf_op jit(solution)/shard_map/attention_back/pallas_call | solution.py:621
  739.5 18.2 %attention_back.3 = (bf16[1024,256]{1,0:T(8,128)(2,1)}, bf16[1024,128]{1,0:T(8,128)(2,1)}, bf16[1024,128]{1,0:T(8,128)(2,1)}) custom-call(s32[4]{0:T(128)} %and_select_fusion.4.first_ref, bf16[1024,512]{1,0:T(8,128)(2,1)} %get-tuple-element.125.q_ref, bf16[1024,256]{1,0:T(8,128)(2,1)} %get-tuple-element.117.k_ref, ...), custom_call_target="tpu_custom_call" | custom-call | flops 5368709120 | bytes 5242880 | tf_op jit(solution)/shard_map/attention_back/pallas_call | solution.py:621
  864.6 11.1 %finish.9 = f32[2,128,8192]{2,1,0:T(8,128)} custom-call(s32[1]{0:T(128)} %bitcast.111.s_ref, bf16[1536,512]{1,0:T(8,128)(2,1)} %pad_maximum_fusion.14.own, bf16[1536,512]{1,0:T(8,128)(2,1)} %collective-permute-done.58.core, bf16[1536,512]{1,0:T(8,128)(2,1)} %constant_dynamic-update-slice_fusion.54.other, bf16[1536,512]{1,0:T(8,128)(2,1)} %collective-permute-done.59.last), custom_call_target="tpu_custom_call" | custom-call | tf_op jit(solution)/shard_map/finish/pallas_call | solution.py:344
  882.0 18.3 %collective-permute-done.79.other = bf16[896,512]{1,0:T(8,128)(2,1)} collective-permute-done((bf16[896,512]{1,0:T(8,128)(2,1)S(1)}, bf16[896,512]{1,0:T(8,128)(2,1)}, u32[]{:S(2)}, u32[]{:S(2)}) %collective-permute-start.79) | collective-permute-done | bytes 917536 | tf_op jit(solution)/shard_map/ppermute | solution.py:320
  (793 shorter events, 512.1 us)
Async XLA Ops:
  3.6 34.2 %collective-permute-start.4 = (bf16[256,768]{1,0:T(8,128)(2,1)}, bf16[256,768]{1,0:T(8,128)(2,1)S(1)}, u32[]{:S(2)}, u32[]{:S(2)}) collective-permute-start(bf16[256,768]{1,0:T(8,128)(2,1)} %pad_maximum_fusion.33), channel_id=1, source_target_pairs={{0,4},{1,5},{2,6},{3,7},{4,0},{5,1},{6,2},{7,3},{8,12},{9,13},{10,... | collective-permute-start | bytes 1179656 | tf_op jit(solution)/shard_map/ppermute | solution.py:125
  65.1 55.6 %collective-permute-start.2 = (bf16[2,256,2176]{2,1,0:T(8,128)(2,1)}, bf16[2,256,2176]{2,1,0:T(8,128)(2,1)}, u32[]{:S(2)}, u32[]{:S(2)}) collective-permute-start(bf16[2,256,2176]{2,1,0:T(8,128)(2,1)} %pad_maximum_fusion.4), channel_id=1, source_target_pairs={{0,8},{8,0},{16,24},{24,16},{1,9},{9,1},{17,25},{25,17},{2,10},{10... | collective-permute-start | bytes 6684680 | tf_op jit(solution)/shard_map/ppermute | solution.py:216
  68.6 48.8 %collective-permute-start.6 = (bf16[1024,768]{1,0:T(8,128)(2,1)}, bf16[1024,768]{1,0:T(8,128)(2,1)}, u32[]{:S(2)}, u32[]{:S(2)}) collective-permute-start(bf16[1024,768]{1,0:T(8,128)(2,1)} %pad_maximum_fusion.12.w_own), channel_id=1, source_target_pairs={{0,1},{1,0},{2,3},{3,2},{4,5},{5,4},{6,7},{7,6},{8,9},{9,8},{10,11... | collective-permute-start | bytes 4718600 | tf_op jit(solution)/shard_map/ppermute | solution.py:137
  117.2 36.4 %collective-permute-start.14 = (bf16[512,1024]{1,0:T(8,128)(2,1)S(1)}, bf16[512,1024]{1,0:T(8,128)(2,1)S(1)}, u32[]{:S(2)}, u32[]{:S(2)}) collective-permute-start(bf16[512,1024]{1,0:T(8,128)(2,1)S(1)} %constant_dynamic-update-slice_fusion.11), channel_id=1, source_target_pairs={{0,2},{1,3},{2,0},{3,1},{4,6},{5,7},{6,4},{7,5},{8,10},{9,11},{10,... | collective-permute-start | bytes 3145736 | tf_op jit(solution)/shard_map/ppermute | solution.py:131
  117.3 36.3 %collective-permute-start.13 = (bf16[256,1024]{1,0:T(8,128)(2,1)S(1)}, bf16[256,1024]{1,0:T(8,128)(2,1)S(1)}, u32[]{:S(2)}, u32[]{:S(2)}) collective-permute-start(bf16[256,1024]{1,0:T(8,128)(2,1)S(1)} %copy-done.64), channel_id=1, source_target_pairs={{0,4},{1,5},{2,6},{3,7},{4,0},{5,1},{6,2},{7,3},{8,12},{9,13},{10,... | collective-permute-start | bytes 1572872 | tf_op jit(solution)/shard_map/ppermute | solution.py:125
  119.1 35.6 %collective-permute-start.11 = (bf16[256,2048]{1,0:T(8,128)(2,1)S(1)}, bf16[256,2048]{1,0:T(8,128)(2,1)S(1)}, u32[]{:S(2)}, u32[]{:S(2)}) collective-permute-start(bf16[256,2048]{1,0:T(8,128)(2,1)S(1)} %constant_dynamic-update-slice_fusion.9), channel_id=1, source_target_pairs={{0,1},{1,0},{2,3},{3,2},{4,5},{5,4},{6,7},{7,6},{8,9},{9,8},{10,11... | collective-permute-start | bytes 3145736 | tf_op jit(solution)/shard_map/ppermute | solution.py:137
  201.7 31.8 %collective-permute-start.15 = (bf16[512,1024]{1,0:T(8,128)(2,1)}, bf16[512,1024]{1,0:T(8,128)(2,1)}, u32[]{:S(2)}, u32[]{:S(2)}) collective-permute-start(bf16[512,1024]{1,0:T(8,128)(2,1)} %copy-done.55), channel_id=1, source_target_pairs={{0,2},{1,3},{2,0},{3,1},{4,6},{5,7},{6,4},{7,5},{8,10},{9,11},{10,... | collective-permute-start | bytes 3145736 | tf_op jit(solution)/shard_map/ppermute | solution.py:131
  203.5 32.7 %collective-permute-start.16 = (bf16[512,1024]{1,0:T(8,128)(2,1)}, bf16[512,1024]{1,0:T(8,128)(2,1)}, u32[]{:S(2)}, u32[]{:S(2)}) collective-permute-start(bf16[512,1024]{1,0:T(8,128)(2,1)} %copy-done.57), channel_id=1, source_target_pairs={{0,1},{1,0},{2,3},{3,2},{4,5},{5,4},{6,7},{7,6},{8,9},{9,8},{10,11... | collective-permute-start | bytes 3145736 | tf_op jit(solution)/shard_map/ppermute | solution.py:1090
  258.4 34.8 %collective-permute-start.18 = (bf16[256,2176]{1,0:T(8,128)(2,1)}, bf16[256,2176]{1,0:T(8,128)(2,1)}, u32[]{:S(2)}, u32[]{:S(2)}) collective-permute-start(bf16[256,2176]{1,0:T(8,128)(2,1)} %fusion.88), channel_id=1, source_target_pairs={{0,16},{8,24},{16,0},{24,8},{1,17},{9,25},{17,1},{25,9},{2,18},{10... | collective-permute-start | bytes 3342344 | tf_op jit(solution)/shard_map/ppermute | solution.py:235
  262.5 38.1 %collective-permute-start.19 = (bf16[512,1024]{1,0:T(8,128)(2,1)}, bf16[512,1024]{1,0:T(8,128)(2,1)}, u32[]{:S(2)}, u32[]{:S(2)}) collective-permute-start(bf16[512,1024]{1,0:T(8,128)(2,1)} %copy-done.83), channel_id=1, source_target_pairs={{0,1},{1,0},{2,3},{3,2},{4,5},{5,4},{6,7},{7,6},{8,9},{9,8},{10,11... | collective-permute-start | bytes 3145736 | tf_op jit(solution)/shard_map/ppermute | solution.py:1091
  264.7 68.5 %collective-permute-start.22 = (bf16[1024,1024]{1,0:T(8,128)(2,1)}, bf16[1024,1024]{1,0:T(8,128)(2,1)}, u32[]{:S(2)}, u32[]{:S(2)}) collective-permute-start(bf16[1024,1024]{1,0:T(8,128)(2,1)} %constant_dynamic-update-slice_fusion.17.refs_11_.refs_8_), channel_id=1, source_target_pairs={{0,1},{1,0},{2,3},{3,2},{4,5},{5,4},{6,7},{7,6},{8,9},{9,8},{10,11... | collective-permute-start | bytes 6291464 | tf_op jit(solution)/shard_map/ppermute | solution.py:137
  291.4 36.4 %collective-permute-start.23 = (bf16[512,1024]{1,0:T(8,128)(2,1)}, bf16[512,1024]{1,0:T(8,128)(2,1)}, u32[]{:S(2)}, u32[]{:S(2)}) collective-permute-start(bf16[512,1024]{1,0:T(8,128)(2,1)} %pad_maximum_fusion.17), channel_id=1, source_target_pairs={{0,2},{1,3},{2,0},{3,1},{4,6},{5,7},{6,4},{7,5},{8,10},{9,11},{10,... | collective-permute-start | bytes 3145736 | tf_op jit(solution)/shard_map/ppermute | solution.py:131
  339.3 43.2 %collective-permute-start.25 = (bf16[2,256,2176]{2,1,0:T(8,128)(2,1)S(1)}, bf16[2,256,2176]{2,1,0:T(8,128)(2,1)S(1)}, u32[]{:S(2)}, u32[]{:S(2)}) collective-permute-start(bf16[2,256,2176]{2,1,0:T(8,128)(2,1)S(1)} %pad_maximum_fusion.6), channel_id=1, source_target_pairs={{0,8},{8,0},{16,24},{24,16},{1,9},{9,1},{17,25},{25,17},{2,10},{10... | collective-permute-start | bytes 6684680 | tf_op jit(solution)/shard_map/ppermute | solution.py:216
  344.8 36.5 %collective-permute-start.26 = (bf16[512,1024]{1,0:T(8,128)(2,1)S(1)}, bf16[512,1024]{1,0:T(8,128)(2,1)S(1)}, u32[]{:S(2)}, u32[]{:S(2)}) collective-permute-start(bf16[512,1024]{1,0:T(8,128)(2,1)S(1)} %pad_maximum_fusion.18), channel_id=1, source_target_pairs={{0,2},{1,3},{2,0},{3,1},{4,6},{5,7},{6,4},{7,5},{8,10},{9,11},{10,... | collective-permute-start | bytes 3145736 | tf_op jit(solution)/shard_map/ppermute | solution.py:131
  349.1 33.3 %collective-permute-start.27 = (bf16[256,1024]{1,0:T(8,128)(2,1)S(1)}, bf16[256,1024]{1,0:T(8,128)(2,1)S(1)}, u32[]{:S(2)}, u32[]{:S(2)}) collective-permute-start(bf16[256,1024]{1,0:T(8,128)(2,1)S(1)} %pad_maximum_fusion.28), channel_id=1, source_target_pairs={{0,4},{1,5},{2,6},{3,7},{4,0},{5,1},{6,2},{7,3},{8,12},{9,13},{10,... | collective-permute-start | bytes 1572872 | tf_op jit(solution)/shard_map/ppermute | solution.py:125
  354.0 48.7 %collective-permute-start.28 = (bf16[1024,1024]{1,0:T(8,128)(2,1)S(1)}, bf16[1024,1024]{1,0:T(8,128)(2,1)}, u32[]{:S(2)}, u32[]{:S(2)}) collective-permute-start(bf16[1024,1024]{1,0:T(8,128)(2,1)S(1)} %constant_dynamic-update-slice_fusion.27.refs_2_), channel_id=1, source_target_pairs={{0,1},{1,0},{2,3},{3,2},{4,5},{5,4},{6,7},{7,6},{8,9},{9,8},{10,11... | collective-permute-start | bytes 6291464 | tf_op jit(solution)/shard_map/ppermute | solution.py:137
  382.4 70.8 %collective-permute-start.31 = (bf16[1024,1024]{1,0:T(8,128)(2,1)}, bf16[1024,1024]{1,0:T(8,128)(2,1)}, u32[]{:S(2)}, u32[]{:S(2)}) collective-permute-start(bf16[1024,1024]{1,0:T(8,128)(2,1)} %constant_dynamic-update-slice_fusion.29.refs_2_), channel_id=1, source_target_pairs={{0,1},{1,0},{2,3},{3,2},{4,5},{5,4},{6,7},{7,6},{8,9},{9,8},{10,11... | collective-permute-start | bytes 6291464 | tf_op jit(solution)/shard_map/ppermute | solution.py:137
  451.9 44.5 %collective-permute-start.34 = (bf16[1024,1024]{1,0:T(8,128)(2,1)}, bf16[1024,1024]{1,0:T(8,128)(2,1)}, u32[]{:S(2)}, u32[]{:S(2)}) collective-permute-start(bf16[1024,1024]{1,0:T(8,128)(2,1)} %constant_dynamic-update-slice_fusion.33.refs_2_), channel_id=1, source_target_pairs={{0,1},{1,0},{2,3},{3,2},{4,5},{5,4},{6,7},{7,6},{8,9},{9,8},{10,11... | collective-permute-start | bytes 6291464 | tf_op jit(solution)/shard_map/ppermute | solution.py:137
  528.4 33.0 %collective-permute-start.37 = (bf16[1024,512]{1,0:T(8,128)(2,1)}, bf16[1024,512]{1,0:T(8,128)(2,1)}, u32[]{:S(2)}, u32[]{:S(2)}) collective-permute-start(bf16[1024,512]{1,0:T(8,128)(2,1)} %constant_dynamic-update-slice_fusion.37.refs_2_), channel_id=1, source_target_pairs={{0,1},{1,0},{2,3},{3,2},{4,5},{5,4},{6,7},{7,6},{8,9},{9,8},{10,11... | collective-permute-start | bytes 3145736 | tf_op jit(solution)/shard_map/ppermute | solution.py:137
  595.8 39.5 %collective-permute-start.40 = (bf16[256,2176]{1,0:T(8,128)(2,1)}, bf16[256,2176]{1,0:T(8,128)(2,1)}, u32[]{:S(2)}, u32[]{:S(2)}) collective-permute-start(bf16[256,2176]{1,0:T(8,128)(2,1)} %fusion.89), channel_id=1, source_target_pairs={{0,16},{8,24},{16,0},{24,8},{1,17},{9,25},{17,1},{25,9},{2,18},{10... | collective-permute-start | bytes 3342344 | tf_op jit(solution)/shard_map/ppermute | solution.py:235
  797.6 32.0 %collective-permute-start.53 = (bf16[2,256,2048]{2,1,0:T(8,128)(2,1)}, bf16[2,256,2048]{2,1,0:T(8,128)(2,1)}, u32[]{:S(2)}, u32[]{:S(2)}) collective-permute-start(bf16[2,256,2048]{2,1,0:T(8,128)(2,1)} %pad_maximum_fusion.11), channel_id=1, source_target_pairs={{0,8},{8,0},{16,24},{24,16},{1,9},{9,1},{17,25},{25,17},{2,10},{10... | collective-permute-start | bytes 6291464 | tf_op jit(solution)/shard_map/ppermute | solution.py:232
  812.7 45.4 %collective-permute-start.58 = (bf16[1536,512]{1,0:T(8,128)(2,1)}, bf16[1536,512]{1,0:T(8,128)(2,1)}, u32[]{:S(2)}, u32[]{:S(2)}) collective-permute-start(bf16[1536,512]{1,0:T(8,128)(2,1)} %pad_maximum_fusion.14.own), channel_id=1, source_target_pairs={{0,8},{8,0},{16,24},{24,16},{1,9},{9,1},{17,25},{25,17},{2,10},{10... | collective-permute-start | bytes 4718600 | tf_op jit(solution)/shard_map/ppermute | solution.py:318
  858.1 48.9 %collective-permute-start.81 = (bf16[896,512]{1,0:T(8,128)(2,1)S(1)}, bf16[896,512]{1,0:T(8,128)(2,1)S(1)}, u32[]{:S(2)}, u32[]{:S(2)}) collective-permute-start(bf16[896,512]{1,0:T(8,128)(2,1)S(1)} %pad_maximum_fusion.20.own), channel_id=1, source_target_pairs={{0,8},{8,0},{16,24},{24,16},{1,9},{9,1},{17,25},{25,17},{2,10},{10... | collective-permute-start | bytes 2752520 | tf_op jit(solution)/shard_map/ppermute | solution.py:318
  877.4 47.9 %collective-permute-start.68 = (bf16[384,512]{1,0:T(8,128)(2,1)}, bf16[384,512]{1,0:T(8,128)(2,1)}, u32[]{:S(2)}, u32[]{:S(2)}) collective-permute-start(bf16[384,512]{1,0:T(8,128)(2,1)} %pad_maximum_fusion.34.own), channel_id=1, source_target_pairs={{0,8},{8,0},{16,24},{24,16},{1,9},{9,1},{17,25},{25,17},{2,10},{10... | collective-permute-start | bytes 1179656 | tf_op jit(solution)/shard_map/ppermute | solution.py:318
  (215 other events, 2320.1 us)

commit v5 on v4

--- a/solution.py
+++ b/solution.py
@@ -271,7 +271,7 @@
             final_hidden(parts, s, 8 * LANES, 1)[0],
         ]
 
-    def sum_features(self, grads, key=None, value=None, mid=(), deps=(), late=(), mark=None):
+    def sum_features(self, grads, key=None, value=None, mid=(), back=(), deps=(), late=(), mark=None):
         if not self.fast:
             grads = grads + ([key, value] if key is not None else [])
             found = []
@@ -282,7 +282,7 @@
         if key is not None:
             rest = jnp.zeros((key.shape[0], PACK - 2 * LANES), F32)
             packed.append(jnp.concatenate([key, value, rest], axis=1))
-        half = self.sum_start(jnp.concatenate(packed, axis=0), mid)
+        half = self.sum_start(jnp.concatenate(packed, axis=0), mid, back)
         parts = self.sum_end(half, deps, late=late)
         self.marks[mark] = parts[2]
         s = self.s.astype(jnp.int32)[None]
@@ -294,7 +294,7 @@
             found.append(final_kv(parts, s, at))
         return found
 
-    def sum_start(self, packed, mid=()):
+    def sum_start(self, packed, mid=(), back=()):
         rows = packed.shape[0]
         halves = packed.reshape(2, rows // 2, PACK)
         got = lax.ppermute(pick(halves, 1 - self.x, 0).astype(BF), "wsh", X_SWAP)
@@ -304,7 +304,7 @@
         for r in range(1, 4):
             out = pick(blocks, (self.z + r) % 4, 0).astype(BF)
             total = total + lax.ppermute(out, "wsh", z_shift(r)).astype(F32)
-        own = total.astype(BF)
+        own = after(total.astype(BF), *back)
         got = [own] + [lax.ppermute(own, "wsh", z_shift(r)) for r in range(1, 4)]
         ring = jnp.stack(got)
         return jnp.concatenate([pick(ring, (self.z - j) % 4, 0) for j in range(4)], axis=0)
@@ -1035,9 +1035,9 @@
         out_swapped = mover.across(out_four, qkv_full[1])
         out_full = mover.head_rows_done(out_swapped, output_weight.shape[0])
         d_mlp = mover.gather_rest(d_mlp_local, after(d_mlp_other, first_all))
-        low_four = mover.near(low_pair, out_four)
-        high_pair = mover.far(down_local[:, half_width:], low_pair, qkv_full[1])
-        first_all = after(first_all, d_mlp)
+        low_near = lax.ppermute(after(low_pair, out_four), "wsh", NEAR_SWAP)
+        high_local = after(down_local[:, half_width:], low_pair, qkv_full[1])
+        high_far = lax.ppermute(high_local, "wsh", FAR_SWAP)
     else:
         qkv_full = mover.across(qkv_pair)
         first_all = mover.gather_tokens(first_cols)
@@ -1084,15 +1084,18 @@
         early,
     )
     if mover.fast:
+        low_four = jnp.concatenate([low_pair, after(low_near, early)], axis=0)
+        high_pair = jnp.concatenate([high_local, after(high_far, early)], axis=0)
         low_rows = low_four.shape[0] // 2
         low_early = after(low_four[:low_rows], out_swapped[1], early)
         low_other = [
             lax.ppermute(low_early, "wsh", X_SWAP),
-            lax.ppermute(low_four[low_rows:], "wsh", X_SWAP),
+            lax.ppermute(after(low_four[low_rows:], early), "wsh", X_SWAP),
         ]
         down_low = (low_four, jnp.concatenate(low_other, axis=0))
-        high_four = mover.near(high_pair, low_four, early)
-        attended = attend_rest(out_full, high_pair)
+        high_near = lax.ppermute(after(high_pair, low_four, early), "wsh", NEAR_SWAP)
+        attended = attend_rest(out_full, high_pair, d_mlp)
+        high_four = jnp.concatenate([high_pair, after(high_near, attended)], axis=0)
         chunk_pairs = [gate_up_far(0, high_four)]
         attended = after(attended, high_four, low_other[0])
         down_high = mover.across(high_four)
@@ -1209,7 +1212,7 @@
     d_attn_cols = jnp.concatenate([d_attn_own, d_la_two_own], axis=1)
     if mover.fast:
         packed = jnp.concatenate([pack(v) for v in (gate_grad, up_grad, down_in_grad)], axis=0)
-        hidden_half = mover.sum_start(packed)
+        hidden_half = mover.sum_start(packed, (mover.marks["second"],))
         d_attn_other = lax.ppermute(d_attn_cols, "seq", Y_SWAP)
         d_attn_all = mover.gather_rest(d_attn_cols, after(d_attn_other, hidden_half))
     else:
@@ -1298,6 +1301,7 @@
     (last_grad,) = mover.sum_features(
         [attention_in_grad],
         mid=(mover.marks.get("first_away"),),
+        back=(first_sent,),
         deps=(mover.marks.get("features"),),
         late=early_grads,
     )

time: 942 us -> 927 us (0.984)
  waiting for transfers between devices: 257 us -> 237 us
    ppermute x9 -> x7, waiting for transfers between devices: 98.5 us -> 69.5 us  [near(): return jnp.concatenate([pair, lax.ppermute(pair, 'wsh', NEAR_SWAP)], axis=0)]
    unnamed x371 -> x350, local copies, waits for them, and re-layouts: 75.3 us -> 77.6 us
    ppermute x9 -> x8, waiting for transfers between devices: 51.8 us -> 51.3 us  [far(): lax.ppermute(chunk, 'wsh', FAR_SWAP)]
  transfers between devices with their start and end apart: 84 -> 84, of which waited for: 34 -> 33; matrix products, arithmetic and copies ran while one was open for 28% -> 30% of each run, Pallas kernels for 18% -> 21%
where the time goes in v5:
time: 927 us; the launch traced here: 915 us
  Pallas kernels  239 us (26%)
  waiting for transfers between devices  237 us (26%)
  local copies, waits for them, and re-layouts  155 us (17%)
  other arithmetic  115 us (12%)
  matrix products  83.9 us (9%)
  starting transfers between devices  82.2 us (9%)
    pallas_call x5, Pallas kernels, mlp_call(): pl.pallas_call(lambda *refs: mlp_body(owners, sums is not None, *refs), g...  97.1 us
    unnamed x350, local copies, waits for them, and re-layouts  77.6 us
    ppermute x7, waiting for transfers between devices, near(): return jnp.concatenate([pair, lax.ppermute(pair, 'wsh', NEAR_SWAP)], axis=0)  69.5 us
    ppermute x8, waiting for transfers between devices, far(): lax.ppermute(chunk, 'wsh', FAR_SWAP)  51.3 us
    dot_general x20, matrix products, low_dot(): return jnp.dot(left, right, preferred_element_type=F32)  49.1 us
    pallas_call x2, Pallas kernels, attention_call(): pl.pallas_call(forward_body, grid_spec=pltpu.PrefetchScalarGridSpec(num_s...  45.9 us
    ppermute x8, waiting for transfers between devices, across(): return (four, lax.ppermute(four, 'wsh', X_SWAP))  37.9 us
    pallas_call x2, Pallas kernels, attention_back_call(): pl.pallas_call(backward_body, grid_spec=pltpu.PrefetchScalarGridSpec(num_...  36.7 us
  transfers between devices with their start and end apart: 84, of which 33 were waited for; matrix products, arithmetic and copies ran while one was open for 30% of the time, Pallas kernels for 21%

profile of v5, /device:TPU:0, one launch (start us, length us, event | category | flops | bytes accessed | tf_op | source)
XLA Modules:
  0.0 915.2 jit_solution(12632919322853407425)
XLA Ops:
  43.0 18.2 %collective-permute-done = bf16[256,2176]{1,0:T(8,128)(2,1)} collective-permute-done((bf16[256,2176]{1,0:T(8,128)(2,1)}, bf16[256,2176]{1,0:T(8,128)(2,1)}, u32[]{:S(2)}, u32[]{:S(2)}) %collective-permute-start) | collective-permute-done | bytes 1114144 | tf_op jit(solution)/shard_map/ppermute | solution.py:1027
  75.9 20.2 %collective-permute-done.8 = bf16[64,2048]{1,0:T(8,128)(2,1)S(1)} collective-permute-done((bf16[64,2048]{1,0:T(8,128)(2,1)S(1)}, bf16[64,2048]{1,0:T(8,128)(2,1)S(1)}, u32[]{:S(2)}, u32[]{:S(2)}) %collective-permute-start.8) | collective-permute-done | bytes 262176 | tf_op jit(solution)/shard_map/ppermute | solution.py:125
  109.1 8.8 collective-permute-done.9
  139.8 9.2 %qkv.1 = (bf16[1024,512]{1,0:T(8,128)(2,1)}, bf16[1024,256]{1,0:T(8,128)(2,1)}, bf16[1024,256]{1,0:T(8,128)(2,1)}) custom-call(bf16[1024,2176]{1,0:T(8,128)(2,1)} %bitcast.447, bf16[1024,768]{1,0:T(8,128)(2,1)} %pad_maximum_fusion.12.w_own, bf16[1024,768]{1,0:T(8,128)(2,1)} %collective-permute-done.5.w_other, bf16[1024,128]{1,0:T(8,128)(2,1)} %fusion.55.la_q, ...), custom_call_target="tpu_custom_call" | custom-call | flops 3221225472 | bytes 12582912 | tf_op jit(solution)/shard_map/qkv/pallas_call | solution.py:443
  149.6 22.8 %attention.2 = (bf16[1024,256]{1,0:T(8,128)(2,1)}, f32[1024,128]{1,0:T(8,128)}) custom-call(s32[4]{0:T(128)} %and_select_fusion.4.first_ref, bf16[1024,512]{1,0:T(8,128)(2,1)} %get-tuple-element.130.q_ref, bf16[1024,256]{1,0:T(8,128)(2,1)} %get-tuple-element.120.k_ref, bf16[1024,256]{1,0:T(8,128)(2,1)} %get-tuple-element.121.v_ref, ...), custom_call_target="tpu_custom_call" | custom-call | flops 2147483648 | bytes 3145728 | tf_op jit(solution)/shard_map/attention/pallas_call | solution.py:517
  188.3 23.1 %attention.3 = (bf16[1024,256]{1,0:T(8,128)(2,1)}, f32[1024,128]{1,0:T(8,128)}) custom-call(s32[4]{0:T(128)} %and_select_fusion.4.first_ref, bf16[1024,512]{1,0:T(8,128)(2,1)} %get-tuple-element.130.q_ref, bf16[1024,256]{1,0:T(8,128)(2,1)} %get-tuple-element.120.k_ref, bf16[1024,256]{1,0:T(8,128)(2,1)} %get-tuple-element.121.v_ref, ...), custom_call_target="tpu_custom_call" | custom-call | flops 2147483648 | bytes 3145728 | tf_op jit(solution)/shard_map/attention/pallas_call | solution.py:517
  247.1 19.2 %collective-permute-done.20 = bf16[256,1024]{1,0:T(8,128)(2,1)} collective-permute-done((bf16[256,1024]{1,0:T(8,128)(2,1)S(1)}, bf16[256,1024]{1,0:T(8,128)(2,1)}, u32[]{:S(2)}, u32[]{:S(2)}) %collective-permute-start.20) | collective-permute-done | bytes 524320 | tf_op jit(solution)/shard_map/ppermute | solution.py:125
  299.5 8.4 collective-permute-done.23
  337.9 23.6 %collective-permute-done.26 = bf16[512,1024]{1,0:T(8,128)(2,1)S(1)} collective-permute-done((bf16[512,1024]{1,0:T(8,128)(2,1)S(1)}, bf16[512,1024]{1,0:T(8,128)(2,1)S(1)}, u32[]{:S(2)}, u32[]{:S(2)}) %collective-permute-start.26) | collective-permute-done | bytes 1048608 | tf_op jit(solution)/shard_map/ppermute | solution.py:131
  367.8 17.1 %collective-permute-done.28.refs_3_ = bf16[1024,1024]{1,0:T(8,128)(2,1)} collective-permute-done((bf16[1024,1024]{1,0:T(8,128)(2,1)S(1)}, bf16[1024,1024]{1,0:T(8,128)(2,1)}, u32[]{:S(2)}, u32[]{:S(2)}) %collective-permute-start.28) | collective-permute-done | bytes 2097184 | tf_op jit(solution)/shard_map/ppermute | solution.py:137
  385.0 20.0 %units.5 = (bf16[1024,512]{1,0:T(8,128)(2,1)}, bf16[1024,512]{1,0:T(8,128)(2,1)}, bf16[1024,512]{1,0:T(8,128)(2,1)}, f32[1024,2048]{1,0:T(8,128)}, f32[1024,256]{1,0:T(8,128)}) custom-call(s32[2]{0:T(128)} %pad_add_fusion.refs_0_, bf16[1024,2176]{1,0:T(8,128)(2,1)} %bitcast.423, bf16[1024,1024]{1,0:T(8,128)(2,1)} %copy-done.89, ...), custom_call_target="tpu_custom_call" | custom-call | flops 10737418240 | bytes 33554432 | tf_op jit(solution)/shard_map/units/pallas_call | solution.py:766
  415.1 18.7 %collective-permute-done.29 = bf16[512,1024]{1,0:T(8,128)(2,1)S(1)} collective-permute-done((bf16[512,1024]{1,0:T(8,128)(2,1)S(1)}, bf16[512,1024]{1,0:T(8,128)(2,1)S(1)}, u32[]{:S(2)}, u32[]{:S(2)}) %collective-permute-start.29) | collective-permute-done | bytes 1048608 | tf_op jit(solution)/shard_map/ppermute | solution.py:131
  436.1 21.4 %units.6 = (bf16[1024,512]{1,0:T(8,128)(2,1)}, bf16[1024,512]{1,0:T(8,128)(2,1)}, bf16[1024,512]{1,0:T(8,128)(2,1)}, f32[1024,2048]{1,0:T(8,128)}, f32[1024,256]{1,0:T(8,128)}) custom-call(s32[2]{0:T(128)} %pad_add_fusion.1.refs_0_, bf16[1024,2176]{1,0:T(8,128)(2,1)} %bitcast.424, ...), custom_call_target="tpu_custom_call", output_to_operand_aliasing={{3}: (15, {}), {4}: (16, {})} | custom-call | flops 10737418240 | bytes 33554432 | tf_op jit(solution)/shard_map/units/pallas_call | solution.py:766
  462.9 8.8 collective-permute-done.33
  479.8 21.3 %units.7 = (bf16[1024,512]{1,0:T(8,128)(2,1)}, bf16[1024,512]{1,0:T(8,128)(2,1)}, bf16[1024,512]{1,0:T(8,128)(2,1)}, f32[1024,2048]{1,0:T(8,128)}, f32[1024,256]{1,0:T(8,128)}) custom-call(s32[2]{0:T(128)} %pad_add_fusion.2.refs_0_, bf16[1024,2176]{1,0:T(8,128)(2,1)} %bitcast.425, ...), custom_call_target="tpu_custom_call", output_to_operand_aliasing={{3}: (15, {}), {4}: (16, {})} | custom-call | flops 10737418240 | bytes 33554432 | tf_op jit(solution)/shard_map/units/pallas_call | solution.py:766
  502.7 8.7 collective-permute-done.35
  527.5 17.3 %units.8 = (bf16[1024,256]{1,0:T(8,128)(2,1)}, bf16[1024,256]{1,0:T(8,128)(2,1)}, bf16[1024,256]{1,0:T(8,128)(2,1)}, f32[1024,2048]{1,0:T(8,128)}, f32[1024,256]{1,0:T(8,128)}) custom-call(s32[2]{0:T(128)} %pad_add_fusion.3.refs_0_, bf16[1024,2176]{1,0:T(8,128)(2,1)} %bitcast.426, ...), custom_call_target="tpu_custom_call", output_to_operand_aliasing={{3}: (15, {}), {4}: (16, {})} | custom-call | flops 5368709120 | bytes 33554432 | tf_op jit(solution)/shard_map/units/pallas_call | solution.py:766
  545.3 17.1 %units.9 = (bf16[1024,256]{1,0:T(8,128)(2,1)}, bf16[1024,256]{1,0:T(8,128)(2,1)}, bf16[1024,256]{1,0:T(8,128)(2,1)}, f32[1024,2048]{1,0:T(8,128)}, f32[1024,256]{1,0:T(8,128)}) custom-call(s32[2]{0:T(128)} %pad_add_fusion.3.refs_0_, bf16[1024,2176]{1,0:T(8,128)(2,1)} %bitcast.427, ...), custom_call_target="tpu_custom_call", output_to_operand_aliasing={{3}: (15, {}), {4}: (16, {})} | custom-call | flops 5368709120 | bytes 33554432 | tf_op jit(solution)/shard_map/units/pallas_call | solution.py:766
  586.9 15.6 %units_out.1 = f32[1024,2048]{1,0:T(8,128)} custom-call(s32[5]{0:T(128)} %stack.205.refs_0_, bf16[1024,512]{1,0:T(8,128)(2,1)} %get-tuple-element.156.refs_1_, bf16[1024,512]{1,0:T(8,128)(2,1)} %get-tuple-element.163.refs_2_, bf16[1024,512]{1,0:T(8,128)(2,1)} %get-tuple-element.170.refs_3_, bf16[1024,256]{1,0:T(8,128)(2,1)} %get-tuple-element.175.refs_4_, ...), custom_call_target="tpu_custom_call" | custom-call | flops 8589934592 | bytes 20971520 | tf_op jit(solution)/shard_map/units_out/pallas_call | solution.py:808
  647.9 10.2 %collective-permute-done.47 = bf16[192,512]{1,0:T(8,128)(2,1)S(1)} collective-permute-done((bf16[192,512]{1,0:T(8,128)(2,1)S(1)}, bf16[192,512]{1,0:T(8,128)(2,1)S(1)}, u32[]{:S(2)}, u32[]{:S(2)}) %collective-permute-start.47) | collective-permute-done | bytes 196640 | tf_op jit(solution)/shard_map/ppermute | solution.py:308
  693.6 18.2 %attention_back.2 = (bf16[1024,256]{1,0:T(8,128)(2,1)}, bf16[1024,128]{1,0:T(8,128)(2,1)}, bf16[1024,128]{1,0:T(8,128)(2,1)}) custom-call(s32[4]{0:T(128)} %and_select_fusion.4.first_ref, bf16[1024,512]{1,0:T(8,128)(2,1)} %get-tuple-element.130.q_ref, bf16[1024,256]{1,0:T(8,128)(2,1)} %get-tuple-element.120.k_ref, ...), custom_call_target="tpu_custom_call" | custom-call | flops 5368709120 | bytes 5242880 | tf_op jit(solution)/shard_map/attention_back/pallas_call | solution.py:621
  724.2 18.4 %attention_back.3 = (bf16[1024,256]{1,0:T(8,128)(2,1)}, bf16[1024,128]{1,0:T(8,128)(2,1)}, bf16[1024,128]{1,0:T(8,128)(2,1)}) custom-call(s32[4]{0:T(128)} %and_select_fusion.4.first_ref, bf16[1024,512]{1,0:T(8,128)(2,1)} %get-tuple-element.130.q_ref, bf16[1024,256]{1,0:T(8,128)(2,1)} %get-tuple-element.120.k_ref, ...), custom_call_target="tpu_custom_call" | custom-call | flops 5368709120 | bytes 5242880 | tf_op jit(solution)/shard_map/attention_back/pallas_call | solution.py:621
  850.8 11.1 %finish.9 = f32[2,128,8192]{2,1,0:T(8,128)} custom-call(s32[1]{0:T(128)} %bitcast.111.s_ref, bf16[1536,512]{1,0:T(8,128)(2,1)} %pad_maximum_fusion.14.own, bf16[1536,512]{1,0:T(8,128)(2,1)} %collective-permute-done.58.core, bf16[1536,512]{1,0:T(8,128)(2,1)} %constant_dynamic-update-slice_fusion.58.other, bf16[1536,512]{1,0:T(8,128)(2,1)} %collective-permute-done.59.last), custom_call_target="tpu_custom_call" | custom-call | tf_op jit(solution)/shard_map/finish/pallas_call | solution.py:344
  870.0 15.0 %collective-permute-done.79.other = bf16[896,512]{1,0:T(8,128)(2,1)} collective-permute-done((bf16[896,512]{1,0:T(8,128)(2,1)S(1)}, bf16[896,512]{1,0:T(8,128)(2,1)}, u32[]{:S(2)}, u32[]{:S(2)}) %collective-permute-start.79) | collective-permute-done | bytes 917536 | tf_op jit(solution)/shard_map/ppermute | solution.py:320
  (770 shorter events, 519.1 us)
Async XLA Ops:
  3.6 34.3 %collective-permute-start.3 = (bf16[256,768]{1,0:T(8,128)(2,1)}, bf16[256,768]{1,0:T(8,128)(2,1)S(1)}, u32[]{:S(2)}, u32[]{:S(2)}) collective-permute-start(bf16[256,768]{1,0:T(8,128)(2,1)} %pad_maximum_fusion.32), channel_id=1, source_target_pairs={{0,4},{1,5},{2,6},{3,7},{4,0},{5,1},{6,2},{7,3},{8,12},{9,13},{10,... | collective-permute-start | bytes 1179656 | tf_op jit(solution)/shard_map/ppermute | solution.py:125
  65.1 58.1 %collective-permute-start.2 = (bf16[2,256,2176]{2,1,0:T(8,128)(2,1)}, bf16[2,256,2176]{2,1,0:T(8,128)(2,1)}, u32[]{:S(2)}, u32[]{:S(2)}) collective-permute-start(bf16[2,256,2176]{2,1,0:T(8,128)(2,1)} %pad_maximum_fusion.4), channel_id=1, source_target_pairs={{0,8},{8,0},{16,24},{24,16},{1,9},{9,1},{17,25},{25,17},{2,10},{10... | collective-permute-start | bytes 6684680 | tf_op jit(solution)/shard_map/ppermute | solution.py:216
  66.5 53.3 %collective-permute-start.5 = (bf16[1024,768]{1,0:T(8,128)(2,1)}, bf16[1024,768]{1,0:T(8,128)(2,1)}, u32[]{:S(2)}, u32[]{:S(2)}) collective-permute-start(bf16[1024,768]{1,0:T(8,128)(2,1)} %pad_maximum_fusion.12.w_own), channel_id=1, source_target_pairs={{0,1},{1,0},{2,3},{3,2},{4,5},{5,4},{6,7},{7,6},{8,9},{9,8},{10,11... | collective-permute-start | bytes 4718600 | tf_op jit(solution)/shard_map/ppermute | solution.py:137
  73.3 33.5 %collective-permute-start.11 = (bf16[256,1024]{1,0:T(8,128)(2,1)}, bf16[256,1024]{1,0:T(8,128)(2,1)}, u32[]{:S(2)}, u32[]{:S(2)}) collective-permute-start(bf16[256,1024]{1,0:T(8,128)(2,1)} %get-tuple-element.126), channel_id=1, source_target_pairs={{0,4},{1,5},{2,6},{3,7},{4,0},{5,1},{6,2},{7,3},{8,12},{9,13},{10,... | collective-permute-start | bytes 1572872 | tf_op jit(solution)/shard_map/ppermute | solution.py:125
  119.8 54.4 %collective-permute-start.14 = (bf16[512,1024]{1,0:T(8,128)(2,1)}, bf16[512,1024]{1,0:T(8,128)(2,1)}, u32[]{:S(2)}, u32[]{:S(2)}) collective-permute-start(bf16[512,1024]{1,0:T(8,128)(2,1)} %get-tuple-element.136), channel_id=1, source_target_pairs={{0,2},{1,3},{2,0},{3,1},{4,6},{5,7},{6,4},{7,5},{8,10},{9,11},{10,... | collective-permute-start | bytes 3145736 | tf_op jit(solution)/shard_map/ppermute | solution.py:1038
  119.8 60.1 %collective-permute-start.10 = (bf16[256,2048]{1,0:T(8,128)(2,1)}, bf16[256,2048]{1,0:T(8,128)(2,1)}, u32[]{:S(2)}, u32[]{:S(2)}) collective-permute-start(bf16[256,2048]{1,0:T(8,128)(2,1)} %constant_dynamic-update-slice_fusion.9), channel_id=1, source_target_pairs={{0,1},{1,0},{2,3},{3,2},{4,5},{5,4},{6,7},{7,6},{8,9},{9,8},{10,11... | collective-permute-start | bytes 3145736 | tf_op jit(solution)/shard_map/ppermute | solution.py:137
  120.3 53.9 %collective-permute-start.12 = (bf16[256,1024]{1,0:T(8,128)(2,1)S(1)}, bf16[256,1024]{1,0:T(8,128)(2,1)}, u32[]{:S(2)}, u32[]{:S(2)}) collective-permute-start(bf16[256,1024]{1,0:T(8,128)(2,1)S(1)} %copy-done.57), channel_id=1, source_target_pairs={{0,4},{1,5},{2,6},{3,7},{4,0},{5,1},{6,2},{7,3},{8,12},{9,13},{10,... | collective-permute-start | bytes 1572872 | tf_op jit(solution)/shard_map/ppermute | solution.py:1040
  178.7 34.7 %collective-permute-start.15 = (bf16[512,1024]{1,0:T(8,128)(2,1)}, bf16[512,1024]{1,0:T(8,128)(2,1)}, u32[]{:S(2)}, u32[]{:S(2)}) collective-permute-start(bf16[512,1024]{1,0:T(8,128)(2,1)} %get-tuple-element.134), channel_id=1, source_target_pairs={{0,2},{1,3},{2,0},{3,1},{4,6},{5,7},{6,4},{7,5},{8,10},{9,11},{10,... | collective-permute-start | bytes 3145736 | tf_op jit(solution)/shard_map/ppermute | solution.py:1096
  179.9 36.0 %collective-permute-start.16 = (bf16[512,1024]{1,0:T(8,128)(2,1)}, bf16[512,1024]{1,0:T(8,128)(2,1)}, u32[]{:S(2)}, u32[]{:S(2)}) collective-permute-start(bf16[512,1024]{1,0:T(8,128)(2,1)} %get-tuple-element.136), channel_id=1, source_target_pairs={{0,1},{1,0},{2,3},{3,2},{4,5},{5,4},{6,7},{7,6},{8,9},{9,8},{10,11... | collective-permute-start | bytes 3145736 | tf_op jit(solution)/shard_map/ppermute | solution.py:1092
  238.1 35.9 %collective-permute-start.18 = (bf16[256,2176]{1,0:T(8,128)(2,1)}, bf16[256,2176]{1,0:T(8,128)(2,1)}, u32[]{:S(2)}, u32[]{:S(2)}) collective-permute-start(bf16[256,2176]{1,0:T(8,128)(2,1)} %fusion.88), channel_id=1, source_target_pairs={{0,16},{8,24},{16,0},{24,8},{1,17},{9,25},{17,1},{25,9},{2,18},{10... | collective-permute-start | bytes 3342344 | tf_op jit(solution)/shard_map/ppermute | solution.py:235
  245.1 36.4 %collective-permute-start.19 = (bf16[512,1024]{1,0:T(8,128)(2,1)}, bf16[512,1024]{1,0:T(8,128)(2,1)}, u32[]{:S(2)}, u32[]{:S(2)}) collective-permute-start(bf16[512,1024]{1,0:T(8,128)(2,1)} %collective-permute-done.14), channel_id=1, source_target_pairs={{0,1},{1,0},{2,3},{3,2},{4,5},{5,4},{6,7},{7,6},{8,9},{9,8},{10,11... | collective-permute-start | bytes 3145736 | tf_op jit(solution)/shard_map/ppermute | solution.py:1093
  245.6 69.7 %collective-permute-start.22 = (bf16[1024,1024]{1,0:T(8,128)(2,1)}, bf16[1024,1024]{1,0:T(8,128)(2,1)}, u32[]{:S(2)}, u32[]{:S(2)}) collective-permute-start(bf16[1024,1024]{1,0:T(8,128)(2,1)} %constant_dynamic-update-slice_fusion.20.refs_11_.refs_8_), channel_id=1, source_target_pairs={{0,1},{1,0},{2,3},{3,2},{4,5},{5,4},{6,7},{7,6},{8,9},{9,8},{10,11... | collective-permute-start | bytes 6291464 | tf_op jit(solution)/shard_map/ppermute | solution.py:137
  271.4 36.4 %collective-permute-start.23 = (bf16[512,1024]{1,0:T(8,128)(2,1)}, bf16[512,1024]{1,0:T(8,128)(2,1)}, u32[]{:S(2)}, u32[]{:S(2)}) collective-permute-start(bf16[512,1024]{1,0:T(8,128)(2,1)} %pad_maximum_fusion.16), channel_id=1, source_target_pairs={{0,2},{1,3},{2,0},{3,1},{4,6},{5,7},{6,4},{7,5},{8,10},{9,11},{10,... | collective-permute-start | bytes 3145736 | tf_op jit(solution)/shard_map/ppermute | solution.py:131
  319.4 43.8 %collective-permute-start.25 = (bf16[2,256,2176]{2,1,0:T(8,128)(2,1)S(1)}, bf16[2,256,2176]{2,1,0:T(8,128)(2,1)S(1)}, u32[]{:S(2)}, u32[]{:S(2)}) collective-permute-start(bf16[2,256,2176]{2,1,0:T(8,128)(2,1)S(1)} %pad_maximum_fusion.6), channel_id=1, source_target_pairs={{0,8},{8,0},{16,24},{24,16},{1,9},{9,1},{17,25},{25,17},{2,10},{10... | collective-permute-start | bytes 6684680 | tf_op jit(solution)/shard_map/ppermute | solution.py:216
  324.7 36.8 %collective-permute-start.26 = (bf16[512,1024]{1,0:T(8,128)(2,1)S(1)}, bf16[512,1024]{1,0:T(8,128)(2,1)S(1)}, u32[]{:S(2)}, u32[]{:S(2)}) collective-permute-start(bf16[512,1024]{1,0:T(8,128)(2,1)S(1)} %pad_maximum_fusion.17), channel_id=1, source_target_pairs={{0,2},{1,3},{2,0},{3,1},{4,6},{5,7},{6,4},{7,5},{8,10},{9,11},{10,... | collective-permute-start | bytes 3145736 | tf_op jit(solution)/shard_map/ppermute | solution.py:131
  336.4 48.6 %collective-permute-start.28 = (bf16[1024,1024]{1,0:T(8,128)(2,1)S(1)}, bf16[1024,1024]{1,0:T(8,128)(2,1)}, u32[]{:S(2)}, u32[]{:S(2)}) collective-permute-start(bf16[1024,1024]{1,0:T(8,128)(2,1)S(1)} %constant_dynamic-update-slice_fusion.31.refs_2_), channel_id=1, source_target_pairs={{0,1},{1,0},{2,3},{3,2},{4,5},{5,4},{6,7},{7,6},{8,9},{9,8},{10,11... | collective-permute-start | bytes 6291464 | tf_op jit(solution)/shard_map/ppermute | solution.py:137
  362.5 73.5 %collective-permute-start.31 = (bf16[1024,1024]{1,0:T(8,128)(2,1)}, bf16[1024,1024]{1,0:T(8,128)(2,1)}, u32[]{:S(2)}, u32[]{:S(2)}) collective-permute-start(bf16[1024,1024]{1,0:T(8,128)(2,1)} %constant_dynamic-update-slice_fusion.33.refs_2_), channel_id=1, source_target_pairs={{0,1},{1,0},{2,3},{3,2},{4,5},{5,4},{6,7},{7,6},{8,9},{9,8},{10,11... | collective-permute-start | bytes 6291464 | tf_op jit(solution)/shard_map/ppermute | solution.py:137
  434.8 45.0 %collective-permute-start.34 = (bf16[1024,1024]{1,0:T(8,128)(2,1)}, bf16[1024,1024]{1,0:T(8,128)(2,1)}, u32[]{:S(2)}, u32[]{:S(2)}) collective-permute-start(bf16[1024,1024]{1,0:T(8,128)(2,1)} %constant_dynamic-update-slice_fusion.37.refs_2_), channel_id=1, source_target_pairs={{0,1},{1,0},{2,3},{3,2},{4,5},{5,4},{6,7},{7,6},{8,9},{9,8},{10,11... | collective-permute-start | bytes 6291464 | tf_op jit(solution)/shard_map/ppermute | solution.py:137
  754.0 43.5 %collective-permute-start.54 = (bf16[1024,128]{1,0:T(8,128)(2,1)}, bf16[1024,128]{1,0:T(8,128)(2,1)}, u32[]{:S(2)}, u32[]{:S(2)}) collective-permute-start(bf16[1024,128]{1,0:T(8,128)(2,1)} %convolution_add_fusion.2), channel_id=1, source_target_pairs={{0,8},{8,0},{16,24},{24,16},{1,9},{9,1},{17,25},{25,17},{2,10},{10... | collective-permute-start | bytes 786440 | tf_op jit(solution)/shard_map/ppermute | solution.py:250
  768.1 39.9 %collective-permute-start.55 = (bf16[768,512]{1,0:T(8,128)(2,1)S(1)}, bf16[768,512]{1,0:T(8,128)(2,1)S(1)}, u32[]{:S(2)}, u32[]{:S(2)}) collective-permute-start(bf16[768,512]{1,0:T(8,128)(2,1)S(1)} %copy-done.47), channel_id=1, source_target_pairs={{0,16},{8,24},{16,0},{24,8},{1,17},{9,25},{17,1},{25,9},{2,18},{10... | collective-permute-start | bytes 2359304 | tf_op jit(solution)/shard_map/ppermute | solution.py:323
  778.2 45.2 %collective-permute-start.53 = (bf16[2,256,2048]{2,1,0:T(8,128)(2,1)}, bf16[2,256,2048]{2,1,0:T(8,128)(2,1)}, u32[]{:S(2)}, u32[]{:S(2)}) collective-permute-start(bf16[2,256,2048]{2,1,0:T(8,128)(2,1)} %pad_maximum_fusion.11), channel_id=1, source_target_pairs={{0,8},{8,0},{16,24},{24,16},{1,9},{9,1},{17,25},{25,17},{2,10},{10... | collective-permute-start | bytes 6291464 | tf_op jit(solution)/shard_map/ppermute | solution.py:232
  801.1 43.4 %collective-permute-start.58 = (bf16[1536,512]{1,0:T(8,128)(2,1)}, bf16[1536,512]{1,0:T(8,128)(2,1)}, u32[]{:S(2)}, u32[]{:S(2)}) collective-permute-start(bf16[1536,512]{1,0:T(8,128)(2,1)} %pad_maximum_fusion.14.own), channel_id=1, source_target_pairs={{0,8},{8,0},{16,24},{24,16},{1,9},{9,1},{17,25},{25,17},{2,10},{10... | collective-permute-start | bytes 4718600 | tf_op jit(solution)/shard_map/ppermute | solution.py:318
  827.8 34.1 %collective-permute-start.57 = (bf16[256,2048]{1,0:T(8,128)(2,1)}, bf16[256,2048]{1,0:T(8,128)(2,1)}, u32[]{:S(2)}, u32[]{:S(2)}) collective-permute-start(bf16[256,2048]{1,0:T(8,128)(2,1)} %fusion.108), channel_id=1, source_target_pairs={{0,16},{8,24},{16,0},{24,8},{1,17},{9,25},{17,1},{25,9},{2,18},{10... | collective-permute-start | bytes 3145736 | tf_op jit(solution)/shard_map/ppermute | solution.py:235
  840.6 51.0 %collective-permute-start.81 = (bf16[896,512]{1,0:T(8,128)(2,1)S(1)}, bf16[896,512]{1,0:T(8,128)(2,1)S(1)}, u32[]{:S(2)}, u32[]{:S(2)}) collective-permute-start(bf16[896,512]{1,0:T(8,128)(2,1)S(1)} %pad_maximum_fusion.19.own), channel_id=1, source_target_pairs={{0,8},{8,0},{16,24},{24,16},{1,9},{9,1},{17,25},{25,17},{2,10},{10... | collective-permute-start | bytes 2752520 | tf_op jit(solution)/shard_map/ppermute | solution.py:318
  (204 other events, 2141.9 us)

commit v6 on v5

--- a/solution.py
+++ b/solution.py
@@ -1148,11 +1148,11 @@
         sums = None
         for i, units in enumerate(chunks):
             if i + 1 < len(chunks):
-                deps = [chunk_fours[i]] + ([] if sums is None else [sums[0]])
+                deps = [chunk_fours[i], second_all if sums is None else sums[0]]
                 chunk_fours.append(mover.near(chunk_pairs[i + 1], *deps))
                 chunk_weights.append(mover.across(chunk_fours[i + 1]))
             if i + 2 < len(chunks):
-                deps = [chunk_pairs[i + 1], down_high[1] if sums is None else sums[0]]
+                deps = [chunk_pairs[i + 1], second_all if sums is None else sums[0]]
                 chunk_pairs.append(gate_up_far(i + 2, *deps))
             lower, upper = chunk_bounds[i]
             units_in = after(second_all, *chunk_fours[i + 1 : i + 2], *chunk_pairs[i + 2 : i + 3])

time: 927 us -> 911 us (0.983)
  Pallas kernels: 239 us -> 224 us
    ppermute x8, waiting for transfers between devices: 51.3 us -> 89 us  [far(): lax.ppermute(chunk, 'wsh', FAR_SWAP)]
    ppermute x7, waiting for transfers between devices: 69.5 us -> 36.5 us  [near(): return jnp.concatenate([pair, lax.ppermute(pair, 'wsh', NEAR_SWAP)], axis=0)]
    ppermute x8, waiting for transfers between devices: 37.9 us -> 26.9 us  [across(): return (four, lax.ppermute(four, 'wsh', X_SWAP))]
    unnamed x350 -> x338, local copies, waits for them, and re-layouts: 77.6 us -> 80.9 us
  transfers between devices with their start and end apart: 84 -> 84, of which waited for: 33 -> 32; matrix products, arithmetic and copies ran while one was open for 30% -> 30% of each run, Pallas kernels for 21% -> 20%
where the time goes in v6:
time: 911 us; the launch traced here: 900 us
  waiting for transfers between devices  237 us (26%)
  Pallas kernels  224 us (25%)
  local copies, waits for them, and re-layouts  157 us (17%)
  other arithmetic  106 us (12%)
  starting transfers between devices  88.8 us (10%)
  matrix products  83.1 us (9%)
    pallas_call x5, Pallas kernels, mlp_call(): pl.pallas_call(lambda *refs: mlp_body(owners, sums is not None, *refs), g...  97.2 us
    ppermute x8, waiting for transfers between devices, far(): lax.ppermute(chunk, 'wsh', FAR_SWAP)  89 us
    unnamed x338, local copies, waits for them, and re-layouts  80.9 us
    dot_general x20, matrix products, low_dot(): return jnp.dot(left, right, preferred_element_type=F32)  48.4 us
    pallas_call x2, Pallas kernels, attention_call(): pl.pallas_call(forward_body, grid_spec=pltpu.PrefetchScalarGridSpec(num_s...  36.7 us
    ppermute x7, waiting for transfers between devices, near(): return jnp.concatenate([pair, lax.ppermute(pair, 'wsh', NEAR_SWAP)], axis=0)  36.5 us
    pallas_call x9, Pallas kernels, final_call(): pl.pallas_call(final_body, grid_spec=pltpu.PrefetchScalarGridSpec(num_sca...  34.4 us
    pallas_call x2, Pallas kernels, attention_back_call(): pl.pallas_call(backward_body, grid_spec=pltpu.PrefetchScalarGridSpec(num_...  30.6 us
  transfers between devices with their start and end apart: 84, of which 32 were waited for; matrix products, arithmetic and copies ran while one was open for 30% of the time, Pallas kernels for 20%

profile of v6, /device:TPU:0, one launch (start us, length us, event | category | flops | bytes accessed | tf_op | source)
XLA Modules:
  0.0 899.9 jit_solution(9302549714008750686)
XLA Ops:
  42.9 18.3 %collective-permute-done = bf16[256,2176]{1,0:T(8,128)(2,1)} collective-permute-done((bf16[256,2176]{1,0:T(8,128)(2,1)}, bf16[256,2176]{1,0:T(8,128)(2,1)}, u32[]{:S(2)}, u32[]{:S(2)}) %collective-permute-start) | collective-permute-done | bytes 1114144 | tf_op jit(solution)/shard_map/ppermute | solution.py:1027
  75.9 20.2 %collective-permute-done.8 = bf16[64,2048]{1,0:T(8,128)(2,1)S(1)} collective-permute-done((bf16[64,2048]{1,0:T(8,128)(2,1)S(1)}, bf16[64,2048]{1,0:T(8,128)(2,1)S(1)}, u32[]{:S(2)}, u32[]{:S(2)}) %collective-permute-start.8) | collective-permute-done | bytes 262176 | tf_op jit(solution)/shard_map/ppermute | solution.py:125
  109.0 8.8 collective-permute-done.9
  139.7 9.2 %qkv.1 = (bf16[1024,512]{1,0:T(8,128)(2,1)}, bf16[1024,256]{1,0:T(8,128)(2,1)}, bf16[1024,256]{1,0:T(8,128)(2,1)}) custom-call(bf16[1024,2176]{1,0:T(8,128)(2,1)} %bitcast.447, bf16[1024,768]{1,0:T(8,128)(2,1)} %pad_maximum_fusion.12.w_own, bf16[1024,768]{1,0:T(8,128)(2,1)} %collective-permute-done.5.w_other, bf16[1024,128]{1,0:T(8,128)(2,1)} %fusion.55.la_q, ...), custom_call_target="tpu_custom_call" | custom-call | flops 3221225472 | bytes 12582912 | tf_op jit(solution)/shard_map/qkv/pallas_call | solution.py:443
  149.6 18.2 %attention.2 = (bf16[1024,256]{1,0:T(8,128)(2,1)}, f32[1024,128]{1,0:T(8,128)}) custom-call(s32[4]{0:T(128)} %and_select_fusion.4.first_ref, bf16[1024,512]{1,0:T(8,128)(2,1)} %get-tuple-element.130.q_ref, bf16[1024,256]{1,0:T(8,128)(2,1)} %get-tuple-element.120.k_ref, bf16[1024,256]{1,0:T(8,128)(2,1)} %get-tuple-element.121.v_ref, ...), custom_call_target="tpu_custom_call" | custom-call | flops 2147483648 | bytes 3145728 | tf_op jit(solution)/shard_map/attention/pallas_call | solution.py:517
  188.0 18.5 %attention.3 = (bf16[1024,256]{1,0:T(8,128)(2,1)}, f32[1024,128]{1,0:T(8,128)}) custom-call(s32[4]{0:T(128)} %and_select_fusion.4.first_ref, bf16[1024,512]{1,0:T(8,128)(2,1)} %get-tuple-element.130.q_ref, bf16[1024,256]{1,0:T(8,128)(2,1)} %get-tuple-element.120.k_ref, bf16[1024,256]{1,0:T(8,128)(2,1)} %get-tuple-element.121.v_ref, ...), custom_call_target="tpu_custom_call" | custom-call | flops 2147483648 | bytes 3145728 | tf_op jit(solution)/shard_map/attention/pallas_call | solution.py:517
  233.2 7.8 collective-permute-start.20
  246.5 17.7 %collective-permute-done.20 = bf16[256,1024]{1,0:T(8,128)(2,1)S(1)} collective-permute-done((bf16[256,1024]{1,0:T(8,128)(2,1)S(1)}, bf16[256,1024]{1,0:T(8,128)(2,1)S(1)}, u32[]{:S(2)}, u32[]{:S(2)}) %collective-permute-start.20) | collective-permute-done | bytes 524320 | tf_op jit(solution)/shard_map/ppermute | solution.py:125
  293.1 15.9 %collective-permute-done.24 = bf16[256,1024]{1,0:T(8,128)(2,1)S(1)} collective-permute-done((bf16[256,1024]{1,0:T(8,128)(2,1)S(1)}, bf16[256,1024]{1,0:T(8,128)(2,1)S(1)}, u32[]{:S(2)}, u32[]{:S(2)}) %collective-permute-start.24) | collective-permute-done | bytes 524320 | tf_op jit(solution)/shard_map/ppermute | solution.py:125
  335.3 25.6 %collective-permute-done.27 = bf16[256,1024]{1,0:T(8,128)(2,1)S(1)} collective-permute-done((bf16[256,1024]{1,0:T(8,128)(2,1)S(1)}, bf16[256,1024]{1,0:T(8,128)(2,1)S(1)}, u32[]{:S(2)}, u32[]{:S(2)}) %collective-permute-start.27) | collective-permute-done | bytes 524320 | tf_op jit(solution)/shard_map/ppermute | solution.py:125
  365.6 9.5 %collective-permute-done.28.refs_3_ = bf16[1024,1024]{1,0:T(8,128)(2,1)} collective-permute-done((bf16[1024,1024]{1,0:T(8,128)(2,1)S(1)}, bf16[1024,1024]{1,0:T(8,128)(2,1)}, u32[]{:S(2)}, u32[]{:S(2)}) %collective-permute-start.28) | collective-permute-done | bytes 2097184 | tf_op jit(solution)/shard_map/ppermute | solution.py:137
  375.1 20.1 %units.5 = (bf16[1024,512]{1,0:T(8,128)(2,1)}, bf16[1024,512]{1,0:T(8,128)(2,1)}, bf16[1024,512]{1,0:T(8,128)(2,1)}, f32[1024,2048]{1,0:T(8,128)}, f32[1024,256]{1,0:T(8,128)}) custom-call(s32[2]{0:T(128)} %pad_add_fusion.refs_0_, bf16[1024,2176]{1,0:T(8,128)(2,1)} %bitcast.423, bf16[1024,1024]{1,0:T(8,128)(2,1)} %copy-done.85, ...), custom_call_target="tpu_custom_call" | custom-call | flops 10737418240 | bytes 33554432 | tf_op jit(solution)/shard_map/units/pallas_call | solution.py:766
  405.0 16.5 %collective-permute-done.29 = bf16[512,1024]{1,0:T(8,128)(2,1)S(1)} collective-permute-done((bf16[512,1024]{1,0:T(8,128)(2,1)S(1)}, bf16[512,1024]{1,0:T(8,128)(2,1)S(1)}, u32[]{:S(2)}, u32[]{:S(2)}) %collective-permute-start.29) | collective-permute-done | bytes 1048608 | tf_op jit(solution)/shard_map/ppermute | solution.py:131
  423.9 21.4 %units.6 = (bf16[1024,512]{1,0:T(8,128)(2,1)}, bf16[1024,512]{1,0:T(8,128)(2,1)}, bf16[1024,512]{1,0:T(8,128)(2,1)}, f32[1024,2048]{1,0:T(8,128)}, f32[1024,256]{1,0:T(8,128)}) custom-call(s32[2]{0:T(128)} %pad_add_fusion.1.refs_0_, bf16[1024,2176]{1,0:T(8,128)(2,1)} %bitcast.424, ...), custom_call_target="tpu_custom_call", output_to_operand_aliasing={{3}: (15, {}), {4}: (16, {})} | custom-call | flops 10737418240 | bytes 33554432 | tf_op jit(solution)/shard_map/units/pallas_call | solution.py:766
  465.3 21.4 %units.7 = (bf16[1024,512]{1,0:T(8,128)(2,1)}, bf16[1024,512]{1,0:T(8,128)(2,1)}, bf16[1024,512]{1,0:T(8,128)(2,1)}, f32[1024,2048]{1,0:T(8,128)}, f32[1024,256]{1,0:T(8,128)}) custom-call(s32[2]{0:T(128)} %pad_add_fusion.2.refs_0_, bf16[1024,2176]{1,0:T(8,128)(2,1)} %bitcast.425, ...), custom_call_target="tpu_custom_call", output_to_operand_aliasing={{3}: (15, {}), {4}: (16, {})} | custom-call | flops 10737418240 | bytes 33554432 | tf_op jit(solution)/shard_map/units/pallas_call | solution.py:766
  503.9 9.1 %collective-permute-done.36.refs_3_ = bf16[1024,512]{1,0:T(8,128)(2,1)} collective-permute-done((bf16[1024,512]{1,0:T(8,128)(2,1)S(1)}, bf16[1024,512]{1,0:T(8,128)(2,1)}, u32[]{:S(2)}, u32[]{:S(2)}) %collective-permute-start.36) | collective-permute-done | bytes 1048608 | tf_op jit(solution)/shard_map/ppermute | solution.py:137
  513.0 17.3 %units.8 = (bf16[1024,256]{1,0:T(8,128)(2,1)}, bf16[1024,256]{1,0:T(8,128)(2,1)}, bf16[1024,256]{1,0:T(8,128)(2,1)}, f32[1024,2048]{1,0:T(8,128)}, f32[1024,256]{1,0:T(8,128)}) custom-call(s32[2]{0:T(128)} %pad_add_fusion.3.refs_0_, bf16[1024,2176]{1,0:T(8,128)(2,1)} %bitcast.426, ...), custom_call_target="tpu_custom_call", output_to_operand_aliasing={{3}: (15, {}), {4}: (16, {})} | custom-call | flops 5368709120 | bytes 33554432 | tf_op jit(solution)/shard_map/units/pallas_call | solution.py:766
  530.4 17.0 %units.9 = (bf16[1024,256]{1,0:T(8,128)(2,1)}, bf16[1024,256]{1,0:T(8,128)(2,1)}, bf16[1024,256]{1,0:T(8,128)(2,1)}, f32[1024,2048]{1,0:T(8,128)}, f32[1024,256]{1,0:T(8,128)}) custom-call(s32[2]{0:T(128)} %pad_add_fusion.3.refs_0_, bf16[1024,2176]{1,0:T(8,128)(2,1)} %bitcast.427, ...), custom_call_target="tpu_custom_call", output_to_operand_aliasing={{3}: (15, {}), {4}: (16, {})} | custom-call | flops 5368709120 | bytes 33554432 | tf_op jit(solution)/shard_map/units/pallas_call | solution.py:766
  571.7 15.6 %units_out.1 = f32[1024,2048]{1,0:T(8,128)} custom-call(s32[5]{0:T(128)} %stack.205.refs_0_, bf16[1024,512]{1,0:T(8,128)(2,1)} %get-tuple-element.156.refs_1_, bf16[1024,512]{1,0:T(8,128)(2,1)} %get-tuple-element.163.refs_2_, bf16[1024,512]{1,0:T(8,128)(2,1)} %get-tuple-element.170.refs_3_, bf16[1024,256]{1,0:T(8,128)(2,1)} %get-tuple-element.175.refs_4_, ...), custom_call_target="tpu_custom_call" | custom-call | flops 8589934592 | bytes 20971520 | tf_op jit(solution)/shard_map/units_out/pallas_call | solution.py:808
  633.9 9.4 %collective-permute-done.47 = bf16[192,512]{1,0:T(8,128)(2,1)S(1)} collective-permute-done((bf16[192,512]{1,0:T(8,128)(2,1)S(1)}, bf16[192,512]{1,0:T(8,128)(2,1)S(1)}, u32[]{:S(2)}, u32[]{:S(2)}) %collective-permute-start.47) | collective-permute-done | bytes 196640 | tf_op jit(solution)/shard_map/ppermute | solution.py:308
  678.7 15.2 %attention_back.2 = (bf16[1024,256]{1,0:T(8,128)(2,1)}, bf16[1024,128]{1,0:T(8,128)(2,1)}, bf16[1024,128]{1,0:T(8,128)(2,1)}) custom-call(s32[4]{0:T(128)} %and_select_fusion.4.first_ref, bf16[1024,512]{1,0:T(8,128)(2,1)} %get-tuple-element.130.q_ref, bf16[1024,256]{1,0:T(8,128)(2,1)} %get-tuple-element.120.k_ref, ...), custom_call_target="tpu_custom_call" | custom-call | flops 5368709120 | bytes 5242880 | tf_op jit(solution)/shard_map/attention_back/pallas_call | solution.py:621
  709.3 15.4 %attention_back.3 = (bf16[1024,256]{1,0:T(8,128)(2,1)}, bf16[1024,128]{1,0:T(8,128)(2,1)}, bf16[1024,128]{1,0:T(8,128)(2,1)}) custom-call(s32[4]{0:T(128)} %and_select_fusion.4.first_ref, bf16[1024,512]{1,0:T(8,128)(2,1)} %get-tuple-element.130.q_ref, bf16[1024,256]{1,0:T(8,128)(2,1)} %get-tuple-element.120.k_ref, ...), custom_call_target="tpu_custom_call" | custom-call | flops 5368709120 | bytes 5242880 | tf_op jit(solution)/shard_map/attention_back/pallas_call | solution.py:621
  835.7 11.1 %finish.9 = f32[2,128,8192]{2,1,0:T(8,128)} custom-call(s32[1]{0:T(128)} %bitcast.111.s_ref, bf16[1536,512]{1,0:T(8,128)(2,1)} %pad_maximum_fusion.14.own, bf16[1536,512]{1,0:T(8,128)(2,1)} %collective-permute-done.58.core, bf16[1536,512]{1,0:T(8,128)(2,1)} %constant_dynamic-update-slice_fusion.58.other, bf16[1536,512]{1,0:T(8,128)(2,1)} %collective-permute-done.59.last), custom_call_target="tpu_custom_call" | custom-call | tf_op jit(solution)/shard_map/finish/pallas_call | solution.py:344
  855.0 14.6 %collective-permute-done.79.other = bf16[896,512]{1,0:T(8,128)(2,1)} collective-permute-done((bf16[896,512]{1,0:T(8,128)(2,1)S(1)}, bf16[896,512]{1,0:T(8,128)(2,1)}, u32[]{:S(2)}, u32[]{:S(2)}) %collective-permute-start.79) | collective-permute-done | bytes 917536 | tf_op jit(solution)/shard_map/ppermute | solution.py:320
  (758 shorter events, 522.4 us)
Async XLA Ops:
  3.6 34.2 %collective-permute-start.3 = (bf16[256,768]{1,0:T(8,128)(2,1)}, bf16[256,768]{1,0:T(8,128)(2,1)S(1)}, u32[]{:S(2)}, u32[]{:S(2)}) collective-permute-start(bf16[256,768]{1,0:T(8,128)(2,1)} %pad_maximum_fusion.32), channel_id=1, source_target_pairs={{0,4},{1,5},{2,6},{3,7},{4,0},{5,1},{6,2},{7,3},{8,12},{9,13},{10,... | collective-permute-start | bytes 1179656 | tf_op jit(solution)/shard_map/ppermute | solution.py:125
  65.0 58.1 %collective-permute-start.2 = (bf16[2,256,2176]{2,1,0:T(8,128)(2,1)}, bf16[2,256,2176]{2,1,0:T(8,128)(2,1)}, u32[]{:S(2)}, u32[]{:S(2)}) collective-permute-start(bf16[2,256,2176]{2,1,0:T(8,128)(2,1)} %pad_maximum_fusion.4), channel_id=1, source_target_pairs={{0,8},{8,0},{16,24},{24,16},{1,9},{9,1},{17,25},{25,17},{2,10},{10... | collective-permute-start | bytes 6684680 | tf_op jit(solution)/shard_map/ppermute | solution.py:216
  66.5 53.3 %collective-permute-start.5 = (bf16[1024,768]{1,0:T(8,128)(2,1)}, bf16[1024,768]{1,0:T(8,128)(2,1)}, u32[]{:S(2)}, u32[]{:S(2)}) collective-permute-start(bf16[1024,768]{1,0:T(8,128)(2,1)} %pad_maximum_fusion.12.w_own), channel_id=1, source_target_pairs={{0,1},{1,0},{2,3},{3,2},{4,5},{5,4},{6,7},{7,6},{8,9},{9,8},{10,11... | collective-permute-start | bytes 4718600 | tf_op jit(solution)/shard_map/ppermute | solution.py:137
  73.3 33.5 %collective-permute-start.11 = (bf16[256,1024]{1,0:T(8,128)(2,1)}, bf16[256,1024]{1,0:T(8,128)(2,1)}, u32[]{:S(2)}, u32[]{:S(2)}) collective-permute-start(bf16[256,1024]{1,0:T(8,128)(2,1)} %get-tuple-element.126), channel_id=1, source_target_pairs={{0,4},{1,5},{2,6},{3,7},{4,0},{5,1},{6,2},{7,3},{8,12},{9,13},{10,... | collective-permute-start | bytes 1572872 | tf_op jit(solution)/shard_map/ppermute | solution.py:125
  119.8 49.8 %collective-permute-start.14 = (bf16[512,1024]{1,0:T(8,128)(2,1)}, bf16[512,1024]{1,0:T(8,128)(2,1)}, u32[]{:S(2)}, u32[]{:S(2)}) collective-permute-start(bf16[512,1024]{1,0:T(8,128)(2,1)} %get-tuple-element.136), channel_id=1, source_target_pairs={{0,2},{1,3},{2,0},{3,1},{4,6},{5,7},{6,4},{7,5},{8,10},{9,11},{10,... | collective-permute-start | bytes 3145736 | tf_op jit(solution)/shard_map/ppermute | solution.py:1038
  119.8 60.0 %collective-permute-start.10 = (bf16[256,2048]{1,0:T(8,128)(2,1)}, bf16[256,2048]{1,0:T(8,128)(2,1)}, u32[]{:S(2)}, u32[]{:S(2)}) collective-permute-start(bf16[256,2048]{1,0:T(8,128)(2,1)} %constant_dynamic-update-slice_fusion.9), channel_id=1, source_target_pairs={{0,1},{1,0},{2,3},{3,2},{4,5},{5,4},{6,7},{7,6},{8,9},{9,8},{10,11... | collective-permute-start | bytes 3145736 | tf_op jit(solution)/shard_map/ppermute | solution.py:137
  120.3 49.3 %collective-permute-start.12 = (bf16[256,1024]{1,0:T(8,128)(2,1)S(1)}, bf16[256,1024]{1,0:T(8,128)(2,1)}, u32[]{:S(2)}, u32[]{:S(2)}) collective-permute-start(bf16[256,1024]{1,0:T(8,128)(2,1)S(1)} %copy-done.55), channel_id=1, source_target_pairs={{0,4},{1,5},{2,6},{3,7},{4,0},{5,1},{6,2},{7,3},{8,12},{9,13},{10,... | collective-permute-start | bytes 1572872 | tf_op jit(solution)/shard_map/ppermute | solution.py:1040
  174.1 34.5 %collective-permute-start.15 = (bf16[512,1024]{1,0:T(8,128)(2,1)}, bf16[512,1024]{1,0:T(8,128)(2,1)}, u32[]{:S(2)}, u32[]{:S(2)}) collective-permute-start(bf16[512,1024]{1,0:T(8,128)(2,1)} %get-tuple-element.134), channel_id=1, source_target_pairs={{0,2},{1,3},{2,0},{3,1},{4,6},{5,7},{6,4},{7,5},{8,10},{9,11},{10,... | collective-permute-start | bytes 3145736 | tf_op jit(solution)/shard_map/ppermute | solution.py:1096
  229.6 36.7 %collective-permute-start.18 = (bf16[256,2176]{1,0:T(8,128)(2,1)S(1)}, bf16[256,2176]{1,0:T(8,128)(2,1)S(1)}, u32[]{:S(2)}, u32[]{:S(2)}) collective-permute-start(bf16[256,2176]{1,0:T(8,128)(2,1)S(1)} %fusion.88), channel_id=1, source_target_pairs={{0,16},{8,24},{16,0},{24,8},{1,17},{9,25},{17,1},{25,9},{2,18},{10... | collective-permute-start | bytes 3342344 | tf_op jit(solution)/shard_map/ppermute | solution.py:235
  245.0 67.9 %collective-permute-start.22 = (bf16[1024,1024]{1,0:T(8,128)(2,1)}, bf16[1024,1024]{1,0:T(8,128)(2,1)}, u32[]{:S(2)}, u32[]{:S(2)}) collective-permute-start(bf16[1024,1024]{1,0:T(8,128)(2,1)} %constant_dynamic-update-slice_fusion.20.refs_11_.refs_8_), channel_id=1, source_target_pairs={{0,1},{1,0},{2,3},{3,2},{4,5},{5,4},{6,7},{7,6},{8,9},{9,8},{10,11... | collective-permute-start | bytes 6291464 | tf_op jit(solution)/shard_map/ppermute | solution.py:137
  265.3 43.8 %collective-permute-start.23 = (bf16[512,1024]{1,0:T(8,128)(2,1)}, bf16[512,1024]{1,0:T(8,128)(2,1)}, u32[]{:S(2)}, u32[]{:S(2)}) collective-permute-start(bf16[512,1024]{1,0:T(8,128)(2,1)} %pad_maximum_fusion.16), channel_id=1, source_target_pairs={{0,2},{1,3},{2,0},{3,1},{4,6},{5,7},{6,4},{7,5},{8,10},{9,11},{10,... | collective-permute-start | bytes 3145736 | tf_op jit(solution)/shard_map/ppermute | solution.py:131
  326.5 48.6 %collective-permute-start.28 = (bf16[1024,1024]{1,0:T(8,128)(2,1)S(1)}, bf16[1024,1024]{1,0:T(8,128)(2,1)}, u32[]{:S(2)}, u32[]{:S(2)}) collective-permute-start(bf16[1024,1024]{1,0:T(8,128)(2,1)S(1)} %constant_dynamic-update-slice_fusion.31.refs_2_), channel_id=1, source_target_pairs={{0,1},{1,0},{2,3},{3,2},{4,5},{5,4},{6,7},{7,6},{8,9},{9,8},{10,11... | collective-permute-start | bytes 6291464 | tf_op jit(solution)/shard_map/ppermute | solution.py:137
  328.3 34.8 %collective-permute-start.26 = (bf16[512,1024]{1,0:T(8,128)(2,1)S(1)}, bf16[512,1024]{1,0:T(8,128)(2,1)S(1)}, u32[]{:S(2)}, u32[]{:S(2)}) collective-permute-start(bf16[512,1024]{1,0:T(8,128)(2,1)S(1)} %pad_maximum_fusion.17), channel_id=1, source_target_pairs={{0,2},{1,3},{2,0},{3,1},{4,6},{5,7},{6,4},{7,5},{8,10},{9,11},{10,... | collective-permute-start | bytes 3145736 | tf_op jit(solution)/shard_map/ppermute | solution.py:131
  364.1 59.7 %collective-permute-start.31 = (bf16[1024,1024]{1,0:T(8,128)(2,1)}, bf16[1024,1024]{1,0:T(8,128)(2,1)}, u32[]{:S(2)}, u32[]{:S(2)}) collective-permute-start(bf16[1024,1024]{1,0:T(8,128)(2,1)} %constant_dynamic-update-slice_fusion.33.refs_2_), channel_id=1, source_target_pairs={{0,1},{1,0},{2,3},{3,2},{4,5},{5,4},{6,7},{7,6},{8,9},{9,8},{10,11... | collective-permute-start | bytes 6291464 | tf_op jit(solution)/shard_map/ppermute | solution.py:137
  422.6 42.7 %collective-permute-start.34 = (bf16[1024,1024]{1,0:T(8,128)(2,1)}, bf16[1024,1024]{1,0:T(8,128)(2,1)}, u32[]{:S(2)}, u32[]{:S(2)}) collective-permute-start(bf16[1024,1024]{1,0:T(8,128)(2,1)} %constant_dynamic-update-slice_fusion.37.refs_2_), channel_id=1, source_target_pairs={{0,1},{1,0},{2,3},{3,2},{4,5},{5,4},{6,7},{7,6},{8,9},{9,8},{10,11... | collective-permute-start | bytes 6291464 | tf_op jit(solution)/shard_map/ppermute | solution.py:137
  496.8 33.5 %collective-permute-start.37 = (bf16[1024,512]{1,0:T(8,128)(2,1)}, bf16[1024,512]{1,0:T(8,128)(2,1)}, u32[]{:S(2)}, u32[]{:S(2)}) collective-permute-start(bf16[1024,512]{1,0:T(8,128)(2,1)} %constant_dynamic-update-slice_fusion.41.refs_2_), channel_id=1, source_target_pairs={{0,1},{1,0},{2,3},{3,2},{4,5},{5,4},{6,7},{7,6},{8,9},{9,8},{10,11... | collective-permute-start | bytes 3145736 | tf_op jit(solution)/shard_map/ppermute | solution.py:137
  564.7 33.3 %collective-permute-start.40 = (bf16[256,2176]{1,0:T(8,128)(2,1)}, bf16[256,2176]{1,0:T(8,128)(2,1)}, u32[]{:S(2)}, u32[]{:S(2)}) collective-permute-start(bf16[256,2176]{1,0:T(8,128)(2,1)} %fusion.89), channel_id=1, source_target_pairs={{0,16},{8,24},{16,0},{24,8},{1,17},{9,25},{17,1},{25,9},{2,18},{10... | collective-permute-start | bytes 3342344 | tf_op jit(solution)/shard_map/ppermute | solution.py:235
  738.4 44.7 %collective-permute-start.54 = (bf16[1024,128]{1,0:T(8,128)(2,1)}, bf16[1024,128]{1,0:T(8,128)(2,1)}, u32[]{:S(2)}, u32[]{:S(2)}) collective-permute-start(bf16[1024,128]{1,0:T(8,128)(2,1)} %convolution_add_fusion.2), channel_id=1, source_target_pairs={{0,8},{8,0},{16,24},{24,16},{1,9},{9,1},{17,25},{25,17},{2,10},{10... | collective-permute-start | bytes 786440 | tf_op jit(solution)/shard_map/ppermute | solution.py:250
  753.6 39.9 %collective-permute-start.55 = (bf16[768,512]{1,0:T(8,128)(2,1)S(1)}, bf16[768,512]{1,0:T(8,128)(2,1)S(1)}, u32[]{:S(2)}, u32[]{:S(2)}) collective-permute-start(bf16[768,512]{1,0:T(8,128)(2,1)S(1)} %copy-done.45), channel_id=1, source_target_pairs={{0,16},{8,24},{16,0},{24,8},{1,17},{9,25},{17,1},{25,9},{2,18},{10... | collective-permute-start | bytes 2359304 | tf_op jit(solution)/shard_map/ppermute | solution.py:323
  763.7 43.9 %collective-permute-start.53 = (bf16[2,256,2048]{2,1,0:T(8,128)(2,1)}, bf16[2,256,2048]{2,1,0:T(8,128)(2,1)}, u32[]{:S(2)}, u32[]{:S(2)}) collective-permute-start(bf16[2,256,2048]{2,1,0:T(8,128)(2,1)} %pad_maximum_fusion.11), channel_id=1, source_target_pairs={{0,8},{8,0},{16,24},{24,16},{1,9},{9,1},{17,25},{25,17},{2,10},{10... | collective-permute-start | bytes 6291464 | tf_op jit(solution)/shard_map/ppermute | solution.py:232
  786.7 42.8 %collective-permute-start.58 = (bf16[1536,512]{1,0:T(8,128)(2,1)}, bf16[1536,512]{1,0:T(8,128)(2,1)}, u32[]{:S(2)}, u32[]{:S(2)}) collective-permute-start(bf16[1536,512]{1,0:T(8,128)(2,1)} %pad_maximum_fusion.14.own), channel_id=1, source_target_pairs={{0,8},{8,0},{16,24},{24,16},{1,9},{9,1},{17,25},{25,17},{2,10},{10... | collective-permute-start | bytes 4718600 | tf_op jit(solution)/shard_map/ppermute | solution.py:318
  795.4 34.1 %collective-permute-start.59 = (bf16[1536,512]{1,0:T(8,128)(2,1)}, bf16[1536,512]{1,0:T(8,128)(2,1)}, u32[]{:S(2)}, u32[]{:S(2)}) collective-permute-start(bf16[1536,512]{1,0:T(8,128)(2,1)} %constant_dynamic-update-slice_fusion.58.other), channel_id=1, source_target_pairs={{0,8},{8,0},{16,24},{24,16},{1,9},{9,1},{17,25},{25,17},{2,10},{10... | collective-permute-start | bytes 4718600 | tf_op jit(solution)/shard_map/ppermute | solution.py:326
  812.4 34.3 %collective-permute-start.57 = (bf16[256,2048]{1,0:T(8,128)(2,1)}, bf16[256,2048]{1,0:T(8,128)(2,1)}, u32[]{:S(2)}, u32[]{:S(2)}) collective-permute-start(bf16[256,2048]{1,0:T(8,128)(2,1)} %fusion.108), channel_id=1, source_target_pairs={{0,16},{8,24},{16,0},{24,8},{1,17},{9,25},{17,1},{25,9},{2,18},{10... | collective-permute-start | bytes 3145736 | tf_op jit(solution)/shard_map/ppermute | solution.py:235
  825.2 51.1 %collective-permute-start.81 = (bf16[896,512]{1,0:T(8,128)(2,1)S(1)}, bf16[896,512]{1,0:T(8,128)(2,1)S(1)}, u32[]{:S(2)}, u32[]{:S(2)}) collective-permute-start(bf16[896,512]{1,0:T(8,128)(2,1)S(1)} %pad_maximum_fusion.19.own), channel_id=1, source_target_pairs={{0,8},{8,0},{16,24},{24,16},{1,9},{9,1},{17,25},{25,17},{2,10},{10... | collective-permute-start | bytes 2752520 | tf_op jit(solution)/shard_map/ppermute | solution.py:318
  (198 other events, 2109.9 us)
